TPU v7x, 512 devices: a whole 4x4x16 slice. The times are simulated.
512 devices in a mesh: ctx: 32 (over z, y_lo), exp: 8 (over x, core), dp: 2 (over y_hi).
Axes of the slice: x: 4, y: 4 (y_hi: 2, y_lo: 2; y = y_hi * 2 + y_lo), z: 16, core: 2. Of those that a mesh axis runs over, the one named last changes fastest.
Arguments:
- hidden_in: bfloat16 [2, 32768, 1024], P('dp', ('ctx', 'exp')), may hold values from -6 to 6
- queries: bfloat16 [2, 32768, 1024], P('dp', ('ctx', 'exp')), may hold values from -6 to 6
- keys: bfloat16 [2, 32768, 1024], P('dp', ('ctx', 'exp')), may hold values from -6 to 6
- values: bfloat16 [2, 32768, 1024], P('dp', ('ctx', 'exp')), may hold values from -6 to 6
- log_decay: float32 [2, 32768, 8], P('dp', ('ctx', 'exp')), may hold values from -1 to 0
- retention_gain: float32 [1024], replicated, may hold values from 0.25 to 1.75
- norm_gain: float32 [1024], replicated, may hold values from 0.25 to 1.75
- routes: int32 [2, 32768, 2], P('dp', ('ctx', 'exp')), may hold values from 0 to 63, all different within a row; in each aligned block of 128 rows (0 to 127, 128 to 255, ..., all dimensions but the last counted through in order) at most 5 rows name the same one
- route_weights: float32 [2, 32768, 2], P('dp', ('ctx', 'exp')), may hold values from 0.1 to 1
- w_gate: bfloat16 [64, 1024, 1408], P(('ctx', 'dp'), 'exp'), may hold values from -0.1875 to 0.1875
- w_up: bfloat16 [64, 1024, 1408], P(('ctx', 'dp'), 'exp'), may hold values from -0.1875 to 0.1875
- w_down: bfloat16 [64, 1024, 1408], P(('ctx', 'dp'), 'exp'), may hold values from -0.15625 to 0.15625
Outputs:
- output: bfloat16 [2, 32768, 1024], P('dp', ('ctx', 'exp'))
Inputs may be any that keep to these rules, and one draw needn't show every extreme that they name: `routes`: in each aligned block of 128 positions (the positions of one device) no expert is named more than 5 times, and a position's 2 experts differ.
All inputs are finite; a program needn't handle non-finite values.
Results may differ from a plain program's by a relative error of at most 0.007.
Values may be sent and summed in bfloat16 or wider, within the bound.
No kernel may reach another device: no remote copies, remote signals or barrier semaphores. Data moves between devices by JAX's collectives and lax.ppermute only.
A program may use at most 128 MiB of HBM per device.

v0:
```python
import jax
import jax.numpy as jnp
from jax import lax
from jax.sharding import PartitionSpec as P


def carried_in(part, axis, combine, identity):
    place = lax.axis_index(axis)
    gathered = jax.tree.map(lambda a: lax.all_gather(a, axis), part)
    state = jax.tree.map(lambda a, e: jnp.zeros_like(a) + jnp.asarray(e, a.dtype), part, identity)

    def one(lap, state):
        return combine(
            state, jax.tree.map(lambda a: lax.dynamic_index_in_dim(a, lap, 0, False), gathered)
        )

    return lax.fori_loop(0, place, one, state)


def rotate(vectors, token_position):
    half_dim = vectors.shape[-1] // 2
    inverse = 10000.0 ** (-jnp.arange(half_dim, dtype=jnp.float32) / half_dim)
    angles = token_position.astype(jnp.float32)[:, None] * inverse[None, :]
    cosine = jnp.cos(angles)[:, None, :]
    sine_part = jnp.sin(angles)[:, None, :]
    leading = vectors[..., :half_dim]
    trailing = vectors[..., half_dim:]
    return jnp.concatenate(
        [leading * cosine - trailing * sine_part, trailing * cosine + leading * sine_part], axis=-1
    )


def chain_combine(earlier, later_part):
    return (earlier[0] * later_part[0], later_part[0][:, None, None] * earlier[1] + later_part[1])


def body(
    hidden_in,
    queries,
    keys,
    values,
    log_decay,
    retention_gain,
    norm_gain,
    routes,
    route_weights,
    w_gate,
    w_up,
    w_down,
):
    tok_rows = hidden_in.shape[1]
    model_width = hidden_in.shape[2]
    head_count = log_decay.shape[2]
    head_dim = model_width // head_count
    block_index = lax.axis_index("ctx") * lax.axis_size("exp") + lax.axis_index("exp")
    token_position = block_index * tok_rows + jnp.arange(tok_rows, dtype=jnp.int32)
    per_head_queries = (
        rotate(
            queries[0].astype(jnp.float32).reshape(tok_rows, head_count, head_dim), token_position
        )
        * head_dim ** (-0.5)
    ).astype(jnp.bfloat16)
    per_head_keys = rotate(
        keys[0].astype(jnp.float32).reshape(tok_rows, head_count, head_dim), token_position
    ).astype(jnp.bfloat16)
    per_head_values = values[0].reshape(tok_rows, head_count, head_dim)
    running_total = jnp.cumsum(log_decay[0], axis=0)
    scores = jnp.einsum(
        "thd,shd->hts", per_head_queries, per_head_keys, preferred_element_type=jnp.float32
    )
    causal = jnp.arange(tok_rows)[:, None] >= jnp.arange(tok_rows)[None, :]
    spread = running_total.T[:, :, None] - running_total.T[:, None, :]
    weights = jnp.where(
        causal[None], scores * jnp.exp(jnp.where(causal[None], spread, 0.0)), 0.0
    ).astype(jnp.bfloat16)
    inside = jnp.einsum(
        "hts,shd->thd", weights, per_head_values, preferred_element_type=jnp.float32
    )
    trailing_decay = jnp.exp(running_total[-1][None, :] - running_total)
    block_summary = jnp.einsum(
        "qpf,qpy->pfy",
        per_head_keys.astype(jnp.float32) * trailing_decay[:, :, None],
        per_head_values.astype(jnp.float32),
        precision=lax.Precision.HIGHEST,
    )
    group_logs, group_sums = (
        lax.all_gather(running_total[-1][None], "exp", axis=0, tiled=True),
        lax.all_gather(block_summary[None], "exp", axis=0, tiled=True),
    )
    group_size = lax.axis_size("exp")
    own_member = lax.axis_index("exp")
    inclusive = jnp.cumsum(group_logs, axis=0)
    exclusive = inclusive - group_logs
    entering_log = lax.dynamic_index_in_dim(exclusive, own_member, 0, keepdims=False)
    before_me = jnp.arange(group_size, dtype=jnp.int32)[:, None] < own_member
    inner_coeff = jnp.where(
        before_me, jnp.exp(jnp.where(before_me, entering_log[None, :] - inclusive, 0.0)), 0.0
    )
    inner_state = jnp.einsum(
        "jh,jhab->hab", inner_coeff, group_sums, precision=lax.Precision.HIGHEST
    )
    total_coeff = jnp.exp(inclusive[-1][None, :] - inclusive)
    group_state = jnp.einsum(
        "jh,jhab->hab", total_coeff, group_sums, precision=lax.Precision.HIGHEST
    )
    group_decay = jnp.exp(inclusive[-1])
    identity = (
        jnp.ones((head_count,), jnp.float32),
        jnp.zeros((head_count, head_dim, head_dim), jnp.float32),
    )
    leading_sum = carried_in((group_decay, group_state), "ctx", chain_combine, identity)
    state_in = jnp.exp(entering_log)[:, None, None] * leading_sum[1] + inner_state
    external_part = jnp.exp(running_total)[:, :, None] * jnp.einsum(
        "wjc,jco->wjo",
        per_head_queries.astype(jnp.float32),
        state_in,
        precision=lax.Precision.HIGHEST,
    )
    retrieved = inside + external_part
    centre = jnp.mean(retrieved, axis=-1, keepdims=True)
    deviation = retrieved - centre
    variance = jnp.mean(deviation * deviation, axis=-1, keepdims=True)
    normalized = (deviation * lax.rsqrt(variance + 1e-05)).reshape(tok_rows, model_width)
    residual = hidden_in[0].astype(jnp.float32) + retention_gain * normalized
    square_mean = jnp.mean(residual * residual, axis=-1, keepdims=True)
    normed = (residual * lax.rsqrt(square_mean + 1e-06) * norm_gain).astype(jnp.bfloat16)
    expert_count = lax.axis_size("ctx") * lax.axis_size("dp")
    top_count = routes.shape[2]
    capacity = (tok_rows * top_count * 5 + 4 * expert_count - 1) // (4 * expert_count)
    slot_count = expert_count * capacity
    route_rows = routes[0]
    expert_hits = (
        route_rows.reshape(tok_rows * top_count)[:, None]
        == jnp.arange(expert_count, dtype=jnp.int32)[None, :]
    ).astype(jnp.int32)
    earlier = jnp.cumsum(expert_hits, axis=0) - expert_hits
    slot_rank = jnp.sum(earlier * expert_hits, axis=1).reshape(tok_rows, top_count)
    destination = route_rows * capacity + slot_rank
    slot_lanes = jnp.arange(slot_count, dtype=jnp.int32)
    placing = jnp.any(destination[None, :, :] == slot_lanes[:, None, None], axis=2).astype(
        jnp.bfloat16
    )
    outgoing = jnp.dot(placing, normed, preferred_element_type=jnp.float32).astype(jnp.bfloat16)
    arrived = lax.all_to_all(
        outgoing.reshape(expert_count, capacity, model_width),
        ("ctx", "dp"),
        split_axis=0,
        concat_axis=0,
        tiled=True,
    ).reshape(slot_count, model_width)
    gate_next = jnp.dot(
        arrived,
        lax.all_gather(w_gate, "exp", axis=1, tiled=True)[0],
        preferred_element_type=jnp.float32,
    )
    up_next = jnp.dot(
        arrived,
        lax.all_gather(w_up, "exp", axis=1, tiled=True)[0],
        preferred_element_type=jnp.float32,
    )
    hidden = (jax.nn.silu(gate_next) * up_next).astype(jnp.bfloat16)
    group_count = lax.axis_size("exp")
    local_features = w_down.shape[1]
    partial_out = lax.dot_general(
        lax.all_gather(hidden, "exp", axis=0, tiled=True),
        w_down[0],
        (((1,), (1,)), ((), ())),
        preferred_element_type=jnp.float32,
    ).astype(jnp.bfloat16)
    expert_out = lax.all_to_all(
        partial_out.reshape(group_count, slot_count, local_features),
        "exp",
        split_axis=0,
        concat_axis=2,
        tiled=True,
    ).reshape(slot_count, group_count * local_features)
    returned = lax.all_to_all(
        expert_out.reshape(expert_count, capacity, model_width),
        ("ctx", "dp"),
        split_axis=0,
        concat_axis=0,
        tiled=True,
    ).reshape(slot_count, model_width)
    output = residual
    for route_index in range(top_count):
        picking = (destination[:, route_index][:, None] == slot_lanes[None, :]).astype(jnp.bfloat16)
        routed = jnp.dot(picking, returned, preferred_element_type=jnp.float32)
        output = output + route_weights[0][:, route_index][:, None] * routed
    return output.astype(jnp.bfloat16)[None]


def solution(mesh):
    in_specs = (
        P("dp", ("ctx", "exp"), None),
        P("dp", ("ctx", "exp"), None),
        P("dp", ("ctx", "exp"), None),
        P("dp", ("ctx", "exp"), None),
        P("dp", ("ctx", "exp"), None),
        P(),
        P(),
        P("dp", ("ctx", "exp"), None),
        P("dp", ("ctx", "exp"), None),
        P(("ctx", "dp"), "exp", None),
        P(("ctx", "dp"), "exp", None),
        P(("ctx", "dp"), "exp", None),
    )
    out_specs = P("dp", ("ctx", "exp"), None)
    return jax.shard_map(body, mesh=mesh, in_specs=in_specs, out_specs=out_specs, check_vma=False)
```

profile of v0, /device:TPU:16, one launch (start us, length us, event | category | flops | bytes accessed | tf_op | source)
XLA Modules:
  0.0 692.3 jit_solution(12312652453799544081)
XLA Ops:
  6.6 1.2 copy.90
  9.2 0.6 fusion.52
  9.9 1.0 copy.121
  10.9 0.3 multiply_cosine_fusion
  11.2 0.3 subtract_convert_fusion
  11.6 0.7 copy-done.4
  12.3 1.6 fusion.21
  14.0 10.6 %all-gather.2 = f32[8,1,8]{2,1,0:T(1,128)S(1)} all-gather(f32[1,1,8]{2,1,0:T(1,128)S(1)} %get-tuple-element.77), channel_id=1, replica_groups=mesh['ctx'=32,'exp'=8,'dp'=2] {'exp'}, dimensions={0}, use_global_device_ids=true | all-gather | bytes 288 | tf_op jit(solution)/shard_map/all_gather | solution.py:87
  24.8 33.3 %all-gather.16.cloned.1.call-done = f32[64,128,128]{2,1,0:T(8,128)} async-done(((f32[8,128,128]{2,1,0:T(8,128)}), f32[64,128,128]{2,1,0:T(8,128)}) %all-gather.16.cloned.1.call-update) | async-done | bytes 4194320 | tf_op jit(solution)/shard_map/all_gather | solution.py:88
  58.1 9.0 %fusion.2 = f32[8,1,128,128]{3,1,2,0:T(1,128)} fusion(f32[8,8,1,1]{0,2,3,1:T(1,128)S(1)} %copy.110, f32[8,8,128,128]{3,2,1,0:T(8,128)} %bitcast.116), kind=kOutput, calls=%fused_computation.4 | convolution fusion | flops 12582912 | bytes 4718848 | tf_op jit(solution)/shard_map/jh,jhab->hab/dot_general | solution.py:103
  67.2 0.7 all-gather.10.cloned.1.call-update
  68.0 0.5 all-gather.12.cloned.1.call-update
  69.0 0.6 reduce-window.6
  70.3 68.1 %all-gather.3 = f32[32,1,8]{2,1,0:T(1,128)S(1)} all-gather(f32[1,1,8]{2,1,0:T(1,128)S(1)} %get-tuple-element.81), channel_id=1, replica_groups=mesh['ctx'=32,'exp'=8,'dp'=2] {'ctx'}, dimensions={0}, use_global_device_ids=true | all-gather | bytes 1056 | tf_op jit(solution)/shard_map/all_gather | solution.py:9
  138.8 8.2 %fusion = f32[8,1,128,128]{3,1,2,0:T(1,128)S(1)} fusion(f32[8,8,1,1]{0,2,3,1:T(1,128)S(1)} %copy.113, f32[8,8,128,128]{3,2,1,0:T(8,128)} %bitcast.117), kind=kOutput, calls=%fused_computation.2 | convolution fusion | flops 12582912 | bytes 4718848 | tf_op jit(solution)/shard_map/jh,jhab->hab/dot_general | solution.py:99
  147.0 288.4 %all-gather.18.cloned.1.call-done = f32[256,128,128]{2,1,0:T(8,128)} async-done(((f32[8,128,128]{2,1,0:T(8,128)}), f32[256,128,128]{2,1,0:T(8,128)}) %all-gather.18.cloned.1.call-update) | async-done | bytes 16777232 | tf_op jit(solution)/shard_map/all_gather | solution.py:9
  435.5 0.7 fusion.12
  436.6 0.6 fusion.53
  437.7 0.4 convolution_convert_fusion.1
  438.4 100.4 %all_to_all.25 = bf16[64,5,1024]{2,1,0:T(8,128)(2,1)S(1)} all-to-all(bf16[64,5,1024]{2,1,0:T(8,128)(2,1)S(1)} %reshape.181), channel_id=1, replica_groups=mesh['ctx'=32,'exp'=8,'dp'=2] {'ctx','dp'}, dimensions={0} | all-to-all | bytes 1310720 | tf_op jit(solution)/shard_map/all_to_all | solution.py:144
  538.7 0.3 reshape.182
  539.0 4.2 fusion.5
  543.3 4.5 fusion.7
  547.8 43.7 %all-gather.14.cloned.1.call-done = bf16[2560,1408]{1,0:T(8,128)(2,1)} async-done(((bf16[320,1408]{1,0:T(8,128)(2,1)}), bf16[2560,1408]{1,0:T(8,128)(2,1)}) %all-gather.14.cloned.1.call-update) | async-done | bytes 7208976 | tf_op jit(solution)/shard_map/all_gather | solution.py:165
  591.5 5.1 convolution_convert_fusion
  596.6 14.7 %all_to_all.26 = bf16[8,320,128]{2,1,0:T(8,128)(2,1)S(1)} all-to-all(bf16[8,320,128]{2,1,0:T(8,128)(2,1)S(1)} %bitcast.126), channel_id=1, replica_groups=mesh['ctx'=32,'exp'=8,'dp'=2] {'exp'}, dimensions={0} | all-to-all | bytes 1310720 | tf_op jit(solution)/shard_map/all_to_all | solution.py:170
  611.3 0.4 copy.108
  611.7 1.7 reshape_reshape.3
  613.4 15.7 %all-to-all-start.2 = ((bf16[64,5,1024]{2,1,0:T(8,128)(2,1)}), bf16[64,5,1024]{2,1,0:T(8,128)(2,1)S(1)}, u32[]{:S(2)}, u32[]{:S(2)}) async-start(bf16[64,5,1024]{2,1,0:T(8,128)(2,1)} %reshape_reshape.3), calls=%async_computation.2 | async-start | bytes 2097152 | tf_op jit(solution)/shard_map/all_to_all | solution.py:177
  629.5 54.6 %all-to-all-done.2 = bf16[64,5,1024]{2,1,0:T(8,128)(2,1)S(1)} async-done(((bf16[64,5,1024]{2,1,0:T(8,128)(2,1)}), bf16[64,5,1024]{2,1,0:T(8,128)(2,1)S(1)}, u32[]{:S(2)}, u32[]{:S(2)}) %all-to-all-start.2) | async-done | bytes 655392 | tf_op jit(solution)/shard_map/all_to_all | solution.py:177
  684.4 0.4 fusion.14
  684.7 1.1 fusion.17
  (95 shorter events, 5.2 us)
Async XLA Ops:
  6.5 585.0 %copy-start = (bf16[1,128,1408]{2,1,0:T(8,128)(2,1)S(1)}, bf16[1,128,1408]{2,1,0:T(8,128)(2,1)}, u32[]{:S(2)}) copy-start(bf16[1,128,1408]{2,1,0:T(8,128)(2,1)} %param.25) | copy-start | bytes 1081348
  6.5 1.7 copy-start.11
  6.5 51.6 %all-gather.16.cloned.1.call-start = ((), (), s32[]{:S(2)}) async-start(), calls=%async_computation.6 | async-start | bytes 4718592 | tf_op jit(solution)/shard_map/all_gather | solution.py:88
  7.7 1.2 copy-start.14
  9.2 2.0 copy-start.8
  10.9 0.7 copy-start.2
  11.5 0.7 copy-start.4
  11.6 0.8 copy-start.6
  14.0 421.4 %all-gather.18.cloned.1.call-start = ((), (), s32[]{:S(2)}) async-start(), calls=%async_computation.7 | async-start | bytes 17301504 | tf_op jit(solution)/shard_map/all_gather | solution.py:9
  58.1 10.4 %copy-start.15 = (s32[1,128,2]{1,2,0:T(2,128)S(1)}, s32[1,128,2]{1,2,0:T(2,128)}, u32[]{:S(2)}) copy-start(s32[1,128,2]{1,2,0:T(2,128)} %param.21) | copy-start | bytes 3076
  58.1 80.3 %copy-start.10 = (f32[128,8]{1,0:T(8,128)S(1)}, f32[128,8]{1,0:T(8,128)}, u32[]{:S(2)}) copy-start(f32[128,8]{1,0:T(8,128)} %get-tuple-element.74) | copy-start | bytes 12292
  58.1 80.3 %copy-start.9 = (f32[128,8]{1,0:T(8,128)S(1)}, f32[128,8]{1,0:T(8,128)}, u32[]{:S(2)}) copy-start(f32[128,8]{1,0:T(8,128)} %copy-done.8) | copy-start | bytes 12292
  67.2 471.8 %all-gather.10.cloned.1.call-start = ((), (), s32[]{:S(2)}) async-start(), calls=%async_computation.3 | async-start | bytes 3244032 | tf_op jit(solution)/shard_map/all_gather | solution.py:153
  67.9 475.3 %all-gather.12.cloned.1.call-start = ((), (), s32[]{:S(2)}) async-start(), calls=%async_computation.4 | async-start | bytes 3244032 | tf_op jit(solution)/shard_map/all_gather | solution.py:158
  68.5 523.0 %all-gather.14.cloned.1.call-start = ((), (), s32[]{:S(2)}) async-start(), calls=%async_computation.5 | async-start | bytes 8110080 | tf_op jit(solution)/shard_map/all_gather | solution.py:165
  435.4 1.0 copy-start.3
  435.4 1.0 copy-start.5
  435.5 1.1 copy-start.7
  436.5 1.0 copy-start.1
  436.5 1.0 copy-start.12
  436.5 1.2 copy-start.13
  611.3 18.2 %copy-start.16 = (f32[1,128,2]{1,2,0:T(2,128)S(1)}, f32[1,128,2]{1,2,0:T(2,128)}, u32[]{:S(2)}) copy-start(f32[1,128,2]{1,2,0:T(2,128)} %param.22) | copy-start | bytes 3076
  613.4 70.7 %all-to-all-start.2 = ((bf16[64,5,1024]{2,1,0:T(8,128)(2,1)}), bf16[64,5,1024]{2,1,0:T(8,128)(2,1)S(1)}, u32[]{:S(2)}, u32[]{:S(2)}) async-start(bf16[64,5,1024]{2,1,0:T(8,128)(2,1)} %reshape_reshape.3), calls=%async_computation.2 | async-start | bytes 2097152 | tf_op jit(solution)/shard_map/all_to_all | solution.py:177
Sparse Core Ops, SparseCore 0:
  14.1 43.9 all-gather.15
  67.3 368.0 all-gather.17
  437.5 35.4 all-gather.9
  475.0 34.6 all-gather.11
  547.9 43.5 all-gather.13
where the time goes:
time: 694 us; the launch traced here: 692 us
  waiting for transfers between devices  421 us (61%)
  blocking collectives  194 us (28%)
  matrix products  35.7 us (5%)
  starting transfers between devices  15.9 us (2%)
  between operations  13.6 us (2%)
  local copies, waits for them, and re-layouts  9.16 us (1%)
    all_gather x1, waiting for transfers between devices, carried_in(): gathered = jax.tree.map(lambda a: lax.all_gather(a, axis), part)  288 us
    all_to_all x1, blocking collectives, body(): lax.all_to_all(outgoing.reshape(expert_count, capacity, model_width), ('c...  100 us
    all_gather x1, blocking collectives, carried_in(): gathered = jax.tree.map(lambda a: lax.all_gather(a, axis), part)  68.1 us
    all_to_all x1, waiting for transfers between devices, body(): lax.all_to_all(expert_out.reshape(expert_count, capacity, model_width), (...  54.6 us
    all_gather x1, waiting for transfers between devices, body(): lax.all_gather(hidden, 'exp', axis=0, tiled=True)  43.7 us
    all_gather x1, waiting for transfers between devices, body(): lax.all_gather(block_summary[None], 'exp', axis=0, tiled=True)  33.3 us
    all_to_all x1, starting transfers between devices, body(): lax.all_to_all(expert_out.reshape(expert_count, capacity, model_width), (...  15.7 us
    all_to_all x1, blocking collectives, body(): lax.all_to_all(partial_out.reshape(group_count, slot_count, local_feature...  14.7 us
  transfers between devices with their start and end apart: 6, of which 4 were waited for; matrix products, arithmetic and copies ran while one was open for 3% of the time, Pallas kernels for 0%

commit v1 on v0

v1 whole, which is shorter than its diff:
```python
import jax
import jax.numpy as jnp
from jax import lax
from jax.sharding import Mesh, PartitionSpec as P

CTX = ("z", "ylo")
EXP = ("x", "core")
OWNERS = ("z", "ylo", "yhi")


def exchange(blocks, axes):
    return lax.all_to_all(blocks, axes, split_axis=0, concat_axis=0, tiled=True)


def rotate(vectors, token_position):
    half_dim = vectors.shape[-1] // 2
    inverse = 10000.0 ** (-jnp.arange(half_dim, dtype=jnp.float32) / half_dim)
    angles = token_position.astype(jnp.float32)[:, None] * inverse[None, :]
    cosine = jnp.cos(angles)[:, None, :]
    sine_part = jnp.sin(angles)[:, None, :]
    leading = vectors[..., :half_dim]
    trailing = vectors[..., half_dim:]
    return jnp.concatenate(
        [leading * cosine - trailing * sine_part, trailing * cosine + leading * sine_part], axis=-1
    )


def entering_state(block_summary, block_log):
    member_count = lax.axis_size(EXP)
    ctx_count = lax.axis_size(CTX)
    own_head = lax.axis_index(EXP)
    own_ctx = lax.axis_index(CTX)
    all_logs = lax.all_gather(block_log, CTX + EXP, axis=0).reshape(ctx_count, member_count, -1)
    head_logs = lax.dynamic_index_in_dim(all_logs, own_head, 2, keepdims=False)
    group_logs = jnp.sum(head_logs, axis=1)
    own_logs = lax.dynamic_index_in_dim(head_logs, own_ctx, 0, keepdims=False)
    members = jnp.arange(member_count)
    ctxs = jnp.arange(ctx_count)

    summaries = exchange(block_summary.astype(jnp.bfloat16), EXP).astype(jnp.float32)
    after = jnp.exp(jnp.sum(jnp.where(members[None, :] > members[:, None], own_logs[None, :], 0.0), 1))
    group_sum = jnp.sum(after[:, None, None] * summaries, axis=0)
    group_sums = lax.all_gather(group_sum.astype(jnp.bfloat16), CTX, axis=0).astype(jnp.float32)
    between = (ctxs[None, :] > ctxs[:, None]) & (ctxs[None, :] < own_ctx)
    reach = jnp.exp(jnp.sum(jnp.where(between, group_logs[None, :], 0.0), 1))
    reach = jnp.where(ctxs < own_ctx, reach, 0.0)
    leading = jnp.sum(reach[:, None, None] * group_sums, axis=0)

    to_block = jnp.exp(jnp.sum(jnp.where(members[None, :] < members[:, None], own_logs[None, :], 0.0), 1))
    inner = (members[None, None, :] > members[None, :, None]) & (
        members[None, None, :] < members[:, None, None]
    )
    inner = jnp.exp(jnp.sum(jnp.where(inner, own_logs[None, None, :], 0.0), 2))
    inner = jnp.where(members[None, :] < members[:, None], inner, 0.0)
    entering = to_block[:, None, None] * leading[None] + jnp.sum(
        inner[:, :, None, None] * summaries[None], axis=1
    )
    return exchange(entering.astype(jnp.bfloat16), EXP)


def body(
    hidden_in,
    queries,
    keys,
    values,
    log_decay,
    retention_gain,
    norm_gain,
    routes,
    route_weights,
    w_gate,
    w_up,
    w_down,
):
    tok_rows = hidden_in.shape[1]
    model_width = hidden_in.shape[2]
    head_count = log_decay.shape[2]
    head_dim = model_width // head_count
    block_index = lax.axis_index(CTX) * lax.axis_size(EXP) + lax.axis_index(EXP)
    token_position = block_index * tok_rows + jnp.arange(tok_rows, dtype=jnp.int32)
    per_head_keys = rotate(
        keys[0].astype(jnp.float32).reshape(tok_rows, head_count, head_dim), token_position
    ).astype(jnp.bfloat16)
    per_head_values = values[0].reshape(tok_rows, head_count, head_dim)
    running_total = jnp.cumsum(log_decay[0], axis=0)
    trailing_decay = jnp.exp(running_total[-1][None, :] - running_total)
    block_summary = jnp.einsum(
        "qpf,qpy->pfy",
        (per_head_keys.astype(jnp.float32) * trailing_decay[:, :, None]),
        per_head_values.astype(jnp.float32),
        precision=lax.Precision.HIGHEST,
    )
    state_in = entering_state(block_summary, running_total[-1])

    per_head_queries = (
        rotate(
            queries[0].astype(jnp.float32).reshape(tok_rows, head_count, head_dim), token_position
        )
        * head_dim ** (-0.5)
    ).astype(jnp.bfloat16)
    scores = jnp.einsum(
        "thd,shd->hts", per_head_queries, per_head_keys, preferred_element_type=jnp.float32
    )
    causal = jnp.arange(tok_rows)[:, None] >= jnp.arange(tok_rows)[None, :]
    spread = running_total.T[:, :, None] - running_total.T[:, None, :]
    weights = jnp.where(
        causal[None], scores * jnp.exp(jnp.where(causal[None], spread, 0.0)), 0.0
    ).astype(jnp.bfloat16)
    inside = jnp.einsum(
        "hts,shd->thd", weights, per_head_values, preferred_element_type=jnp.float32
    )
    external_part = jnp.exp(running_total)[:, :, None] * jnp.einsum(
        "wjc,jco->wjo", per_head_queries, state_in, preferred_element_type=jnp.float32
    )
    retrieved = inside + external_part
    centre = jnp.mean(retrieved, axis=-1, keepdims=True)
    deviation = retrieved - centre
    variance = jnp.mean(deviation * deviation, axis=-1, keepdims=True)
    normalized = (deviation * lax.rsqrt(variance + 1e-05)).reshape(tok_rows, model_width)
    residual = hidden_in[0].astype(jnp.float32) + retention_gain * normalized
    square_mean = jnp.mean(residual * residual, axis=-1, keepdims=True)
    normed = (residual * lax.rsqrt(square_mean + 1e-06) * norm_gain).astype(jnp.bfloat16)

    expert_count = lax.axis_size(OWNERS)
    top_count = routes.shape[2]
    capacity = (tok_rows * top_count * 5 + 4 * expert_count - 1) // (4 * expert_count)
    slot_count = expert_count * capacity
    route_rows = routes[0]
    expert_hits = (
        route_rows.reshape(tok_rows * top_count)[:, None]
        == jnp.arange(expert_count, dtype=jnp.int32)[None, :]
    ).astype(jnp.int32)
    earlier = jnp.cumsum(expert_hits, axis=0) - expert_hits
    slot_rank = jnp.sum(earlier * expert_hits, axis=1).reshape(tok_rows, top_count)
    destination = route_rows * capacity + slot_rank
    slot_lanes = jnp.arange(slot_count, dtype=jnp.int32)
    placing = jnp.any(destination[None, :, :] == slot_lanes[:, None, None], axis=2).astype(
        jnp.bfloat16
    )
    outgoing = jnp.dot(placing, normed, preferred_element_type=jnp.float32).astype(jnp.bfloat16)
    lanes = 128
    packed = (expert_count, capacity * model_width // lanes, lanes)
    arrived = exchange(outgoing.reshape(packed), OWNERS).reshape(slot_count, model_width)
    gate_full = lax.all_gather(w_gate[0], EXP, axis=0, tiled=True)
    up_full = lax.all_gather(w_up[0], EXP, axis=0, tiled=True)
    down_full = lax.all_gather(w_down[0], EXP, axis=0, tiled=True)
    gate_next = jnp.dot(arrived, gate_full, preferred_element_type=jnp.float32)
    up_next = jnp.dot(arrived, up_full, preferred_element_type=jnp.float32)
    hidden = (jax.nn.silu(gate_next) * up_next).astype(jnp.bfloat16)
    expert_out = lax.dot_general(
        hidden, down_full, (((1,), (1,)), ((), ())), preferred_element_type=jnp.float32
    ).astype(jnp.bfloat16)
    returned = exchange(expert_out.reshape(packed), OWNERS).reshape(slot_count, model_width)
    output = residual
    for route_index in range(top_count):
        picking = (destination[:, route_index][:, None] == slot_lanes[None, :]).astype(jnp.bfloat16)
        routed = jnp.dot(picking, returned, preferred_element_type=jnp.float32)
        output = output + route_weights[0][:, route_index][:, None] * routed
    return output.astype(jnp.bfloat16)[None]


def solution(mesh):
    ctx, exp, dp = mesh.shape["ctx"], mesh.shape["exp"], mesh.shape["dp"]
    split = Mesh(
        mesh.devices.reshape(ctx // 2, 2, exp // 2, 2, dp), ("z", "ylo", "x", "core", "yhi")
    )
    tokens = P("yhi", CTX + EXP, None)
    experts = P(OWNERS, EXP, None)
    in_specs = (tokens,) * 5 + (P(), P()) + (tokens,) * 2 + (experts,) * 3
    return jax.shard_map(body, mesh=split, in_specs=in_specs, out_specs=tokens, check_vma=False)
```

time: 694 us -> 634 us (0.914)
  the two profiles are of different devices: /device:TPU:16 before, /device:TPU:8 now
where the time goes in v1:
time: 634 us
  blocking collectives  358 us (56%)
  waiting for transfers between devices  209 us (33%)
  starting transfers between devices  24.4 us (4%)
  matrix products  14 us (2%)
  between operations  13.6 us (2%)
  local copies, waits for them, and re-layouts  8.17 us (1%)
  other arithmetic  6.77 us (1%)
    all_gather x1, blocking collectives, entering_state(): lax.all_gather(block_log, CTX + EXP, axis=0)  305 us
    all_gather x1, waiting for transfers between devices, entering_state(): lax.all_gather(group_sum.astype(jnp.bfloat16), CTX, axis=0)  125 us
    all_to_all x1, blocking collectives, exchange(): return lax.all_to_all(blocks, axes, split_axis=0, concat_axis=0, tiled=True)  52.5 us
    all_to_all x3, waiting for transfers between devices, exchange(): return lax.all_to_all(blocks, axes, split_axis=0, concat_axis=0, tiled=True)  45.5 us
    all_gather x1, waiting for transfers between devices, body(): down_full = lax.all_gather(w_down[0], EXP, axis=0, tiled=True)  36.3 us
    all_to_all x3, starting transfers between devices, exchange(): return lax.all_to_all(blocks, axes, split_axis=0, concat_axis=0, tiled=True)  24.2 us
  transfers between devices with their start and end apart: 7, of which 4 were waited for; matrix products, arithmetic and copies ran while one was open for 2% of the time, Pallas kernels for 0%

profile of v1, /device:TPU:8, one launch (start us, length us, event | category | flops | bytes accessed | tf_op | source)
XLA Modules:
  0.0 633.6 jit_solution(9688745371011176003)
XLA Ops:
  6.6 1.2 copy.84
  9.2 1.0 copy.114
  10.2 0.3 multiply_cosine_fusion
  10.6 0.3 multiply_subtract_fusion
  10.9 0.7 copy-done.1
  11.7 1.5 convolution_convert_fusion.1
  13.2 4.3 all-to-all-start
  17.6 305.4 %all-gather.4 = f32[256,1,8]{2,1,0:T(1,128)S(1)} all-gather(f32[1,1,8]{2,1,0:T(1,128)S(1)} %get-tuple-element.21), channel_id=1, replica_groups=mesh['z'=16,'ylo'=2,'x'=4,'core'=2,'yhi'=2] {'z','ylo','x','core'}, dimensions={0}, use_global_device_ids=true | all-gather | bytes 8224 | tf_op jit(solution)/shard_map/all_gather | solution.py:33
  323.3 0.7 multiply_reduce_fusion.3
  324.1 0.7 all-gather.12.cloned.1.call-update
  324.9 0.7 all-gather.14.cloned.1.call-update
  325.6 0.5 all-gather.16.cloned.1.call-update
  326.2 0.5 dynamic-slice_reduce_fusion
  327.3 0.6 reduce-window.6
  328.6 0.6 multiply_reduce_fusion
  329.4 125.0 %all-gather.10.cloned.1.call-done = bf16[4096,128]{1,0:T(8,128)(2,1)} async-done(((bf16[128,128]{1,0:T(8,128)(2,1)}), bf16[4096,128]{1,0:T(8,128)(2,1)}) %all-gather.10.cloned.1.call-update) | async-done | bytes 1048592 | tf_op jit(solution)/shard_map/all_gather | solution.py:43
  454.4 1.5 fusion.8
  456.0 0.8 add_convert_fusion
  456.9 4.2 all-to-all-start.1
  461.4 7.1 %all-to-all-done.1 = bf16[8,128,128]{1,2,0:T(8,128)(2,1)S(1)} async-done(((bf16[8,128,128]{1,2,0:T(8,128)(2,1)}), bf16[8,128,128]{1,2,0:T(8,128)(2,1)S(1)}, u32[]{:S(2)}, u32[]{:S(2)}) %all-to-all-start.1) | async-done | bytes 262176 | tf_op jit(solution)/shard_map/all_to_all | solution.py:12
  468.6 0.3 fusion.13
  468.9 0.6 fusion.53
  470.2 0.4 convolution_convert_fusion
  470.9 52.5 %all_to_all.20 = bf16[64,40,128]{2,1,0:T(8,128)(2,1)S(1)} all-to-all(bf16[64,40,128]{2,1,0:T(8,128)(2,1)S(1)} %reshape.252), channel_id=1, replica_groups=mesh['z'=16,'ylo'=2,'x'=4,'core'=2,'yhi'=2] {'z','ylo','yhi'}, dimensions={0} | all-to-all | bytes 1310720 | tf_op jit(solution)/shard_map/all_to_all | solution.py:12
  523.7 4.3 fusion.3
  528.0 36.3 %all-gather.16.cloned.1.call-done = bf16[1,1024,1408]{2,1,0:T(8,128)(2,1)} async-done(((bf16[1,128,1408]{2,1,0:T(8,128)(2,1)}), bf16[1,1024,1408]{2,1,0:T(8,128)(2,1)}) %all-gather.16.cloned.1.call-update) | async-done | bytes 2883600 | tf_op jit(solution)/shard_map/all_gather | solution.py:146
  564.3 5.4 fusion.9
  569.8 1.1 reshape.254
  570.9 15.7 %all-to-all-start.3 = ((bf16[64,40,128]{2,1,0:T(8,128)(2,1)}), bf16[64,40,128]{2,1,0:T(8,128)(2,1)S(1)}, u32[]{:S(2)}, u32[]{:S(2)}) async-start(bf16[64,40,128]{2,1,0:T(8,128)(2,1)} %reshape.254), calls=%async_computation.3 | async-start | bytes 1310720 | tf_op jit(solution)/shard_map/all_to_all | solution.py:12
  587.0 38.4 %all-to-all-done.3 = bf16[64,40,128]{2,1,0:T(8,128)(2,1)S(1)} async-done(((bf16[64,40,128]{2,1,0:T(8,128)(2,1)}), bf16[64,40,128]{2,1,0:T(8,128)(2,1)S(1)}, u32[]{:S(2)}, u32[]{:S(2)}) %all-to-all-start.3) | async-done | bytes 655392 | tf_op jit(solution)/shard_map/all_to_all | solution.py:12
  625.7 0.4 fusion.16
  626.0 1.1 fusion.19
  (87 shorter events, 5.8 us)
Async XLA Ops:
  6.5 1.7 copy-start.5
  8.0 0.9 copy-start.8
  10.9 0.7 copy-start.1
  10.9 0.8 copy-start.3
  10.9 315.8 %copy-start.9 = (s32[1,128,2]{1,2,0:T(2,128)S(1)}, s32[1,128,2]{1,2,0:T(2,128)}, u32[]{:S(2)}) copy-start(s32[1,128,2]{1,2,0:T(2,128)} %param.19) | copy-start | bytes 3076
  13.2 310.1 %all-to-all-start = ((bf16[8,128,128]{2,1,0:T(8,128)(2,1)}), bf16[8,128,128]{2,1,0:T(8,128)(2,1)S(1)}, u32[]{:S(2)}, u32[]{:S(2)}) async-start(bf16[8,128,128]{2,1,0:T(8,128)(2,1)} %convolution_convert_fusion.1), calls=%async_computation | async-start | bytes 524288 | tf_op jit(solution)/shard_map/all_to_all | solution.py:12
  17.5 436.9 %all-gather.10.cloned.1.call-start = ((), (), s32[]{:S(2)}) async-start(), calls=%async_computation.4 | async-start | bytes 1081344 | tf_op jit(solution)/shard_map/all_gather | solution.py:43
  324.1 199.6 %all-gather.12.cloned.1.call-start = ((), (), s32[]{:S(2)}) async-start(), calls=%async_computation.5 | async-start | bytes 3244032 | tf_op jit(solution)/shard_map/all_gather | solution.py:144
  324.8 203.2 %all-gather.14.cloned.1.call-start = ((), (), s32[]{:S(2)}) async-start(), calls=%async_computation.6 | async-start | bytes 3244032 | tf_op jit(solution)/shard_map/all_gather | solution.py:145
  325.6 238.7 %all-gather.16.cloned.1.call-start = ((), (), s32[]{:S(2)}) async-start(), calls=%async_computation.7 | async-start | bytes 3244032 | tf_op jit(solution)/shard_map/all_gather | solution.py:146
  455.9 12.9 %copy-start.2 = (bf16[128,8,64]{2,0,1:T(8,128)(2,1)S(1)}, bf16[128,8,64]{2,0,1:T(8,128)(2,1)}, u32[]{:S(2)}) copy-start(bf16[128,8,64]{2,0,1:T(8,128)(2,1)} %copy-done.1) | copy-start | bytes 393220
  455.9 12.9 %copy-start.4 = (bf16[128,8,64]{2,0,1:T(8,128)(2,1)S(1)}, bf16[128,8,64]{2,0,1:T(8,128)(2,1)}, u32[]{:S(2)}) copy-start(bf16[128,8,64]{2,0,1:T(8,128)(2,1)} %copy-done.3) | copy-start | bytes 393220
  456.9 11.7 %all-to-all-start.1 = ((bf16[8,128,128]{1,2,0:T(8,128)(2,1)}), bf16[8,128,128]{1,2,0:T(8,128)(2,1)S(1)}, u32[]{:S(2)}, u32[]{:S(2)}) async-start(bf16[8,128,128]{1,2,0:T(8,128)(2,1)} %add_convert_fusion), calls=%async_computation.1 | async-start | bytes 524288 | tf_op jit(solution)/shard_map/all_to_all | solution.py:12
  468.9 1.0 copy-start
  468.9 1.0 copy-start.6
  469.5 0.7 copy-start.7
  569.8 17.2 %copy-start.10 = (f32[1,128,2]{1,2,0:T(2,128)S(1)}, f32[1,128,2]{1,2,0:T(2,128)}, u32[]{:S(2)}) copy-start(f32[1,128,2]{1,2,0:T(2,128)} %param.20) | copy-start | bytes 3076
  570.9 54.5 %all-to-all-start.3 = ((bf16[64,40,128]{2,1,0:T(8,128)(2,1)}), bf16[64,40,128]{2,1,0:T(8,128)(2,1)S(1)}, u32[]{:S(2)}, u32[]{:S(2)}) async-start(bf16[64,40,128]{2,1,0:T(8,128)(2,1)} %reshape.254), calls=%async_computation.3 | async-start | bytes 1310720 | tf_op jit(solution)/shard_map/all_to_all | solution.py:12
Sparse Core Ops, SparseCore 0:
  324.2 130.1 all-gather.9
  456.5 34.1 all-gather.11
  492.9 34.6 all-gather.13
  529.6 34.6 all-gather.15

commit v2 on v1

v2 whole, which is shorter than its diff:
```python
import jax
import jax.numpy as jnp
import numpy as np
from jax import lax
from jax.experimental import pallas as pl
from jax.experimental.pallas import tpu as pltpu
from jax.sharding import Mesh, PartitionSpec as P

CTX = ("z", "ylo")
EXP = ("x", "core")
PLANE = ("ylo", "x", "core")
OWNERS = ("z", "ylo", "yhi")
LOG_ROWS = 8
F32, BF16 = jnp.float32, jnp.bfloat16


def exchange(blocks, axes):
    return lax.all_to_all(blocks, axes, split_axis=0, concat_axis=0, tiled=True)


def dot32(left, right):
    return jnp.dot(left, right, preferred_element_type=F32)


def cost(flops, moved):
    return pl.CostEstimate(flops=flops, bytes_accessed=moved, transcendentals=flops // 1000)


def log_rows(value):
    high = value.astype(BF16).astype(F32)
    middle = (value - high).astype(BF16).astype(F32)
    low = value - high - middle
    line = lax.broadcasted_iota(jnp.int32, (LOG_ROWS, value.shape[1]), 0)
    rows = jnp.where(line == 0, high, jnp.where(line == 1, middle, jnp.where(line == 2, low, 0.0)))
    return rows.astype(BF16)


def log_row(rows):
    return jnp.sum(rows.astype(F32), axis=0, keepdims=True)


def turned(block, cosine, sine):
    return block * cosine + pltpu.roll(block, block.shape[1] // 2, 1) * sine


def summary_kernel(keys_ref, values_ref, log_ref, cos_ref, sin_ref, message_ref, turned_ref, total_ref):
    heads, count = log_ref.shape
    head_dim = cos_ref.shape[1]
    parts = message_ref.shape[0] // heads
    rows = head_dim // parts
    earlier = lax.broadcasted_iota(jnp.int32, (count, count), 0)
    upto = lax.broadcasted_iota(jnp.int32, (count, count), 1)
    ones = jnp.where(earlier <= upto, 1.0, 0.0).astype(F32)
    total = jnp.dot(
        log_ref[...], ones, precision=lax.Precision.HIGHEST, preferred_element_type=F32
    )
    total_ref[...] = total
    last = total[:, count - 1 :]
    trailing = jnp.exp(last - total)
    wide = jnp.broadcast_to(last, (heads, head_dim))
    for head in range(heads):
        lanes = slice(head * head_dim, (head + 1) * head_dim)
        keys = turned(keys_ref[:, lanes].astype(F32), cos_ref[...], sin_ref[...]).astype(BF16)
        turned_ref[:, lanes] = keys
        faded = keys.astype(F32).T * trailing[head : head + 1]
        coarse = faded.astype(BF16)
        fine = (faded - coarse.astype(F32)).astype(BF16)
        summary = dot32(coarse, values_ref[:, lanes]) + dot32(fine, values_ref[:, lanes])
        summary = summary.astype(BF16)
        logs = log_rows(wide[head : head + 1])
        for part in range(parts):
            message_ref[head * parts + part, :rows] = summary[part * rows : (part + 1) * rows]
            message_ref[head * parts + part, rows:] = logs


def inside_kernel(
    queries_ref, keys_ref, values_ref, total_ref, cos_ref, sin_ref, turned_ref, inside_ref, fade_ref
):
    heads, count = total_ref.shape
    head_dim = cos_ref.shape[1]
    row = lax.broadcasted_iota(jnp.int32, (count, count), 0)
    column = lax.broadcasted_iota(jnp.int32, (count, count), 1)
    causal = row >= column
    for head in range(heads):
        lanes = slice(head * head_dim, (head + 1) * head_dim)
        queries = turned(queries_ref[:, lanes].astype(F32), cos_ref[...], sin_ref[...])
        queries = (queries * head_dim ** (-0.5)).astype(BF16)
        turned_ref[:, lanes] = queries
        scores = lax.dot_general(
            queries, keys_ref[:, lanes], (((1,), (1,)), ((), ())), preferred_element_type=F32
        )
        here = total_ref[head : head + 1, :]
        down = jnp.broadcast_to(here, (head_dim, count)).T
        spread = jnp.where(causal, down - here, 0.0)
        weights = jnp.where(causal, scores * jnp.exp(spread), 0.0).astype(BF16)
        inside_ref[:, lanes] = dot32(weights, values_ref[:, lanes])
        fade_ref[:, lanes] = jnp.exp(down)


def plane_sum_kernel(arrived_ref, message_ref):
    plane, rows, head_dim = arrived_ref.shape
    rows = rows - LOG_ROWS
    total = jnp.zeros((rows, head_dim), F32)
    log_total = jnp.zeros((1, head_dim), F32)
    for block in range(plane):
        log = log_row(arrived_ref[block, rows:])
        total = jnp.exp(log) * total + arrived_ref[block, :rows].astype(F32)
        log_total = log_total + log
    total, logs = total.astype(BF16), log_rows(log_total)
    for z in range(message_ref.shape[0]):
        message_ref[z, :rows] = total
        message_ref[z, rows:] = logs


def entering_kernel(own_ref, arrived_ref, planes_ref, entering_ref):
    rows = entering_ref.shape[1]
    own = own_ref[0]
    state = jnp.zeros(entering_ref.shape[1:], F32)
    for z in range(planes_ref.shape[0]):
        log = log_row(planes_ref[z, rows:])
        later = jnp.exp(log) * state + planes_ref[z, :rows].astype(F32)
        state = jnp.where(z < own, later, state)
    for block in range(arrived_ref.shape[0]):
        entering_ref[block] = state.astype(BF16)
        log = log_row(arrived_ref[block, rows:])
        state = jnp.exp(log) * state + arrived_ref[block, :rows].astype(F32)


def outgoing_kernel(
    own_ref,
    state_ref,
    queries_ref,
    inside_ref,
    fade_ref,
    hidden_ref,
    group_gain_ref,
    norm_gain_ref,
    placing_ref,
    residual_ref,
    outgoing_ref,
    normed_ref,
):
    chunks, count, head_dim = normed_ref.shape
    square = jnp.zeros((count, 1), F32)
    for head in range(chunks):
        lanes = slice(head * head_dim, (head + 1) * head_dim)
        far = dot32(queries_ref[:, lanes], state_ref[head * head_dim : (head + 1) * head_dim, :])
        retrieved = inside_ref[:, lanes] + fade_ref[:, lanes] * far
        deviation = retrieved - jnp.mean(retrieved, axis=1, keepdims=True)
        variance = jnp.mean(deviation * deviation, axis=1, keepdims=True)
        normalized = deviation * lax.rsqrt(variance + 1e-05)
        residual = hidden_ref[:, lanes].astype(F32) + group_gain_ref[:, lanes] * normalized
        residual_ref[:, lanes] = residual
        square = square + jnp.sum(residual * residual, axis=1, keepdims=True)
    scale = lax.rsqrt(square * (1.0 / (chunks * head_dim)) + 1e-06)
    for chunk in range(chunks):
        lanes = slice(chunk * head_dim, (chunk + 1) * head_dim)
        normed = residual_ref[:, lanes] * scale * norm_gain_ref[:, lanes]
        normed_ref[own_ref[chunk]] = normed.astype(BF16)
    for chunk in range(chunks):
        lanes = slice(chunk * head_dim, (chunk + 1) * head_dim)
        outgoing_ref[:, lanes] = dot32(placing_ref[...], normed_ref[chunk]).astype(BF16)


def expert_kernel(*refs):
    arrived_ref, pieces, out_ref = refs[0], refs[1:-4], refs[-4]
    weights_ref, hidden_ref, sems = refs[-3], refs[-2], refs[-1]
    width = weights_ref.shape[2]
    copies = []
    for index in range(3):
        start = 0
        for number, piece in enumerate(pieces):
            size = piece.shape[1]
            copy = pltpu.make_async_copy(
                piece.at[index],
                weights_ref.at[index, pl.ds(start, size), :],
                sems.at[index, number],
            )
            copy.start()
            copies.append(copy)
            start += size
    count = len(pieces)
    for copy in copies[: 2 * count]:
        copy.wait()
    tile = 512
    for start in range(0, width, tile):
        columns = slice(start, min(width, start + tile))
        gate = dot32(arrived_ref[...], weights_ref[0, :, columns])
        up = dot32(arrived_ref[...], weights_ref[1, :, columns])
        hidden_ref[:, columns] = (gate / (1.0 + jnp.exp(-gate)) * up).astype(BF16)
    for copy in copies[2 * count :]:
        copy.wait()
    tile = 256
    for start in range(0, out_ref.shape[1], tile):
        rows = slice(start, start + tile)
        out_ref[:, rows] = lax.dot_general(
            hidden_ref[...],
            weights_ref[2, rows, :],
            (((1,), (1,)), ((), ())),
            preferred_element_type=F32,
        ).astype(BF16)


def shape(dims, kind):
    return jax.ShapeDtypeStruct(dims, kind)


def run_experts(arrived, pieces):
    rows, model_width = arrived.shape
    width = pieces[0].shape[2]
    anywhere = pl.BlockSpec(memory_space=pl.ANY)
    return pl.pallas_call(
        expert_kernel,
        name="experts",
        out_shape=shape((rows, model_width), BF16),
        in_specs=[pl.BlockSpec(memory_space=pltpu.VMEM)] + [anywhere] * len(pieces),
        out_specs=pl.BlockSpec(memory_space=pltpu.VMEM),
        scratch_shapes=[
            pltpu.VMEM((3, model_width, width), BF16),
            pltpu.VMEM((rows, width), BF16),
            pltpu.SemaphoreType.DMA((3, len(pieces))),
        ],
        cost_estimate=cost(6 * rows * model_width * width, 6 * model_width * width),
    )(arrived, *pieces)


def along_x(piece, step):
    size = lax.axis_size("x")
    return lax.ppermute(piece, "x", [(i, (i - step) % size) for i in range(size)])


def swapped(piece):
    return lax.ppermute(piece, "core", [(0, 1), (1, 0)])


def own_places():
    chips, cores = lax.axis_size("x"), lax.axis_size("core")
    chunk = jnp.arange(chips * cores, dtype=jnp.int32)
    chip = (chunk // cores + chips - lax.axis_index("x")) % chips
    return chip * cores + (chunk + lax.axis_index("core")) % cores


def model_order(rows):
    chips, cores = lax.axis_size("x"), lax.axis_size("core")
    count, width = rows.shape
    view = rows.reshape(count, chips, cores, width // (chips * cores))
    view = jnp.where(lax.axis_index("core") == 1, view[:, :, ::-1], view)
    start = (chips - lax.axis_index("x")) % chips
    twice = jnp.concatenate([view, view], axis=1)
    return lax.dynamic_slice_in_dim(twice, start, chips, axis=1).reshape(count, width)


def body(
    hidden_in,
    queries,
    keys,
    values,
    log_decay,
    retention_gain,
    norm_gain,
    routes,
    route_weights,
    w_gate,
    w_up,
    w_down,
):
    tok_rows = hidden_in.shape[1]
    model_width = hidden_in.shape[2]
    head_count = log_decay.shape[2]
    head_dim = model_width // head_count
    wide = (tok_rows, model_width)
    plane, depth = lax.axis_size(PLANE), lax.axis_size("z")
    part_rows = head_count * head_dim // plane
    message = (plane, part_rows + LOG_ROWS, head_dim)

    half = head_dim // 2
    inverse = (10000.0 ** (-np.arange(half) / half)).astype(np.float32)
    sign = np.repeat(np.array([-1.0, 1.0], np.float32), half)
    block_index = lax.axis_index(CTX) * lax.axis_size(EXP) + lax.axis_index(EXP)
    position = block_index * tok_rows + jnp.arange(tok_rows, dtype=jnp.int32)
    angles = position.astype(F32)[:, None] * np.tile(inverse, 2)[None, :]
    cosine, sine = jnp.cos(angles), jnp.sin(angles) * sign

    out_message, turned_keys, total = pl.pallas_call(
        summary_kernel,
        name="summary",
        out_shape=(shape(message, BF16), shape(wide, BF16), shape((head_count, tok_rows), F32)),
        cost_estimate=cost(70000000, 1200000),
    )(keys[0], values[0], log_decay[0].T, cosine, sine)
    summaries = exchange(out_message, PLANE)
    stacked = jnp.stack([w_gate[0], w_up[0], w_down[0]])
    after, before = along_x(stacked, 1), along_x(stacked, -1)
    turned_queries, inside, fade = pl.pallas_call(
        inside_kernel,
        name="inside",
        out_shape=(shape(wide, BF16), shape(wide, F32), shape(wide, F32)),
        cost_estimate=cost(70000000, 2200000),
    )(queries[0], turned_keys, values[0], total, cosine, sine)
    sums = pl.pallas_call(
        plane_sum_kernel,
        name="plane_sum",
        out_shape=shape((depth,) + message[1:], BF16),
        cost_estimate=cost(500000, 600000),
    )(summaries)
    sums = exchange(sums, "z")
    own_other = swapped(stacked)
    entering = pl.pallas_call(
        entering_kernel,
        name="enter",
        out_shape=shape((plane, part_rows, head_dim), BF16),
        in_specs=[pl.BlockSpec(memory_space=pltpu.SMEM)]
        + [pl.BlockSpec(memory_space=pltpu.VMEM)] * 2,
        cost_estimate=cost(900000, 900000),
    )(lax.axis_index("z")[None], summaries, sums)
    state_in = exchange(entering, PLANE).reshape(model_width, head_dim)
    after_other, before_other = swapped(after), swapped(before)

    expert_count = lax.axis_size(OWNERS)
    top_count = routes.shape[2]
    capacity = (tok_rows * top_count * 5 + 4 * expert_count - 1) // (4 * expert_count)
    slot_count = expert_count * capacity
    route_rows = routes[0]
    expert_hits = (
        route_rows.reshape(tok_rows * top_count)[:, None]
        == jnp.arange(expert_count, dtype=jnp.int32)[None, :]
    ).astype(jnp.int32)
    earlier = jnp.cumsum(expert_hits, axis=0) - expert_hits
    slot_rank = jnp.sum(earlier * expert_hits, axis=1).reshape(tok_rows, top_count)
    destination = route_rows * capacity + slot_rank
    slot_lanes = jnp.arange(slot_count, dtype=jnp.int32)
    placing = jnp.any(destination[None, :, :] == slot_lanes[:, None, None], axis=2).astype(BF16)

    residual, outgoing = pl.pallas_call(
        outgoing_kernel,
        name="outgoing",
        out_shape=(shape(wide, F32), shape((slot_count, model_width), BF16)),
        in_specs=[pl.BlockSpec(memory_space=pltpu.SMEM)]
        + [pl.BlockSpec(memory_space=pltpu.VMEM)] * 8,
        scratch_shapes=[pltpu.VMEM((head_count, tok_rows, head_dim), BF16)],
        cost_estimate=cost(120000000, 3000000),
    )(
        own_places(),
        state_in,
        turned_queries,
        inside,
        fade,
        hidden_in[0],
        retention_gain[None],
        norm_gain[None],
        placing,
    )
    lanes = 128
    packed = (expert_count, capacity * model_width // lanes, lanes)
    arrived = exchange(outgoing.reshape(packed), OWNERS).reshape(slot_count, model_width)
    cut = stacked.shape[1] // 2
    far = [along_x(after[:, :cut], 1), along_x(before[:, cut:], -1)]
    far_other = [swapped(piece) for piece in far]
    pieces = [stacked, own_other, after, after_other, *far, *far_other, before, before_other]
    expert_out = run_experts(arrived, pieces)
    returned = exchange(expert_out.reshape(packed), OWNERS).reshape(slot_count, model_width)
    mixed = jnp.zeros(wide, F32)
    for route_index in range(top_count):
        picking = (destination[:, route_index][:, None] == slot_lanes[None, :]).astype(BF16)
        routed = dot32(picking, returned)
        mixed = mixed + route_weights[0][:, route_index][:, None] * routed
    return (residual + model_order(mixed)).astype(BF16)[None]


def solution(mesh):
    ctx, exp, dp = mesh.shape["ctx"], mesh.shape["exp"], mesh.shape["dp"]
    split = Mesh(
        mesh.devices.reshape(ctx // 2, 2, exp // 2, 2, dp), ("z", "ylo", "x", "core", "yhi")
    )
    tokens = P("yhi", CTX + EXP, None)
    experts = P(OWNERS, EXP, None)
    in_specs = (tokens,) * 5 + (P(), P()) + (tokens,) * 2 + (experts,) * 3
    return jax.shard_map(body, mesh=split, in_specs=in_specs, out_specs=tokens, check_vma=False)
```

time: 634 us -> 212 us (0.33)
  blocking collectives: 358 us -> 16.7 us
  waiting for transfers between devices: 209 us -> 89.8 us
  starting transfers between devices: 24.4 us -> 63.7 us
  Pallas kernels: 0 us -> 21.3 us
  matrix products: 14 us -> 0.7 us
  between operations: 13.6 us -> 0.36 us
    all_gather x1 -> x0, blocking collectives: 305 us -> none  [entering_state(): lax.all_gather(block_log, CTX + EXP, axis=0)]
    all_gather x4 -> x0, waiting for transfers between devices: 161 us -> none  [the longest x1 125 us: entering_state(): lax.all_gather(group_sum.astype(jnp.bfloat16), CTX, axis=0)]
    all_to_all x1, blocking collectives: 52.5 us -> 16.7 us  [exchange(): return lax.all_to_all(blocks, axes, split_axis=0, concat_axis=0, tiled=True)]
    ppermute x0 -> x9, waiting for transfers between devices: none -> 32 us  [the longest x4 30.9 us: along_x(): lax.ppermute(piece, 'x', [(i, (i - step) % size) for i in range(size)])]
    ppermute x0 -> x9, starting transfers between devices: none -> 22.4 us  [the longest x4 12.4 us: along_x(): lax.ppermute(piece, 'x', [(i, (i - step) % size) for i in range(size)])]
    pallas_call x0 -> x6, Pallas kernels: none -> 21.3 us  [the longest x1 8.28 us: run_experts(): pl.pallas_call(expert_kernel, name='experts', out_shape=shape((rows, mode...]
    all_to_all x3 -> x4, starting transfers between devices: 24.2 us -> 41.2 us  [exchange(): return lax.all_to_all(blocks, axes, split_axis=0, concat_axis=0, tiled=True)]
    dot_general x8 -> x2, matrix products: 14 us -> 0.7 us  [dot32(): return jnp.dot(left, right, preferred_element_type=F32)]
  transfers between devices with their start and end apart: 7 -> 13, of which waited for: 4 -> 7; matrix products, arithmetic and copies ran while one was open for 2% -> 3% of each run, Pallas kernels for 0% -> 2%
where the time goes in v2:
time: 212 us; the launch traced here: 210 us
  waiting for transfers between devices  89.8 us (42%)
  starting transfers between devices  63.7 us (30%)
  Pallas kernels  21.3 us (10%)
  blocking collectives  16.7 us (8%)
  local copies, waits for them, and re-layouts  13.1 us (6%)
  other arithmetic  4.91 us (2%)
    all_to_all x4, waiting for transfers between devices, exchange(): return lax.all_to_all(blocks, axes, split_axis=0, concat_axis=0, tiled=True)  57.8 us
    all_to_all x4, starting transfers between devices, exchange(): return lax.all_to_all(blocks, axes, split_axis=0, concat_axis=0, tiled=True)  41.2 us
    ppermute x4, waiting for transfers between devices, along_x(): lax.ppermute(piece, 'x', [(i, (i - step) % size) for i in range(size)])  30.9 us
    all_to_all x1, blocking collectives, exchange(): return lax.all_to_all(blocks, axes, split_axis=0, concat_axis=0, tiled=True)  16.7 us
    ppermute x4, starting transfers between devices, along_x(): lax.ppermute(piece, 'x', [(i, (i - step) % size) for i in range(size)])  12.4 us
    ppermute x5, starting transfers between devices, swapped(): return lax.ppermute(piece, 'core', [(0, 1), (1, 0)])  10.1 us
    pallas_call x1, Pallas kernels, run_experts(): pl.pallas_call(expert_kernel, name='experts', out_shape=shape((rows, mode...  8.28 us
  transfers between devices with their start and end apart: 13, of which 7 were waited for; matrix products, arithmetic and copies ran while one was open for 3% of the time, Pallas kernels for 2%

profile of v2, /device:TPU:8, one launch (start us, length us, event | category | flops | bytes accessed | tf_op | source)
XLA Modules:
  0.0 210.5 jit_solution(5136877431144328148)
XLA Ops:
  0.0 1.6 fusion.6
  1.6 2.4 %summary.1 = (bf16[16,72,128]{2,1,0:T(8,128)(2,1)}, bf16[128,1024]{1,0:T(8,128)(2,1)}, f32[8,128]{1,0:T(8,128)}) custom-call(bf16[128,1024]{1,0:T(8,128)(2,1)} %bitcast.53, bf16[128,1024]{1,0:T(8,128)(2,1)} %bitcast.49, f32[8,128]{1,0:T(8,128)} %bitcast.55, f32[128,128]{1,0:T(8,128)} %get-tuple-element.26.cos_ref, f32[128,128]{1,0:T(8,128)} %get-tuple-element.25.sin_ref), custom_call_target="tpu_custom_call" | custom-call | flops 70000000 | bytes 1200000 | tf_op jit(solution)/shard_map/summary/pallas_call | solution.py:284
  4.1 16.7 %all_to_all.25.arrived_ref = bf16[16,72,128]{2,1,0:T(8,128)(2,1)} all-to-all(bf16[16,72,128]{2,1,0:T(8,128)(2,1)} %get-tuple-element.13), channel_id=1, replica_groups=mesh['z'=16,'ylo'=2,'x'=4,'core'=2,'yhi'=2] {'ylo','x','core'}, dimensions={0} | all-to-all | bytes 589824 | tf_op jit(solution)/shard_map/all_to_all | solution.py:18
  20.7 1.8 plane_sum.1
  22.5 11.2 %all-to-all-start.1 = ((bf16[16,72,128]{2,1,0:T(8,128)(2,1)}), bf16[16,72,128]{2,1,0:T(8,128)(2,1)S(1)}, u32[]{:S(2)}, u32[]{:S(2)}) async-start(bf16[16,72,128]{2,1,0:T(8,128)(2,1)} %plane_sum.1), calls=%async_computation.1 | async-start | bytes 589824 | tf_op jit(solution)/shard_map/all_to_all | solution.py:18
  35.4 18.2 %all-to-all-done.1.planes_ref = bf16[16,72,128]{2,1,0:T(8,128)(2,1)S(1)} async-done(((bf16[16,72,128]{2,1,0:T(8,128)(2,1)}), bf16[16,72,128]{2,1,0:T(8,128)(2,1)S(1)}, u32[]{:S(2)}, u32[]{:S(2)}) %all-to-all-start.1) | async-done | bytes 294944 | tf_op jit(solution)/shard_map/all_to_all | solution.py:18
  54.3 2.0 enter.1
  56.3 4.4 %all-to-all-start.2 = ((bf16[16,64,128]{2,1,0:T(8,128)(2,1)}), bf16[16,64,128]{2,1,0:T(8,128)(2,1)S(1)}, u32[]{:S(2)}, u32[]{:S(2)}) async-start(bf16[16,64,128]{2,1,0:T(8,128)(2,1)} %enter.1), calls=%async_computation.2 | async-start | bytes 524288 | tf_op jit(solution)/shard_map/all_to_all | solution.py:18
  61.9 3.5 %inside.1 = (bf16[128,1024]{1,0:T(8,128)(2,1)}, f32[128,1024]{1,0:T(8,128)}, f32[128,1024]{1,0:T(8,128)}) custom-call(bf16[128,1024]{1,0:T(8,128)(2,1)} %bitcast.52, bf16[128,1024]{1,0:T(8,128)(2,1)} %get-tuple-element.14.keys_ref, bf16[128,1024]{1,0:T(8,128)(2,1)} %bitcast.50, f32[8,128]{1,0:T(8,128)} %get-tuple-element.15.total_ref, ...), custom_call_target="tpu_custom_call" | custom-call | flops 70000000 | bytes 2200000 | tf_op jit(solution)/shard_map/inside/pallas_call | solution.py:293
  66.1 1.0 all-to-all-done.2
  67.8 3.3 %outgoing.1 = (f32[128,1024]{1,0:T(8,128)}, bf16[320,1024]{1,0:T(8,128)(2,1)}) custom-call(s32[8]{0:T(128)} %fusion.11.own_ref, bf16[1024,128]{1,0:T(8,128)(2,1)} %bitcast.51, bf16[128,1024]{1,0:T(8,128)(2,1)} %get-tuple-element.16.queries_ref, f32[128,1024]{1,0:T(8,128)} %get-tuple-element.17.inside_ref, f32[128,1024]{1,0:T(8,128)} %get-tuple-element.18.fade_ref, ...), custom_call_target="tpu_custom_call" | custom-call | flops 120000000 | bytes 3000000 | tf_op jit(solution)/shard_map/outgoing/pallas_call | solution.py:333
  71.2 2.2 %reshape.56 = bf16[64,40,128]{2,1,0:T(8,128)(2,1)} reshape(bf16[320,1024]{1,0:T(8,128)(2,1)} %get-tuple-element.20) | data formatting | bytes 1310720 | tf_op jit(solution)/shard_map/reshape | solution.py:354
  73.4 10.4 %all-to-all-start.3 = ((bf16[64,40,128]{2,1,0:T(8,128)(2,1)}), bf16[64,40,128]{2,1,0:T(8,128)(2,1)S(1)}, u32[]{:S(2)}, u32[]{:S(2)}) async-start(bf16[64,40,128]{2,1,0:T(8,128)(2,1)} %reshape.56), calls=%async_computation.3 | async-start | bytes 1310720 | tf_op jit(solution)/shard_map/all_to_all | solution.py:18
  85.3 2.7 %collective-permute-start.1 = (bf16[3,128,1408]{2,1,0:T(8,128)(2,1)}, bf16[3,128,1408]{2,1,0:T(8,128)(2,1)S(1)}, u32[]{:S(2)}, u32[]{:S(2)}) collective-permute-start(bf16[3,128,1408]{2,1,0:T(8,128)(2,1)} %constant_dynamic-update-slice_fusion.refs_1_), channel_id=1, source_target_pairs={{0,12},{4,0},{8,4},{12,8},{1,13},{5,1},{9,5},{13,9},{2,14},{6,2},{... | collective-permute-start | bytes 3244040 | tf_op jit(solution)/shard_map/ppermute | solution.py:229
  88.0 3.2 %collective-permute-start.4 = (bf16[3,128,1408]{2,1,0:T(8,128)(2,1)}, bf16[3,128,1408]{2,1,0:T(8,128)(2,1)S(1)}, u32[]{:S(2)}, u32[]{:S(2)}) collective-permute-start(bf16[3,128,1408]{2,1,0:T(8,128)(2,1)} %constant_dynamic-update-slice_fusion.refs_1_), channel_id=1, source_target_pairs={{0,4},{4,8},{8,12},{12,0},{1,5},{5,9},{9,13},{13,1},{2,6},{6,10},{... | collective-permute-start | bytes 3244040 | tf_op jit(solution)/shard_map/ppermute | solution.py:229
  91.2 1.9 collective-permute-start
  93.1 19.3 %collective-permute-done.1.refs_3_ = bf16[3,128,1408]{2,1,0:T(8,128)(2,1)S(1)} collective-permute-done((bf16[3,128,1408]{2,1,0:T(8,128)(2,1)}, bf16[3,128,1408]{2,1,0:T(8,128)(2,1)S(1)}, u32[]{:S(2)}, u32[]{:S(2)}) %collective-permute-start.1) | collective-permute-done | bytes 1081376 | tf_op jit(solution)/shard_map/ppermute | solution.py:229
  112.4 4.6 %collective-permute-start.3 = (bf16[3,64,1408]{2,1,0:T(8,128)(2,1)S(1)}, bf16[3,64,1408]{2,1,0:T(8,128)(2,1)S(1)}, u32[]{:S(2)}, u32[]{:S(2)}) collective-permute-start(bf16[3,64,1408]{2,1,0:T(8,128)(2,1)S(1)} %slice.34), channel_id=1, source_target_pairs={{0,12},{4,0},{8,4},{12,8},{1,13},{5,1},{9,5},{13,9},{2,14},{6,2},{... | collective-permute-start | bytes 1622024 | tf_op jit(solution)/shard_map/ppermute | solution.py:229
  117.1 1.9 collective-permute-start.2
  119.1 1.9 collective-permute-start.5
  121.0 2.4 %collective-permute-start.8 = (bf16[3,128,1408]{2,1,0:T(8,128)(2,1)S(1)}, bf16[3,128,1408]{2,1,0:T(8,128)(2,1)}, u32[]{:S(2)}, u32[]{:S(2)}) collective-permute-start(bf16[3,128,1408]{2,1,0:T(8,128)(2,1)S(1)} %collective-permute-done.4.refs_9_), channel_id=1, source_target_pairs={{0,2},{2,0},{1,3},{3,1},{4,6},{6,4},{5,7},{7,5},{8,10},{10,8},{9,1... | collective-permute-start | bytes 3244040 | tf_op jit(solution)/shard_map/ppermute | solution.py:233
  123.4 4.4 %collective-permute-done.3.refs_5_ = bf16[3,64,1408]{2,1,0:T(8,128)(2,1)S(1)} collective-permute-done((bf16[3,64,1408]{2,1,0:T(8,128)(2,1)S(1)}, bf16[3,64,1408]{2,1,0:T(8,128)(2,1)S(1)}, u32[]{:S(2)}, u32[]{:S(2)}) %collective-permute-start.3) | collective-permute-done | bytes 540704 | tf_op jit(solution)/shard_map/ppermute | solution.py:229
  127.8 1.9 collective-permute-start.6
  129.7 7.2 %collective-permute-done.5.refs_6_ = bf16[3,64,1408]{2,1,0:T(8,128)(2,1)} collective-permute-done((bf16[3,64,1408]{2,1,0:T(8,128)(2,1)S(1)}, bf16[3,64,1408]{2,1,0:T(8,128)(2,1)}, u32[]{:S(2)}, u32[]{:S(2)}) %collective-permute-start.5) | collective-permute-done | bytes 540704 | tf_op jit(solution)/shard_map/ppermute | solution.py:229
  137.0 1.9 collective-permute-start.7
  138.9 1.1 reshape.57.refs_0_
  140.0 1.1 collective-permute-done.7.refs_8_
  141.1 8.3 %experts.1 = bf16[320,1024]{1,0:T(8,128)(2,1)} custom-call(bf16[320,1024]{1,0:T(8,128)(2,1)} %reshape.57.refs_0_, bf16[3,128,1408]{2,1,0:T(8,128)(2,1)} %constant_dynamic-update-slice_fusion.refs_1_, bf16[3,128,1408]{2,1,0:T(8,128)(2,1)} %collective-permute-done.refs_2_, bf16[3,128,1408]{2,1,0:T(8,128)(2,1)} %copy-done.6, ...), custom_call_target="tpu_custom_call" | custom-call | flops 2768240640 | bytes 8650752 | tf_op jit(solution)/shard_map/experts/pallas_call | solution.py:212
  149.4 2.1 %reshape.58 = bf16[64,40,128]{2,1,0:T(8,128)(2,1)} reshape(bf16[320,1024]{1,0:T(8,128)(2,1)} %experts.1) | data formatting | bytes 1310720 | tf_op jit(solution)/shard_map/reshape | solution.py:360
  151.6 15.2 %all-to-all-start.4 = ((bf16[64,40,128]{2,1,0:T(8,128)(2,1)}), bf16[64,40,128]{2,1,0:T(8,128)(2,1)S(1)}, u32[]{:S(2)}, u32[]{:S(2)}) async-start(bf16[64,40,128]{2,1,0:T(8,128)(2,1)} %reshape.58), calls=%async_computation.4 | async-start | bytes 1310720 | tf_op jit(solution)/shard_map/all_to_all | solution.py:18
  167.2 38.6 %all-to-all-done.4 = bf16[64,40,128]{2,1,0:T(8,128)(2,1)S(1)} async-done(((bf16[64,40,128]{2,1,0:T(8,128)(2,1)}), bf16[64,40,128]{2,1,0:T(8,128)(2,1)S(1)}, u32[]{:S(2)}, u32[]{:S(2)}) %all-to-all-start.4) | async-done | bytes 655392 | tf_op jit(solution)/shard_map/all_to_all | solution.py:18
  207.2 1.4 rev.3
  (61 shorter events, 10.3 us)
Async XLA Ops:
  1.6 32.1 %copy-start.8 = (s32[1,128,2]{1,2,0:T(2,128)S(1)}, s32[1,128,2]{1,2,0:T(2,128)}, u32[]{:S(2)}) copy-start(s32[1,128,2]{1,2,0:T(2,128)} %param.21) | copy-start | bytes 3076
  22.5 31.1 %all-to-all-start.1 = ((bf16[16,72,128]{2,1,0:T(8,128)(2,1)}), bf16[16,72,128]{2,1,0:T(8,128)(2,1)S(1)}, u32[]{:S(2)}, u32[]{:S(2)}) async-start(bf16[16,72,128]{2,1,0:T(8,128)(2,1)} %plane_sum.1), calls=%async_computation.1 | async-start | bytes 589824 | tf_op jit(solution)/shard_map/all_to_all | solution.py:18
  53.6 0.7 copy-start
  54.3 11.0 %copy-start.3 = (bf16[1,128,1408]{2,1,0:T(8,128)(2,1)S(1)}, bf16[1,128,1408]{2,1,0:T(8,128)(2,1)}, u32[]{:S(2)}) copy-start(bf16[1,128,1408]{2,1,0:T(8,128)(2,1)} %param.23) | copy-start | bytes 1081348
  56.3 10.8 %all-to-all-start.2 = ((bf16[16,64,128]{2,1,0:T(8,128)(2,1)}), bf16[16,64,128]{2,1,0:T(8,128)(2,1)S(1)}, u32[]{:S(2)}, u32[]{:S(2)}) async-start(bf16[16,64,128]{2,1,0:T(8,128)(2,1)} %enter.1), calls=%async_computation.2 | async-start | bytes 524288 | tf_op jit(solution)/shard_map/all_to_all | solution.py:18
  67.1 0.7 copy-start.1
  71.2 12.6 %copy-start.4 = (bf16[1,128,1408]{2,1,0:T(8,128)(2,1)S(1)}, bf16[1,128,1408]{2,1,0:T(8,128)(2,1)}, u32[]{:S(2)}) copy-start(bf16[1,128,1408]{2,1,0:T(8,128)(2,1)} %param.24) | copy-start | bytes 1081348
  73.4 11.2 %copy-start.5 = (bf16[1,128,1408]{2,1,0:T(8,128)(2,1)S(1)}, bf16[1,128,1408]{2,1,0:T(8,128)(2,1)}, u32[]{:S(2)}) copy-start(bf16[1,128,1408]{2,1,0:T(8,128)(2,1)} %param.25) | copy-start | bytes 1081348
  73.4 65.5 %all-to-all-start.3 = ((bf16[64,40,128]{2,1,0:T(8,128)(2,1)}), bf16[64,40,128]{2,1,0:T(8,128)(2,1)S(1)}, u32[]{:S(2)}, u32[]{:S(2)}) async-start(bf16[64,40,128]{2,1,0:T(8,128)(2,1)} %reshape.56), calls=%async_computation.3 | async-start | bytes 1310720 | tf_op jit(solution)/shard_map/all_to_all | solution.py:18
  85.3 27.0 %collective-permute-start.1 = (bf16[3,128,1408]{2,1,0:T(8,128)(2,1)}, bf16[3,128,1408]{2,1,0:T(8,128)(2,1)S(1)}, u32[]{:S(2)}, u32[]{:S(2)}) collective-permute-start(bf16[3,128,1408]{2,1,0:T(8,128)(2,1)} %constant_dynamic-update-slice_fusion.refs_1_), channel_id=1, source_target_pairs={{0,12},{4,0},{8,4},{12,8},{1,13},{5,1},{9,5},{13,9},{2,14},{6,2},{... | collective-permute-start | bytes 3244040 | tf_op jit(solution)/shard_map/ppermute | solution.py:229
  88.0 31.0 %collective-permute-start.4 = (bf16[3,128,1408]{2,1,0:T(8,128)(2,1)}, bf16[3,128,1408]{2,1,0:T(8,128)(2,1)S(1)}, u32[]{:S(2)}, u32[]{:S(2)}) collective-permute-start(bf16[3,128,1408]{2,1,0:T(8,128)(2,1)} %constant_dynamic-update-slice_fusion.refs_1_), channel_id=1, source_target_pairs={{0,4},{4,8},{8,12},{12,0},{1,5},{5,9},{9,13},{13,1},{2,6},{6,10},{... | collective-permute-start | bytes 3244040 | tf_op jit(solution)/shard_map/ppermute | solution.py:229
  91.2 48.8 %collective-permute-start = (bf16[3,128,1408]{2,1,0:T(8,128)(2,1)}, bf16[3,128,1408]{2,1,0:T(8,128)(2,1)}, u32[]{:S(2)}, u32[]{:S(2)}) collective-permute-start(bf16[3,128,1408]{2,1,0:T(8,128)(2,1)} %constant_dynamic-update-slice_fusion.refs_1_), channel_id=1, source_target_pairs={{0,2},{2,0},{1,3},{3,1},{4,6},{6,4},{5,7},{7,5},{8,10},{10,8},{9,1... | collective-permute-start | bytes 3244040 | tf_op jit(solution)/shard_map/ppermute | solution.py:233
  112.4 27.6 %copy-start.6 = (bf16[3,128,1408]{2,1,0:T(8,128)(2,1)}, bf16[3,128,1408]{2,1,0:T(8,128)(2,1)S(1)}, u32[]{:S(2)}) copy-start(bf16[3,128,1408]{2,1,0:T(8,128)(2,1)S(1)} %collective-permute-done.1.refs_3_) | copy-start | bytes 3244036
  112.4 15.4 %collective-permute-start.3 = (bf16[3,64,1408]{2,1,0:T(8,128)(2,1)S(1)}, bf16[3,64,1408]{2,1,0:T(8,128)(2,1)S(1)}, u32[]{:S(2)}, u32[]{:S(2)}) collective-permute-start(bf16[3,64,1408]{2,1,0:T(8,128)(2,1)S(1)} %slice.34), channel_id=1, source_target_pairs={{0,12},{4,0},{8,4},{12,8},{1,13},{5,1},{9,5},{13,9},{2,14},{6,2},{... | collective-permute-start | bytes 1622024 | tf_op jit(solution)/shard_map/ppermute | solution.py:229
  117.1 22.9 %collective-permute-start.2 = (bf16[3,128,1408]{2,1,0:T(8,128)(2,1)S(1)}, bf16[3,128,1408]{2,1,0:T(8,128)(2,1)}, u32[]{:S(2)}, u32[]{:S(2)}) collective-permute-start(bf16[3,128,1408]{2,1,0:T(8,128)(2,1)S(1)} %collective-permute-done.1.refs_3_), channel_id=1, source_target_pairs={{0,2},{2,0},{1,3},{3,1},{4,6},{6,4},{5,7},{7,5},{8,10},{10,8},{9,1... | collective-permute-start | bytes 3244040 | tf_op jit(solution)/shard_map/ppermute | solution.py:233
  119.0 21.0 %copy-start.7 = (bf16[3,128,1408]{2,1,0:T(8,128)(2,1)}, bf16[3,128,1408]{2,1,0:T(8,128)(2,1)S(1)}, u32[]{:S(2)}) copy-start(bf16[3,128,1408]{2,1,0:T(8,128)(2,1)S(1)} %collective-permute-done.4.refs_9_) | copy-start | bytes 3244036
  119.1 17.9 %collective-permute-start.5 = (bf16[3,64,1408]{2,1,0:T(8,128)(2,1)S(1)}, bf16[3,64,1408]{2,1,0:T(8,128)(2,1)}, u32[]{:S(2)}, u32[]{:S(2)}) collective-permute-start(bf16[3,64,1408]{2,1,0:T(8,128)(2,1)S(1)} %slice.35), channel_id=1, source_target_pairs={{0,4},{4,8},{8,12},{12,0},{1,5},{5,9},{9,13},{13,1},{2,6},{6,10},{... | collective-permute-start | bytes 1622024 | tf_op jit(solution)/shard_map/ppermute | solution.py:229
  121.0 20.1 %collective-permute-start.8 = (bf16[3,128,1408]{2,1,0:T(8,128)(2,1)S(1)}, bf16[3,128,1408]{2,1,0:T(8,128)(2,1)}, u32[]{:S(2)}, u32[]{:S(2)}) collective-permute-start(bf16[3,128,1408]{2,1,0:T(8,128)(2,1)S(1)} %collective-permute-done.4.refs_9_), channel_id=1, source_target_pairs={{0,2},{2,0},{1,3},{3,1},{4,6},{6,4},{5,7},{7,5},{8,10},{10,8},{9,1... | collective-permute-start | bytes 3244040 | tf_op jit(solution)/shard_map/ppermute | solution.py:233
  127.8 13.3 %copy-start.10 = (bf16[3,64,1408]{2,1,0:T(8,128)(2,1)}, bf16[3,64,1408]{2,1,0:T(8,128)(2,1)S(1)}, u32[]{:S(2)}) copy-start(bf16[3,64,1408]{2,1,0:T(8,128)(2,1)S(1)} %collective-permute-done.3.refs_5_) | copy-start | bytes 1622020
  127.8 12.2 %collective-permute-start.6 = (bf16[3,64,1408]{2,1,0:T(8,128)(2,1)S(1)}, bf16[3,64,1408]{2,1,0:T(8,128)(2,1)}, u32[]{:S(2)}, u32[]{:S(2)}) collective-permute-start(bf16[3,64,1408]{2,1,0:T(8,128)(2,1)S(1)} %collective-permute-done.3.refs_5_), channel_id=1, source_target_pairs={{0,2},{2,0},{1,3},{3,1},{4,6},{6,4},{5,7},{7,5},{8,10},{10,8},{9,1... | collective-permute-start | bytes 1622024 | tf_op jit(solution)/shard_map/ppermute | solution.py:233
  137.0 4.2 %collective-permute-start.7 = (bf16[3,64,1408]{2,1,0:T(8,128)(2,1)}, bf16[3,64,1408]{2,1,0:T(8,128)(2,1)}, u32[]{:S(2)}, u32[]{:S(2)}) collective-permute-start(bf16[3,64,1408]{2,1,0:T(8,128)(2,1)} %collective-permute-done.5.refs_6_), channel_id=1, source_target_pairs={{0,2},{2,0},{1,3},{3,1},{4,6},{6,4},{5,7},{7,5},{8,10},{10,8},{9,1... | collective-permute-start | bytes 1622024 | tf_op jit(solution)/shard_map/ppermute | solution.py:233
  151.6 15.6 %copy-start.9 = (f32[1,128,2]{1,2,0:T(2,128)S(1)}, f32[1,128,2]{1,2,0:T(2,128)}, u32[]{:S(2)}) copy-start(f32[1,128,2]{1,2,0:T(2,128)} %param.22) | copy-start | bytes 3076
  151.6 54.2 %all-to-all-start.4 = ((bf16[64,40,128]{2,1,0:T(8,128)(2,1)}), bf16[64,40,128]{2,1,0:T(8,128)(2,1)S(1)}, u32[]{:S(2)}, u32[]{:S(2)}) async-start(bf16[64,40,128]{2,1,0:T(8,128)(2,1)} %reshape.58), calls=%async_computation.4 | async-start | bytes 1310720 | tf_op jit(solution)/shard_map/all_to_all | solution.py:18
  208.7 1.0 copy-start.2

commit v3 on v2

--- a/solution.py
+++ b/solution.py
@@ -11,6 +11,7 @@
 PLANE = ("ylo", "x", "core")
 OWNERS = ("z", "ylo", "yhi")
 LOG_ROWS = 8
+LANES = 128
 F32, BF16 = jnp.float32, jnp.bfloat16
 
 
@@ -139,6 +140,7 @@
     residual_ref,
     outgoing_ref,
     normed_ref,
+    packed_ref,
 ):
     chunks, count, head_dim = normed_ref.shape
     square = jnp.zeros((count, 1), F32)
@@ -157,14 +159,32 @@
         lanes = slice(chunk * head_dim, (chunk + 1) * head_dim)
         normed = residual_ref[:, lanes] * scale * norm_gain_ref[:, lanes]
         normed_ref[own_ref[chunk]] = normed.astype(BF16)
+    slots = placing_ref.shape[0]
     for chunk in range(chunks):
-        lanes = slice(chunk * head_dim, (chunk + 1) * head_dim)
-        outgoing_ref[:, lanes] = dot32(placing_ref[...], normed_ref[chunk]).astype(BF16)
+        packed_ref[pl.ds(chunk, slots, stride=chunks), :] = dot32(
+            placing_ref[...], normed_ref[chunk]
+        )
+    outgoing_ref[...] = packed_ref[...].astype(BF16)
+
+
+def combine_kernel(
+    own_ref, returned_ref, first_ref, second_ref, weights_ref, residual_ref, out_ref, mixed_ref
+):
+    chunks, _, lanes_count = mixed_ref.shape
+    for chunk in range(chunks):
+        lanes = slice(chunk * lanes_count, (chunk + 1) * lanes_count)
+        rows = returned_ref[:, lanes]
+        mixed_ref[chunk] = weights_ref[:, :1] * dot32(first_ref[...], rows) + weights_ref[
+            :, 1:
+        ] * dot32(second_ref[...], rows)
+    for chunk in range(chunks):
+        lanes = slice(chunk * lanes_count, (chunk + 1) * lanes_count)
+        out_ref[:, lanes] = (residual_ref[:, lanes] + mixed_ref[own_ref[chunk]]).astype(BF16)
 
 
 def expert_kernel(*refs):
-    arrived_ref, pieces, out_ref = refs[0], refs[1:-4], refs[-4]
-    weights_ref, hidden_ref, sems = refs[-3], refs[-2], refs[-1]
+    arrived_ref, pieces, out_ref = refs[0], refs[1:-5], refs[-5]
+    weights_ref, hidden_ref, packed_ref, sems = refs[-4:]
     width = weights_ref.shape[2]
     copies = []
     for index in range(3):
@@ -190,19 +210,28 @@
         hidden_ref[:, columns] = (gate / (1.0 + jnp.exp(-gate)) * up).astype(BF16)
     for copy in copies[2 * count :]:
         copy.wait()
-    tile = 256
-    for start in range(0, out_ref.shape[1], tile):
-        rows = slice(start, start + tile)
-        out_ref[:, rows] = lax.dot_general(
+    rows, lanes = arrived_ref.shape[0], packed_ref.shape[1]
+    chunks = packed_ref.shape[0] // rows
+    for chunk in range(0, chunks, 2):
+        pair = lax.dot_general(
             hidden_ref[...],
-            weights_ref[2, rows, :],
+            weights_ref[2, chunk * lanes : (chunk + 2) * lanes, :],
             (((1,), (1,)), ((), ())),
             preferred_element_type=F32,
-        ).astype(BF16)
+        )
+        for side in range(2):
+            packed_ref[pl.ds(chunk + side, rows, stride=chunks), :] = pair[
+                :, side * lanes : (side + 1) * lanes
+            ]
+    out_ref[...] = packed_ref[...].astype(BF16)
 
 
 def shape(dims, kind):
     return jax.ShapeDtypeStruct(dims, kind)
+
+
+def vmem(mebibytes):
+    return pltpu.CompilerParams(vmem_limit_bytes=mebibytes << 20)
 
 
 def run_experts(arrived, pieces):
@@ -212,15 +241,17 @@
     return pl.pallas_call(
         expert_kernel,
         name="experts",
-        out_shape=shape((rows, model_width), BF16),
+        out_shape=shape((rows * model_width // LANES, LANES), BF16),
         in_specs=[pl.BlockSpec(memory_space=pltpu.VMEM)] + [anywhere] * len(pieces),
         out_specs=pl.BlockSpec(memory_space=pltpu.VMEM),
         scratch_shapes=[
             pltpu.VMEM((3, model_width, width), BF16),
             pltpu.VMEM((rows, width), BF16),
+            pltpu.VMEM((rows * model_width // LANES, LANES), F32),
             pltpu.SemaphoreType.DMA((3, len(pieces))),
         ],
         cost_estimate=cost(6 * rows * model_width * width, 6 * model_width * width),
+        compiler_params=vmem(20),
     )(arrived, *pieces)
 
 
@@ -238,16 +269,6 @@
     chunk = jnp.arange(chips * cores, dtype=jnp.int32)
     chip = (chunk // cores + chips - lax.axis_index("x")) % chips
     return chip * cores + (chunk + lax.axis_index("core")) % cores
-
-
-def model_order(rows):
-    chips, cores = lax.axis_size("x"), lax.axis_size("core")
-    count, width = rows.shape
-    view = rows.reshape(count, chips, cores, width // (chips * cores))
-    view = jnp.where(lax.axis_index("core") == 1, view[:, :, ::-1], view)
-    start = (chips - lax.axis_index("x")) % chips
-    twice = jnp.concatenate([view, view], axis=1)
-    return lax.dynamic_slice_in_dim(twice, start, chips, axis=1).reshape(count, width)
 
 
 def body(
@@ -286,6 +307,7 @@
         name="summary",
         out_shape=(shape(message, BF16), shape(wide, BF16), shape((head_count, tok_rows), F32)),
         cost_estimate=cost(70000000, 1200000),
+        compiler_params=vmem(6),
     )(keys[0], values[0], log_decay[0].T, cosine, sine)
     summaries = exchange(out_message, PLANE)
     stacked = jnp.stack([w_gate[0], w_up[0], w_down[0]])
@@ -295,12 +317,14 @@
         name="inside",
         out_shape=(shape(wide, BF16), shape(wide, F32), shape(wide, F32)),
         cost_estimate=cost(70000000, 2200000),
+        compiler_params=vmem(8),
     )(queries[0], turned_keys, values[0], total, cosine, sine)
     sums = pl.pallas_call(
         plane_sum_kernel,
         name="plane_sum",
         out_shape=shape((depth,) + message[1:], BF16),
         cost_estimate=cost(500000, 600000),
+        compiler_params=vmem(4),
     )(summaries)
     sums = exchange(sums, "z")
     own_other = swapped(stacked)
@@ -311,6 +335,7 @@
         in_specs=[pl.BlockSpec(memory_space=pltpu.SMEM)]
         + [pl.BlockSpec(memory_space=pltpu.VMEM)] * 2,
         cost_estimate=cost(900000, 900000),
+        compiler_params=vmem(4),
     )(lax.axis_index("z")[None], summaries, sums)
     state_in = exchange(entering, PLANE).reshape(model_width, head_dim)
     after_other, before_other = swapped(after), swapped(before)
@@ -330,16 +355,22 @@
     slot_lanes = jnp.arange(slot_count, dtype=jnp.int32)
     placing = jnp.any(destination[None, :, :] == slot_lanes[:, None, None], axis=2).astype(BF16)
 
+    flat = (slot_count * model_width // LANES, LANES)
+    places = own_places()
     residual, outgoing = pl.pallas_call(
         outgoing_kernel,
         name="outgoing",
-        out_shape=(shape(wide, F32), shape((slot_count, model_width), BF16)),
+        out_shape=(shape(wide, F32), shape(flat, BF16)),
         in_specs=[pl.BlockSpec(memory_space=pltpu.SMEM)]
         + [pl.BlockSpec(memory_space=pltpu.VMEM)] * 8,
-        scratch_shapes=[pltpu.VMEM((head_count, tok_rows, head_dim), BF16)],
+        scratch_shapes=[
+            pltpu.VMEM((head_count, tok_rows, head_dim), BF16),
+            pltpu.VMEM(flat, F32),
+        ],
         cost_estimate=cost(120000000, 3000000),
+        compiler_params=vmem(10),
     )(
-        own_places(),
+        places,
         state_in,
         turned_queries,
         inside,
@@ -349,8 +380,7 @@
         norm_gain[None],
         placing,
     )
-    lanes = 128
-    packed = (expert_count, capacity * model_width // lanes, lanes)
+    packed = (expert_count, capacity * model_width // LANES, LANES)
     arrived = exchange(outgoing.reshape(packed), OWNERS).reshape(slot_count, model_width)
     cut = stacked.shape[1] // 2
     far = [along_x(after[:, :cut], 1), along_x(before[:, cut:], -1)]
@@ -358,12 +388,21 @@
     pieces = [stacked, own_other, after, after_other, *far, *far_other, before, before_other]
     expert_out = run_experts(arrived, pieces)
     returned = exchange(expert_out.reshape(packed), OWNERS).reshape(slot_count, model_width)
-    mixed = jnp.zeros(wide, F32)
-    for route_index in range(top_count):
-        picking = (destination[:, route_index][:, None] == slot_lanes[None, :]).astype(BF16)
-        routed = dot32(picking, returned)
-        mixed = mixed + route_weights[0][:, route_index][:, None] * routed
-    return (residual + model_order(mixed)).astype(BF16)[None]
+    picks = [
+        (destination[:, index][:, None] == slot_lanes[None, :]).astype(BF16)
+        for index in range(top_count)
+    ]
+    output = pl.pallas_call(
+        combine_kernel,
+        name="combine",
+        out_shape=shape(wide, BF16),
+        in_specs=[pl.BlockSpec(memory_space=pltpu.SMEM)]
+        + [pl.BlockSpec(memory_space=pltpu.VMEM)] * 5,
+        scratch_shapes=[pltpu.VMEM((head_count, tok_rows, head_dim), F32)],
+        cost_estimate=cost(180000000, 2000000),
+        compiler_params=vmem(8),
+    )(places, returned, *picks, route_weights[0], residual)
+    return output[None]
 
 
 def solution(mesh):

time: 212 us -> 195 us (0.920)
  Pallas kernels: 21.3 us -> 15.2 us
  local copies, waits for them, and re-layouts: 13.1 us -> 7.89 us
  other arithmetic: 4.91 us -> 1.97 us
    reshape x4 -> x0, local copies, waits for them, and re-layouts: 5.17 us -> none  [the longest x1 2.18 us: body(): outgoing.reshape(packed)]
    ppermute x4, waiting for transfers between devices: 30.9 us -> 27.4 us  [along_x(): lax.ppermute(piece, 'x', [(i, (i - step) % size) for i in range(size)])]
    all_to_all x4, waiting for transfers between devices: 57.8 us -> 60.8 us  [exchange(): return lax.all_to_all(blocks, axes, split_axis=0, concat_axis=0, tiled=True)]
    unnamed x25 -> x30, local copies, waits for them, and re-layouts: 3.29 us -> 4.41 us
    pallas_call x1 -> x2, Pallas kernels: 8.28 us -> 8.94 us  [the longest x1 7.02 us: run_experts(): pl.pallas_call(expert_kernel, name='experts', out_shape=shape((rows * mod...]
  transfers between devices with their start and end apart: 13 -> 13, of which waited for: 7 -> 7; matrix products, arithmetic and copies ran while one was open for 3% -> 3% of each run, Pallas kernels for 2% -> 1%
where the time goes in v3:
time: 195 us
  waiting for transfers between devices  89 us (46%)
  starting transfers between devices  65.1 us (33%)
  Pallas kernels  15.2 us (8%)
  blocking collectives  15.1 us (8%)
  local copies, waits for them, and re-layouts  7.89 us (4%)
  other arithmetic  1.97 us (1%)
    all_to_all x4, waiting for transfers between devices, exchange(): return lax.all_to_all(blocks, axes, split_axis=0, concat_axis=0, tiled=True)  60.8 us
    all_to_all x4, starting transfers between devices, exchange(): return lax.all_to_all(blocks, axes, split_axis=0, concat_axis=0, tiled=True)  42.7 us
    ppermute x4, waiting for transfers between devices, along_x(): lax.ppermute(piece, 'x', [(i, (i - step) % size) for i in range(size)])  27.4 us
    all_to_all x1, blocking collectives, exchange(): return lax.all_to_all(blocks, axes, split_axis=0, concat_axis=0, tiled=True)  15.1 us
    ppermute x4, starting transfers between devices, along_x(): lax.ppermute(piece, 'x', [(i, (i - step) % size) for i in range(size)])  12.4 us
    ppermute x5, starting transfers between devices, swapped(): return lax.ppermute(piece, 'core', [(0, 1), (1, 0)])  10.1 us
    pallas_call x1, Pallas kernels, run_experts(): pl.pallas_call(expert_kernel, name='experts', out_shape=shape((rows * mod...  7.02 us
    unnamed x30, local copies, waits for them, and re-layouts  4.41 us
  transfers between devices with their start and end apart: 13, of which 7 were waited for; matrix products, arithmetic and copies ran while one was open for 3% of the time, Pallas kernels for 1%

profile of v3, /device:TPU:8, one launch (start us, length us, event | category | flops | bytes accessed | tf_op | source)
XLA Modules:
  0.0 194.6 jit_solution(15225942892525199265)
XLA Ops:
  0.0 1.0 fusion.3
  1.0 0.9 copy-done
  1.9 0.9 copy-done.3
  4.2 15.1 %all_to_all.25.arrived_ref = bf16[16,72,128]{2,1,0:T(8,128)(2,1)S(1)} all-to-all(bf16[16,72,128]{2,1,0:T(8,128)(2,1)S(1)} %get-tuple-element.13), channel_id=1, replica_groups=mesh['z'=16,'ylo'=2,'x'=4,'core'=2,'yhi'=2] {'ylo','x','core'}, dimensions={0} | all-to-all | bytes 589824 | tf_op jit(solution)/shard_map/all_to_all | solution.py:19
  19.3 0.8 plane_sum.1
  20.1 12.5 %all-to-all-start.1 = ((bf16[16,72,128]{2,1,0:T(8,128)(2,1)}), bf16[16,72,128]{2,1,0:T(8,128)(2,1)S(1)}, u32[]{:S(2)}, u32[]{:S(2)}) async-start(bf16[16,72,128]{2,1,0:T(8,128)(2,1)} %plane_sum.1), calls=%async_computation.1 | async-start | bytes 589824 | tf_op jit(solution)/shard_map/all_to_all | solution.py:19
  34.3 18.2 %all-to-all-done.1.planes_ref = bf16[16,72,128]{2,1,0:T(8,128)(2,1)S(1)} async-done(((bf16[16,72,128]{2,1,0:T(8,128)(2,1)}), bf16[16,72,128]{2,1,0:T(8,128)(2,1)S(1)}, u32[]{:S(2)}, u32[]{:S(2)}) %all-to-all-start.1) | async-done | bytes 294944 | tf_op jit(solution)/shard_map/all_to_all | solution.py:19
  52.5 0.9 enter.1
  53.4 4.5 %all-to-all-start.2 = ((bf16[16,64,128]{2,1,0:T(8,128)(2,1)}), bf16[16,64,128]{2,1,0:T(8,128)(2,1)S(1)}, u32[]{:S(2)}, u32[]{:S(2)}) async-start(bf16[16,64,128]{2,1,0:T(8,128)(2,1)} %enter.1), calls=%async_computation.2 | async-start | bytes 524288 | tf_op jit(solution)/shard_map/all_to_all | solution.py:19
  57.9 1.4 inside.1
  59.3 0.8 constant_dynamic-update-slice_fusion.2
  60.1 4.2 %all-to-all-done.2 = bf16[16,64,128]{2,1,0:T(8,128)(2,1)S(1)} async-done(((bf16[16,64,128]{2,1,0:T(8,128)(2,1)}), bf16[16,64,128]{2,1,0:T(8,128)(2,1)S(1)}, u32[]{:S(2)}, u32[]{:S(2)}) %all-to-all-start.2) | async-done | bytes 262176 | tf_op jit(solution)/shard_map/all_to_all | solution.py:19
  64.4 2.6 %outgoing.1 = (f32[128,1024]{1,0:T(8,128)S(1)}, bf16[2560,128]{1,0:T(8,128)(2,1)}) custom-call(s32[8]{0:T(128)S(1)} %fusion.8.own_ref, bf16[1024,128]{1,0:T(8,128)(2,1)S(1)} %bitcast.40, bf16[128,1024]{1,0:T(8,128)(2,1)S(1)} %get-tuple-element.16.queries_ref, f32[128,1024]{1,0:T(8,128)S(1)} %get-tuple-element.17.inside_ref, ...), custom_call_target="tpu_custom_call" | custom-call | flops 120000000 | bytes 3000000 | tf_op jit(solution)/shard_map/outgoing/pallas_call | solution.py:360
  66.9 10.6 %all-to-all-start.3 = ((bf16[64,40,128]{2,1,0:T(8,128)(2,1)}), bf16[64,40,128]{2,1,0:T(8,128)(2,1)}, u32[]{:S(2)}, u32[]{:S(2)}) async-start(bf16[64,40,128]{2,1,0:T(8,128)(2,1)} %bitcast.12), calls=%async_computation.3 | async-start | bytes 1310720 | tf_op jit(solution)/shard_map/all_to_all | solution.py:19
  79.1 2.7 %collective-permute-start.1 = (bf16[3,128,1408]{2,1,0:T(8,128)(2,1)}, bf16[3,128,1408]{2,1,0:T(8,128)(2,1)S(1)}, u32[]{:S(2)}, u32[]{:S(2)}) collective-permute-start(bf16[3,128,1408]{2,1,0:T(8,128)(2,1)} %constant_dynamic-update-slice_fusion.refs_1_), channel_id=1, source_target_pairs={{0,12},{4,0},{8,4},{12,8},{1,13},{5,1},{9,5},{13,9},{2,14},{6,2},{... | collective-permute-start | bytes 3244040 | tf_op jit(solution)/shard_map/ppermute | solution.py:260
  81.8 3.2 %collective-permute-start.4 = (bf16[3,128,1408]{2,1,0:T(8,128)(2,1)}, bf16[3,128,1408]{2,1,0:T(8,128)(2,1)S(1)}, u32[]{:S(2)}, u32[]{:S(2)}) collective-permute-start(bf16[3,128,1408]{2,1,0:T(8,128)(2,1)} %constant_dynamic-update-slice_fusion.refs_1_), channel_id=1, source_target_pairs={{0,4},{4,8},{8,12},{12,0},{1,5},{5,9},{9,13},{13,1},{2,6},{6,10},{... | collective-permute-start | bytes 3244040 | tf_op jit(solution)/shard_map/ppermute | solution.py:260
  84.9 1.9 collective-permute-start
  86.9 19.3 %collective-permute-done.1.refs_3_ = bf16[3,128,1408]{2,1,0:T(8,128)(2,1)S(1)} collective-permute-done((bf16[3,128,1408]{2,1,0:T(8,128)(2,1)}, bf16[3,128,1408]{2,1,0:T(8,128)(2,1)S(1)}, u32[]{:S(2)}, u32[]{:S(2)}) %collective-permute-start.1) | collective-permute-done | bytes 1081376 | tf_op jit(solution)/shard_map/ppermute | solution.py:260
  106.2 4.6 %collective-permute-start.3 = (bf16[3,64,1408]{2,1,0:T(8,128)(2,1)S(1)}, bf16[3,64,1408]{2,1,0:T(8,128)(2,1)}, u32[]{:S(2)}, u32[]{:S(2)}) collective-permute-start(bf16[3,64,1408]{2,1,0:T(8,128)(2,1)S(1)} %slice.25), channel_id=1, source_target_pairs={{0,12},{4,0},{8,4},{12,8},{1,13},{5,1},{9,5},{13,9},{2,14},{6,2},{... | collective-permute-start | bytes 1622024 | tf_op jit(solution)/shard_map/ppermute | solution.py:260
  110.9 1.9 collective-permute-start.5
  112.8 1.9 collective-permute-start.2
  114.7 2.4 %collective-permute-start.8 = (bf16[3,128,1408]{2,1,0:T(8,128)(2,1)S(1)}, bf16[3,128,1408]{2,1,0:T(8,128)(2,1)}, u32[]{:S(2)}, u32[]{:S(2)}) collective-permute-start(bf16[3,128,1408]{2,1,0:T(8,128)(2,1)S(1)} %collective-permute-done.4.refs_9_), channel_id=1, source_target_pairs={{0,2},{2,0},{1,3},{3,1},{4,6},{6,4},{5,7},{7,5},{8,10},{10,8},{9,1... | collective-permute-start | bytes 3244040 | tf_op jit(solution)/shard_map/ppermute | solution.py:264
  117.1 4.5 %collective-permute-done.3.refs_5_ = bf16[3,64,1408]{2,1,0:T(8,128)(2,1)} collective-permute-done((bf16[3,64,1408]{2,1,0:T(8,128)(2,1)S(1)}, bf16[3,64,1408]{2,1,0:T(8,128)(2,1)}, u32[]{:S(2)}, u32[]{:S(2)}) %collective-permute-start.3) | collective-permute-done | bytes 540704 | tf_op jit(solution)/shard_map/ppermute | solution.py:260
  121.7 1.9 collective-permute-start.6
  123.6 3.6 %collective-permute-done.5.refs_6_ = bf16[3,64,1408]{2,1,0:T(8,128)(2,1)} collective-permute-done((bf16[3,64,1408]{2,1,0:T(8,128)(2,1)S(1)}, bf16[3,64,1408]{2,1,0:T(8,128)(2,1)}, u32[]{:S(2)}, u32[]{:S(2)}) %collective-permute-start.5) | collective-permute-done | bytes 540704 | tf_op jit(solution)/shard_map/ppermute | solution.py:260
  127.1 1.9 collective-permute-start.7
  129.1 1.4 reshape.50.refs_0_
  130.5 0.8 collective-permute-done.7.refs_8_
  131.3 7.0 %experts.1 = bf16[2560,128]{1,0:T(8,128)(2,1)} custom-call(bf16[320,1024]{1,0:T(8,128)(2,1)S(1)} %reshape.50.refs_0_, bf16[3,128,1408]{2,1,0:T(8,128)(2,1)} %constant_dynamic-update-slice_fusion.refs_1_, bf16[3,128,1408]{2,1,0:T(8,128)(2,1)} %collective-permute-done.refs_2_, bf16[3,128,1408]{2,1,0:T(8,128)(2,1)S(1)} %collective-permute-done.1.refs_3_, ...), custom_call_target="tpu_custom_call" | custom-call | flops 2768240640 | bytes 8650752 | tf_op jit(solution)/shard_map/experts/pallas_call | solution.py:241
  138.4 15.0 %all-to-all-start.4 = ((bf16[64,40,128]{2,1,0:T(8,128)(2,1)}), bf16[64,40,128]{2,1,0:T(8,128)(2,1)S(1)}, u32[]{:S(2)}, u32[]{:S(2)}) async-start(bf16[64,40,128]{2,1,0:T(8,128)(2,1)} %bitcast.13), calls=%async_computation.4 | async-start | bytes 1310720 | tf_op jit(solution)/shard_map/all_to_all | solution.py:19
  154.0 38.4 %all-to-all-done.4 = bf16[64,40,128]{2,1,0:T(8,128)(2,1)S(1)} async-done(((bf16[64,40,128]{2,1,0:T(8,128)(2,1)}), bf16[64,40,128]{2,1,0:T(8,128)(2,1)S(1)}, u32[]{:S(2)}, u32[]{:S(2)}) %all-to-all-start.4) | async-done | bytes 655392 | tf_op jit(solution)/shard_map/all_to_all | solution.py:19
  192.7 1.9 combine.1
  (57 shorter events, 5.5 us)
Async XLA Ops:
  1.0 1.0 copy-start
  1.9 0.9 copy-start.3
  2.9 0.7 copy-start.5
  3.6 29.0 %copy-start.11 = (s32[1,128,2]{1,2,0:T(2,128)S(1)}, s32[1,128,2]{1,2,0:T(2,128)}, u32[]{:S(2)}) copy-start(s32[1,128,2]{1,2,0:T(2,128)} %param.21) | copy-start | bytes 3076
  20.1 32.4 %all-to-all-start.1 = ((bf16[16,72,128]{2,1,0:T(8,128)(2,1)}), bf16[16,72,128]{2,1,0:T(8,128)(2,1)S(1)}, u32[]{:S(2)}, u32[]{:S(2)}) async-start(bf16[16,72,128]{2,1,0:T(8,128)(2,1)} %plane_sum.1), calls=%async_computation.1 | async-start | bytes 589824 | tf_op jit(solution)/shard_map/all_to_all | solution.py:19
  33.0 24.9 %copy-start.1 = (bf16[1,128,1024]{2,1,0:T(8,128)(2,1)S(1)}, bf16[1,128,1024]{2,1,0:T(8,128)(2,1)}, u32[]{:S(2)}) copy-start(bf16[1,128,1024]{2,1,0:T(8,128)(2,1)} %param.17) | copy-start | bytes 786436
  33.0 24.9 %copy-start.2 = (bf16[1,128,1024]{2,1,0:T(8,128)(2,1)S(1)}, bf16[1,128,1024]{2,1,0:T(8,128)(2,1)}, u32[]{:S(2)}) copy-start(bf16[1,128,1024]{2,1,0:T(8,128)(2,1)} %param.15) | copy-start | bytes 786436
  52.5 6.9 %copy-start.8 = (bf16[1,128,1408]{2,1,0:T(8,128)(2,1)S(1)}, bf16[1,128,1408]{2,1,0:T(8,128)(2,1)}, u32[]{:S(2)}) copy-start(bf16[1,128,1408]{2,1,0:T(8,128)(2,1)} %param.23) | copy-start | bytes 1081348
  53.4 11.0 %copy-start.4 = (bf16[1,128,1024]{2,1,0:T(8,128)(2,1)S(1)}, bf16[1,128,1024]{2,1,0:T(8,128)(2,1)}, u32[]{:S(2)}) copy-start(bf16[1,128,1024]{2,1,0:T(8,128)(2,1)} %param.14) | copy-start | bytes 786436
  53.4 11.0 %copy-start.6 = (f32[1024]{0:T(1024)S(1)}, f32[1024]{0:T(1024)}, u32[]{:S(2)}) copy-start(f32[1024]{0:T(1024)} %param.19) | copy-start | bytes 12292
  53.4 11.0 %copy-start.7 = (f32[1024]{0:T(1024)S(1)}, f32[1024]{0:T(1024)}, u32[]{:S(2)}) copy-start(f32[1024]{0:T(1024)} %param.20) | copy-start | bytes 12292
  53.4 11.0 %all-to-all-start.2 = ((bf16[16,64,128]{2,1,0:T(8,128)(2,1)}), bf16[16,64,128]{2,1,0:T(8,128)(2,1)S(1)}, u32[]{:S(2)}, u32[]{:S(2)}) async-start(bf16[16,64,128]{2,1,0:T(8,128)(2,1)} %enter.1), calls=%async_computation.2 | async-start | bytes 524288 | tf_op jit(solution)/shard_map/all_to_all | solution.py:19
  66.9 10.6 %copy-start.9 = (bf16[1,128,1408]{2,1,0:T(8,128)(2,1)S(1)}, bf16[1,128,1408]{2,1,0:T(8,128)(2,1)}, u32[]{:S(2)}) copy-start(bf16[1,128,1408]{2,1,0:T(8,128)(2,1)} %param.24) | copy-start | bytes 1081348
  66.9 11.4 %copy-start.10 = (bf16[1,128,1408]{2,1,0:T(8,128)(2,1)S(1)}, bf16[1,128,1408]{2,1,0:T(8,128)(2,1)}, u32[]{:S(2)}) copy-start(bf16[1,128,1408]{2,1,0:T(8,128)(2,1)} %param.25) | copy-start | bytes 1081348
  66.9 62.2 %all-to-all-start.3 = ((bf16[64,40,128]{2,1,0:T(8,128)(2,1)}), bf16[64,40,128]{2,1,0:T(8,128)(2,1)}, u32[]{:S(2)}, u32[]{:S(2)}) async-start(bf16[64,40,128]{2,1,0:T(8,128)(2,1)} %bitcast.12), calls=%async_computation.3 | async-start | bytes 1310720 | tf_op jit(solution)/shard_map/all_to_all | solution.py:19
  79.1 27.0 %collective-permute-start.1 = (bf16[3,128,1408]{2,1,0:T(8,128)(2,1)}, bf16[3,128,1408]{2,1,0:T(8,128)(2,1)S(1)}, u32[]{:S(2)}, u32[]{:S(2)}) collective-permute-start(bf16[3,128,1408]{2,1,0:T(8,128)(2,1)} %constant_dynamic-update-slice_fusion.refs_1_), channel_id=1, source_target_pairs={{0,12},{4,0},{8,4},{12,8},{1,13},{5,1},{9,5},{13,9},{2,14},{6,2},{... | collective-permute-start | bytes 3244040 | tf_op jit(solution)/shard_map/ppermute | solution.py:260
  81.8 29.1 %collective-permute-start.4 = (bf16[3,128,1408]{2,1,0:T(8,128)(2,1)}, bf16[3,128,1408]{2,1,0:T(8,128)(2,1)S(1)}, u32[]{:S(2)}, u32[]{:S(2)}) collective-permute-start(bf16[3,128,1408]{2,1,0:T(8,128)(2,1)} %constant_dynamic-update-slice_fusion.refs_1_), channel_id=1, source_target_pairs={{0,4},{4,8},{8,12},{12,0},{1,5},{5,9},{9,13},{13,1},{2,6},{6,10},{... | collective-permute-start | bytes 3244040 | tf_op jit(solution)/shard_map/ppermute | solution.py:260
  84.9 45.5 %collective-permute-start = (bf16[3,128,1408]{2,1,0:T(8,128)(2,1)}, bf16[3,128,1408]{2,1,0:T(8,128)(2,1)}, u32[]{:S(2)}, u32[]{:S(2)}) collective-permute-start(bf16[3,128,1408]{2,1,0:T(8,128)(2,1)} %constant_dynamic-update-slice_fusion.refs_1_), channel_id=1, source_target_pairs={{0,2},{2,0},{1,3},{3,1},{4,6},{6,4},{5,7},{7,5},{8,10},{10,8},{9,1... | collective-permute-start | bytes 3244040 | tf_op jit(solution)/shard_map/ppermute | solution.py:264
  106.2 15.5 %collective-permute-start.3 = (bf16[3,64,1408]{2,1,0:T(8,128)(2,1)S(1)}, bf16[3,64,1408]{2,1,0:T(8,128)(2,1)}, u32[]{:S(2)}, u32[]{:S(2)}) collective-permute-start(bf16[3,64,1408]{2,1,0:T(8,128)(2,1)S(1)} %slice.25), channel_id=1, source_target_pairs={{0,12},{4,0},{8,4},{12,8},{1,13},{5,1},{9,5},{13,9},{2,14},{6,2},{... | collective-permute-start | bytes 1622024 | tf_op jit(solution)/shard_map/ppermute | solution.py:260
  110.9 16.3 %collective-permute-start.5 = (bf16[3,64,1408]{2,1,0:T(8,128)(2,1)S(1)}, bf16[3,64,1408]{2,1,0:T(8,128)(2,1)}, u32[]{:S(2)}, u32[]{:S(2)}) collective-permute-start(bf16[3,64,1408]{2,1,0:T(8,128)(2,1)S(1)} %slice.26), channel_id=1, source_target_pairs={{0,4},{4,8},{8,12},{12,0},{1,5},{5,9},{9,13},{13,1},{2,6},{6,10},{... | collective-permute-start | bytes 1622024 | tf_op jit(solution)/shard_map/ppermute | solution.py:260
  112.8 18.5 %collective-permute-start.2 = (bf16[3,128,1408]{2,1,0:T(8,128)(2,1)S(1)}, bf16[3,128,1408]{2,1,0:T(8,128)(2,1)}, u32[]{:S(2)}, u32[]{:S(2)}) collective-permute-start(bf16[3,128,1408]{2,1,0:T(8,128)(2,1)S(1)} %collective-permute-done.1.refs_3_), channel_id=1, source_target_pairs={{0,2},{2,0},{1,3},{3,1},{4,6},{6,4},{5,7},{7,5},{8,10},{10,8},{9,1... | collective-permute-start | bytes 3244040 | tf_op jit(solution)/shard_map/ppermute | solution.py:264
  114.7 16.6 %collective-permute-start.8 = (bf16[3,128,1408]{2,1,0:T(8,128)(2,1)S(1)}, bf16[3,128,1408]{2,1,0:T(8,128)(2,1)}, u32[]{:S(2)}, u32[]{:S(2)}) collective-permute-start(bf16[3,128,1408]{2,1,0:T(8,128)(2,1)S(1)} %collective-permute-done.4.refs_9_), channel_id=1, source_target_pairs={{0,2},{2,0},{1,3},{3,1},{4,6},{6,4},{5,7},{7,5},{8,10},{10,8},{9,1... | collective-permute-start | bytes 3244040 | tf_op jit(solution)/shard_map/ppermute | solution.py:264
  121.7 8.8 %collective-permute-start.6 = (bf16[3,64,1408]{2,1,0:T(8,128)(2,1)}, bf16[3,64,1408]{2,1,0:T(8,128)(2,1)}, u32[]{:S(2)}, u32[]{:S(2)}) collective-permute-start(bf16[3,64,1408]{2,1,0:T(8,128)(2,1)} %collective-permute-done.3.refs_5_), channel_id=1, source_target_pairs={{0,2},{2,0},{1,3},{3,1},{4,6},{6,4},{5,7},{7,5},{8,10},{10,8},{9,1... | collective-permute-start | bytes 1622024 | tf_op jit(solution)/shard_map/ppermute | solution.py:264
  127.1 4.2 %collective-permute-start.7 = (bf16[3,64,1408]{2,1,0:T(8,128)(2,1)}, bf16[3,64,1408]{2,1,0:T(8,128)(2,1)}, u32[]{:S(2)}, u32[]{:S(2)}) collective-permute-start(bf16[3,64,1408]{2,1,0:T(8,128)(2,1)} %collective-permute-done.5.refs_6_), channel_id=1, source_target_pairs={{0,2},{2,0},{1,3},{3,1},{4,6},{6,4},{5,7},{7,5},{8,10},{10,8},{9,1... | collective-permute-start | bytes 1622024 | tf_op jit(solution)/shard_map/ppermute | solution.py:264
  138.3 15.2 %copy-start.12 = (f32[1,128,2]{1,2,0:T(2,128)S(1)}, f32[1,128,2]{1,2,0:T(2,128)}, u32[]{:S(2)}) copy-start(f32[1,128,2]{1,2,0:T(2,128)} %param.22) | copy-start | bytes 3076
  138.4 54.0 %all-to-all-start.4 = ((bf16[64,40,128]{2,1,0:T(8,128)(2,1)}), bf16[64,40,128]{2,1,0:T(8,128)(2,1)S(1)}, u32[]{:S(2)}, u32[]{:S(2)}) async-start(bf16[64,40,128]{2,1,0:T(8,128)(2,1)} %bitcast.13), calls=%async_computation.4 | async-start | bytes 1310720 | tf_op jit(solution)/shard_map/all_to_all | solution.py:19

commit v4 on v3

--- a/solution.py
+++ b/solution.py
@@ -12,6 +12,7 @@
 OWNERS = ("z", "ylo", "yhi")
 LOG_ROWS = 8
 LANES = 128
+TILE = 512
 F32, BF16 = jnp.float32, jnp.bfloat16
 
 
@@ -44,7 +45,7 @@
     return block * cosine + pltpu.roll(block, block.shape[1] // 2, 1) * sine
 
 
-def summary_kernel(keys_ref, values_ref, log_ref, cos_ref, sin_ref, message_ref, turned_ref, total_ref):
+def summary_kernel(keys_ref, values_ref, log_ref, cos_ref, sin_ref, message_ref, total_ref):
     heads, count = log_ref.shape
     head_dim = cos_ref.shape[1]
     parts = message_ref.shape[0] // heads
@@ -62,7 +63,6 @@
     for head in range(heads):
         lanes = slice(head * head_dim, (head + 1) * head_dim)
         keys = turned(keys_ref[:, lanes].astype(F32), cos_ref[...], sin_ref[...]).astype(BF16)
-        turned_ref[:, lanes] = keys
         faded = keys.astype(F32).T * trailing[head : head + 1]
         coarse = faded.astype(BF16)
         fine = (faded - coarse.astype(F32)).astype(BF16)
@@ -87,8 +87,9 @@
         queries = turned(queries_ref[:, lanes].astype(F32), cos_ref[...], sin_ref[...])
         queries = (queries * head_dim ** (-0.5)).astype(BF16)
         turned_ref[:, lanes] = queries
+        keys = turned(keys_ref[:, lanes].astype(F32), cos_ref[...], sin_ref[...]).astype(BF16)
         scores = lax.dot_general(
-            queries, keys_ref[:, lanes], (((1,), (1,)), ((), ())), preferred_element_type=F32
+            queries, keys, (((1,), (1,)), ((), ())), preferred_element_type=F32
         )
         here = total_ref[head : head + 1, :]
         down = jnp.broadcast_to(here, (head_dim, count)).T
@@ -186,29 +187,29 @@
     arrived_ref, pieces, out_ref = refs[0], refs[1:-5], refs[-5]
     weights_ref, hidden_ref, packed_ref, sems = refs[-4:]
     width = weights_ref.shape[2]
-    copies = []
-    for index in range(3):
-        start = 0
-        for number, piece in enumerate(pieces):
-            size = piece.shape[1]
-            copy = pltpu.make_async_copy(
-                piece.at[index],
-                weights_ref.at[index, pl.ds(start, size), :],
-                sems.at[index, number],
-            )
-            copy.start()
-            copies.append(copy)
-            start += size
-    count = len(pieces)
-    for copy in copies[: 2 * count]:
-        copy.wait()
-    tile = 512
-    for start in range(0, width, tile):
-        columns = slice(start, min(width, start + tile))
+    tiles = [slice(start, min(width, start + TILE)) for start in range(0, width, TILE)]
+    groups = [[(index, tile) for index in range(2)] for tile in tiles] + [[(2, slice(0, width))]]
+    copies = [[] for _ in groups]
+    for group, (members, started) in enumerate(zip(groups, copies)):
+        for index, columns in members:
+            start = 0
+            for number, piece in enumerate(pieces):
+                size = piece.shape[1]
+                copy = pltpu.make_async_copy(
+                    piece.at[index, :, columns],
+                    weights_ref.at[index, start : start + size, columns],
+                    sems.at[group, index, number],
+                )
+                copy.start()
+                started.append(copy)
+                start += size
+    for columns, started in zip(tiles, copies):
+        for copy in started:
+            copy.wait()
         gate = dot32(arrived_ref[...], weights_ref[0, :, columns])
         up = dot32(arrived_ref[...], weights_ref[1, :, columns])
         hidden_ref[:, columns] = (gate / (1.0 + jnp.exp(-gate)) * up).astype(BF16)
-    for copy in copies[2 * count :]:
+    for copy in copies[-1]:
         copy.wait()
     rows, lanes = arrived_ref.shape[0], packed_ref.shape[1]
     chunks = packed_ref.shape[0] // rows
@@ -248,7 +249,7 @@
             pltpu.VMEM((3, model_width, width), BF16),
             pltpu.VMEM((rows, width), BF16),
             pltpu.VMEM((rows * model_width // LANES, LANES), F32),
-            pltpu.SemaphoreType.DMA((3, len(pieces))),
+            pltpu.SemaphoreType.DMA((-(-width // TILE) + 1, 3, len(pieces))),
         ],
         cost_estimate=cost(6 * rows * model_width * width, 6 * model_width * width),
         compiler_params=vmem(20),
@@ -302,23 +303,23 @@
     angles = position.astype(F32)[:, None] * np.tile(inverse, 2)[None, :]
     cosine, sine = jnp.cos(angles), jnp.sin(angles) * sign
 
-    out_message, turned_keys, total = pl.pallas_call(
+    out_message, total = pl.pallas_call(
         summary_kernel,
         name="summary",
-        out_shape=(shape(message, BF16), shape(wide, BF16), shape((head_count, tok_rows), F32)),
+        out_shape=(shape(message, BF16), shape((head_count, tok_rows), F32)),
         cost_estimate=cost(70000000, 1200000),
-        compiler_params=vmem(6),
     )(keys[0], values[0], log_decay[0].T, cosine, sine)
     summaries = exchange(out_message, PLANE)
     stacked = jnp.stack([w_gate[0], w_up[0], w_down[0]])
-    after, before = along_x(stacked, 1), along_x(stacked, -1)
+    after = along_x(stacked, 1)
+    before = along_x(stacked, -1)
     turned_queries, inside, fade = pl.pallas_call(
         inside_kernel,
         name="inside",
         out_shape=(shape(wide, BF16), shape(wide, F32), shape(wide, F32)),
         cost_estimate=cost(70000000, 2200000),
         compiler_params=vmem(8),
-    )(queries[0], turned_keys, values[0], total, cosine, sine)
+    )(queries[0], keys[0], values[0], total, cosine, sine)
     sums = pl.pallas_call(
         plane_sum_kernel,
         name="plane_sum",

time: 195 us -> 196 us (level)
  Pallas kernels: 15.2 us -> 17.3 us
  transfers between devices with their start and end apart: 13 -> 13, of which waited for: 7 -> 7; matrix products, arithmetic and copies ran while one was open for 3% -> 4% of each run, Pallas kernels for 1% -> 1%
where the time goes in v4:
time: 196 us; the launch traced here: 195 us
  waiting for transfers between devices  87.9 us (45%)
  starting transfers between devices  64.4 us (33%)
  Pallas kernels  17.3 us (9%)
  blocking collectives  15.9 us (8%)
  local copies, waits for them, and re-layouts  6.31 us (3%)
  other arithmetic  2.64 us (1%)
    all_to_all x4, waiting for transfers between devices, exchange(): return lax.all_to_all(blocks, axes, split_axis=0, concat_axis=0, tiled=True)  59.7 us
    all_to_all x4, starting transfers between devices, exchange(): return lax.all_to_all(blocks, axes, split_axis=0, concat_axis=0, tiled=True)  42 us
    ppermute x4, waiting for transfers between devices, along_x(): lax.ppermute(piece, 'x', [(i, (i - step) % size) for i in range(size)])  27.4 us
    all_to_all x1, blocking collectives, exchange(): return lax.all_to_all(blocks, axes, split_axis=0, concat_axis=0, tiled=True)  15.9 us
    ppermute x4, starting transfers between devices, along_x(): lax.ppermute(piece, 'x', [(i, (i - step) % size) for i in range(size)])  12.4 us
    ppermute x5, starting transfers between devices, swapped(): return lax.ppermute(piece, 'core', [(0, 1), (1, 0)])  10.1 us
    pallas_call x1, Pallas kernels, run_experts(): pl.pallas_call(expert_kernel, name='experts', out_shape=shape((rows * mod...  7.34 us
  transfers between devices with their start and end apart: 13, of which 7 were waited for; matrix products, arithmetic and copies ran while one was open for 4% of the time, Pallas kernels for 1%

profile of v4, /device:TPU:8, one launch (start us, length us, event | category | flops | bytes accessed | tf_op | source)
XLA Modules:
  0.0 194.9 jit_solution(4268076125296359374)
XLA Ops:
  0.0 1.6 fusion.3
  1.6 2.4 %summary.1 = (bf16[16,72,128]{2,1,0:T(8,128)(2,1)}, f32[8,128]{1,0:T(8,128)}) custom-call(bf16[128,1024]{1,0:T(8,128)(2,1)} %bitcast.38, bf16[128,1024]{1,0:T(8,128)(2,1)} %bitcast.40, f32[8,128]{1,0:T(8,128)} %bitcast.48, f32[128,128]{1,0:T(8,128)} %get-tuple-element.22.cos_ref, f32[128,128]{1,0:T(8,128)} %get-tuple-element.21.sin_ref), custom_call_target="tpu_custom_call" | custom-call | flops 70000000 | bytes 1200000 | tf_op jit(solution)/shard_map/summary/pallas_call | solution.py:306
  4.1 15.9 %all_to_all.25.arrived_ref = bf16[16,72,128]{2,1,0:T(8,128)(2,1)S(1)} all-to-all(bf16[16,72,128]{2,1,0:T(8,128)(2,1)} %get-tuple-element.12), channel_id=1, replica_groups=mesh['z'=16,'ylo'=2,'x'=4,'core'=2,'yhi'=2] {'ylo','x','core'}, dimensions={0} | all-to-all | bytes 589824 | tf_op jit(solution)/shard_map/all_to_all | solution.py:20
  20.0 0.8 plane_sum.1
  20.8 11.8 %all-to-all-start.1 = ((bf16[16,72,128]{2,1,0:T(8,128)(2,1)}), bf16[16,72,128]{2,1,0:T(8,128)(2,1)S(1)}, u32[]{:S(2)}, u32[]{:S(2)}) async-start(bf16[16,72,128]{2,1,0:T(8,128)(2,1)} %plane_sum.1), calls=%async_computation.1 | async-start | bytes 589824 | tf_op jit(solution)/shard_map/all_to_all | solution.py:20
  34.4 18.1 %all-to-all-done.1.planes_ref = bf16[16,72,128]{2,1,0:T(8,128)(2,1)S(1)} async-done(((bf16[16,72,128]{2,1,0:T(8,128)(2,1)}), bf16[16,72,128]{2,1,0:T(8,128)(2,1)S(1)}, u32[]{:S(2)}, u32[]{:S(2)}) %all-to-all-start.1) | async-done | bytes 294944 | tf_op jit(solution)/shard_map/all_to_all | solution.py:20
  52.5 0.9 enter.1
  53.4 4.5 %all-to-all-start.2 = ((bf16[16,64,128]{2,1,0:T(8,128)(2,1)}), bf16[16,64,128]{2,1,0:T(8,128)(2,1)S(1)}, u32[]{:S(2)}, u32[]{:S(2)}) async-start(bf16[16,64,128]{2,1,0:T(8,128)(2,1)} %enter.1), calls=%async_computation.2 | async-start | bytes 524288 | tf_op jit(solution)/shard_map/all_to_all | solution.py:20
  58.0 1.4 inside.1
  59.4 1.8 constant_dynamic-update-slice_fusion.2
  61.2 3.2 %all-to-all-done.2 = bf16[16,64,128]{2,1,0:T(8,128)(2,1)S(1)} async-done(((bf16[16,64,128]{2,1,0:T(8,128)(2,1)}), bf16[16,64,128]{2,1,0:T(8,128)(2,1)S(1)}, u32[]{:S(2)}, u32[]{:S(2)}) %all-to-all-start.2) | async-done | bytes 262176 | tf_op jit(solution)/shard_map/all_to_all | solution.py:20
  64.4 2.5 %outgoing.1 = (f32[128,1024]{1,0:T(8,128)S(1)}, bf16[2560,128]{1,0:T(8,128)(2,1)}) custom-call(s32[8]{0:T(128)S(1)} %fusion.8.own_ref, bf16[1024,128]{1,0:T(8,128)(2,1)S(1)} %bitcast.42, bf16[128,1024]{1,0:T(8,128)(2,1)S(1)} %get-tuple-element.14.queries_ref, f32[128,1024]{1,0:T(8,128)S(1)} %get-tuple-element.15.inside_ref, ...), custom_call_target="tpu_custom_call" | custom-call | flops 120000000 | bytes 3000000 | tf_op jit(solution)/shard_map/outgoing/pallas_call | solution.py:361
  66.9 10.6 %all-to-all-start.3 = ((bf16[64,40,128]{2,1,0:T(8,128)(2,1)}), bf16[64,40,128]{2,1,0:T(8,128)(2,1)}, u32[]{:S(2)}, u32[]{:S(2)}) async-start(bf16[64,40,128]{2,1,0:T(8,128)(2,1)} %bitcast.12), calls=%async_computation.3 | async-start | bytes 1310720 | tf_op jit(solution)/shard_map/all_to_all | solution.py:20
  77.6 0.8 constant_dynamic-update-slice_fusion.1
  79.1 2.7 %collective-permute-start.1 = (bf16[3,128,1408]{2,1,0:T(8,128)(2,1)}, bf16[3,128,1408]{2,1,0:T(8,128)(2,1)S(1)}, u32[]{:S(2)}, u32[]{:S(2)}) collective-permute-start(bf16[3,128,1408]{2,1,0:T(8,128)(2,1)} %constant_dynamic-update-slice_fusion.refs_1_), channel_id=1, source_target_pairs={{0,12},{4,0},{8,4},{12,8},{1,13},{5,1},{9,5},{13,9},{2,14},{6,2},{... | collective-permute-start | bytes 3244040 | tf_op jit(solution)/shard_map/ppermute | solution.py:261
  81.8 3.2 %collective-permute-start.4 = (bf16[3,128,1408]{2,1,0:T(8,128)(2,1)}, bf16[3,128,1408]{2,1,0:T(8,128)(2,1)S(1)}, u32[]{:S(2)}, u32[]{:S(2)}) collective-permute-start(bf16[3,128,1408]{2,1,0:T(8,128)(2,1)} %constant_dynamic-update-slice_fusion.refs_1_), channel_id=1, source_target_pairs={{0,4},{4,8},{8,12},{12,0},{1,5},{5,9},{9,13},{13,1},{2,6},{6,10},{... | collective-permute-start | bytes 3244040 | tf_op jit(solution)/shard_map/ppermute | solution.py:261
  85.0 1.9 collective-permute-start
  86.9 19.3 %collective-permute-done.1.refs_3_ = bf16[3,128,1408]{2,1,0:T(8,128)(2,1)S(1)} collective-permute-done((bf16[3,128,1408]{2,1,0:T(8,128)(2,1)}, bf16[3,128,1408]{2,1,0:T(8,128)(2,1)S(1)}, u32[]{:S(2)}, u32[]{:S(2)}) %collective-permute-start.1) | collective-permute-done | bytes 1081376 | tf_op jit(solution)/shard_map/ppermute | solution.py:261
  106.2 4.6 %collective-permute-start.3 = (bf16[3,64,1408]{2,1,0:T(8,128)(2,1)S(1)}, bf16[3,64,1408]{2,1,0:T(8,128)(2,1)}, u32[]{:S(2)}, u32[]{:S(2)}) collective-permute-start(bf16[3,64,1408]{2,1,0:T(8,128)(2,1)S(1)} %slice.25), channel_id=1, source_target_pairs={{0,12},{4,0},{8,4},{12,8},{1,13},{5,1},{9,5},{13,9},{2,14},{6,2},{... | collective-permute-start | bytes 1622024 | tf_op jit(solution)/shard_map/ppermute | solution.py:261
  110.9 1.9 collective-permute-start.5
  112.8 1.9 collective-permute-start.2
  114.8 2.4 %collective-permute-start.8 = (bf16[3,128,1408]{2,1,0:T(8,128)(2,1)S(1)}, bf16[3,128,1408]{2,1,0:T(8,128)(2,1)}, u32[]{:S(2)}, u32[]{:S(2)}) collective-permute-start(bf16[3,128,1408]{2,1,0:T(8,128)(2,1)S(1)} %collective-permute-done.4.refs_9_), channel_id=1, source_target_pairs={{0,2},{2,0},{1,3},{3,1},{4,6},{6,4},{5,7},{7,5},{8,10},{10,8},{9,1... | collective-permute-start | bytes 3244040 | tf_op jit(solution)/shard_map/ppermute | solution.py:265
  117.2 4.5 %collective-permute-done.3.refs_5_ = bf16[3,64,1408]{2,1,0:T(8,128)(2,1)} collective-permute-done((bf16[3,64,1408]{2,1,0:T(8,128)(2,1)S(1)}, bf16[3,64,1408]{2,1,0:T(8,128)(2,1)}, u32[]{:S(2)}, u32[]{:S(2)}) %collective-permute-start.3) | collective-permute-done | bytes 540704 | tf_op jit(solution)/shard_map/ppermute | solution.py:261
  121.7 1.9 collective-permute-start.6
  123.6 3.6 %collective-permute-done.5.refs_6_ = bf16[3,64,1408]{2,1,0:T(8,128)(2,1)} collective-permute-done((bf16[3,64,1408]{2,1,0:T(8,128)(2,1)S(1)}, bf16[3,64,1408]{2,1,0:T(8,128)(2,1)}, u32[]{:S(2)}, u32[]{:S(2)}) %collective-permute-start.5) | collective-permute-done | bytes 540704 | tf_op jit(solution)/shard_map/ppermute | solution.py:261
  127.2 1.9 collective-permute-start.7
  129.1 1.4 reshape.50.refs_0_
  130.5 0.8 collective-permute-done.7.refs_8_
  131.4 7.3 %experts.1 = bf16[2560,128]{1,0:T(8,128)(2,1)} custom-call(bf16[320,1024]{1,0:T(8,128)(2,1)S(1)} %reshape.50.refs_0_, bf16[3,128,1408]{2,1,0:T(8,128)(2,1)} %constant_dynamic-update-slice_fusion.refs_1_, bf16[3,128,1408]{2,1,0:T(8,128)(2,1)} %collective-permute-done.refs_2_, bf16[3,128,1408]{2,1,0:T(8,128)(2,1)S(1)} %collective-permute-done.1.refs_3_, ...), custom_call_target="tpu_custom_call" | custom-call | flops 2768240640 | bytes 8650752 | tf_op jit(solution)/shard_map/experts/pallas_call | solution.py:242
  138.7 15.0 %all-to-all-start.4 = ((bf16[64,40,128]{2,1,0:T(8,128)(2,1)}), bf16[64,40,128]{2,1,0:T(8,128)(2,1)S(1)}, u32[]{:S(2)}, u32[]{:S(2)}) async-start(bf16[64,40,128]{2,1,0:T(8,128)(2,1)} %bitcast.13), calls=%async_computation.4 | async-start | bytes 1310720 | tf_op jit(solution)/shard_map/all_to_all | solution.py:20
  154.3 38.4 %all-to-all-done.4 = bf16[64,40,128]{2,1,0:T(8,128)(2,1)S(1)} async-done(((bf16[64,40,128]{2,1,0:T(8,128)(2,1)}), bf16[64,40,128]{2,1,0:T(8,128)(2,1)S(1)}, u32[]{:S(2)}, u32[]{:S(2)}) %all-to-all-start.4) | async-done | bytes 655392 | tf_op jit(solution)/shard_map/all_to_all | solution.py:20
  193.0 1.9 combine.1
  (57 shorter events, 3.4 us)
Async XLA Ops:
  1.6 31.0 %copy-start.11 = (s32[1,128,2]{1,2,0:T(2,128)S(1)}, s32[1,128,2]{1,2,0:T(2,128)}, u32[]{:S(2)}) copy-start(s32[1,128,2]{1,2,0:T(2,128)} %param.21) | copy-start | bytes 3076
  20.8 31.7 %all-to-all-start.1 = ((bf16[16,72,128]{2,1,0:T(8,128)(2,1)}), bf16[16,72,128]{2,1,0:T(8,128)(2,1)S(1)}, u32[]{:S(2)}, u32[]{:S(2)}) async-start(bf16[16,72,128]{2,1,0:T(8,128)(2,1)} %plane_sum.1), calls=%async_computation.1 | async-start | bytes 589824 | tf_op jit(solution)/shard_map/all_to_all | solution.py:20
  33.1 24.9 %copy-start = (bf16[1,128,1024]{2,1,0:T(8,128)(2,1)S(1)}, bf16[1,128,1024]{2,1,0:T(8,128)(2,1)}, u32[]{:S(2)}) copy-start(bf16[1,128,1024]{2,1,0:T(8,128)(2,1)} %param.16) | copy-start | bytes 786436
  33.1 24.9 %copy-start.1 = (bf16[1,128,1024]{2,1,0:T(8,128)(2,1)S(1)}, bf16[1,128,1024]{2,1,0:T(8,128)(2,1)}, u32[]{:S(2)}) copy-start(bf16[1,128,1024]{2,1,0:T(8,128)(2,1)} %param.17) | copy-start | bytes 786436
  33.1 24.9 %copy-start.2 = (f32[128,128]{1,0:T(8,128)S(1)}, f32[128,128]{1,0:T(8,128)}, u32[]{:S(2)}) copy-start(f32[128,128]{1,0:T(8,128)} %get-tuple-element.21.sin_ref) | copy-start | bytes 196612
  33.1 24.9 %copy-start.3 = (f32[128,128]{1,0:T(8,128)S(1)}, f32[128,128]{1,0:T(8,128)}, u32[]{:S(2)}) copy-start(f32[128,128]{1,0:T(8,128)} %get-tuple-element.22.cos_ref) | copy-start | bytes 196612
  33.1 24.9 %copy-start.4 = (bf16[1,128,1024]{2,1,0:T(8,128)(2,1)S(1)}, bf16[1,128,1024]{2,1,0:T(8,128)(2,1)}, u32[]{:S(2)}) copy-start(bf16[1,128,1024]{2,1,0:T(8,128)(2,1)} %param.15) | copy-start | bytes 786436
  33.1 24.9 %copy-start.8 = (f32[8,128]{1,0:T(8,128)S(1)}, f32[8,128]{1,0:T(8,128)}, u32[]{:S(2)}) copy-start(f32[8,128]{1,0:T(8,128)} %get-tuple-element.13.total_ref) | copy-start | bytes 12292
  53.4 11.0 %copy-start.5 = (bf16[1,128,1024]{2,1,0:T(8,128)(2,1)S(1)}, bf16[1,128,1024]{2,1,0:T(8,128)(2,1)}, u32[]{:S(2)}) copy-start(bf16[1,128,1024]{2,1,0:T(8,128)(2,1)} %param.14) | copy-start | bytes 786436
  53.4 11.0 %copy-start.6 = (f32[1024]{0:T(1024)S(1)}, f32[1024]{0:T(1024)}, u32[]{:S(2)}) copy-start(f32[1024]{0:T(1024)} %param.19) | copy-start | bytes 12292
  53.4 11.0 %copy-start.7 = (f32[1024]{0:T(1024)S(1)}, f32[1024]{0:T(1024)}, u32[]{:S(2)}) copy-start(f32[1024]{0:T(1024)} %param.20) | copy-start | bytes 12292
  53.4 11.0 %all-to-all-start.2 = ((bf16[16,64,128]{2,1,0:T(8,128)(2,1)}), bf16[16,64,128]{2,1,0:T(8,128)(2,1)S(1)}, u32[]{:S(2)}, u32[]{:S(2)}) async-start(bf16[16,64,128]{2,1,0:T(8,128)(2,1)} %enter.1), calls=%async_computation.2 | async-start | bytes 524288 | tf_op jit(solution)/shard_map/all_to_all | solution.py:20
  66.9 10.6 %copy-start.9 = (bf16[1,128,1408]{2,1,0:T(8,128)(2,1)S(1)}, bf16[1,128,1408]{2,1,0:T(8,128)(2,1)}, u32[]{:S(2)}) copy-start(bf16[1,128,1408]{2,1,0:T(8,128)(2,1)} %param.24) | copy-start | bytes 1081348
  66.9 11.4 %copy-start.10 = (bf16[1,128,1408]{2,1,0:T(8,128)(2,1)S(1)}, bf16[1,128,1408]{2,1,0:T(8,128)(2,1)}, u32[]{:S(2)}) copy-start(bf16[1,128,1408]{2,1,0:T(8,128)(2,1)} %param.25) | copy-start | bytes 1081348
  66.9 62.2 %all-to-all-start.3 = ((bf16[64,40,128]{2,1,0:T(8,128)(2,1)}), bf16[64,40,128]{2,1,0:T(8,128)(2,1)}, u32[]{:S(2)}, u32[]{:S(2)}) async-start(bf16[64,40,128]{2,1,0:T(8,128)(2,1)} %bitcast.12), calls=%async_computation.3 | async-start | bytes 1310720 | tf_op jit(solution)/shard_map/all_to_all | solution.py:20
  79.1 27.0 %collective-permute-start.1 = (bf16[3,128,1408]{2,1,0:T(8,128)(2,1)}, bf16[3,128,1408]{2,1,0:T(8,128)(2,1)S(1)}, u32[]{:S(2)}, u32[]{:S(2)}) collective-permute-start(bf16[3,128,1408]{2,1,0:T(8,128)(2,1)} %constant_dynamic-update-slice_fusion.refs_1_), channel_id=1, source_target_pairs={{0,12},{4,0},{8,4},{12,8},{1,13},{5,1},{9,5},{13,9},{2,14},{6,2},{... | collective-permute-start | bytes 3244040 | tf_op jit(solution)/shard_map/ppermute | solution.py:261
  81.8 29.1 %collective-permute-start.4 = (bf16[3,128,1408]{2,1,0:T(8,128)(2,1)}, bf16[3,128,1408]{2,1,0:T(8,128)(2,1)S(1)}, u32[]{:S(2)}, u32[]{:S(2)}) collective-permute-start(bf16[3,128,1408]{2,1,0:T(8,128)(2,1)} %constant_dynamic-update-slice_fusion.refs_1_), channel_id=1, source_target_pairs={{0,4},{4,8},{8,12},{12,0},{1,5},{5,9},{9,13},{13,1},{2,6},{6,10},{... | collective-permute-start | bytes 3244040 | tf_op jit(solution)/shard_map/ppermute | solution.py:261
  85.0 45.5 %collective-permute-start = (bf16[3,128,1408]{2,1,0:T(8,128)(2,1)}, bf16[3,128,1408]{2,1,0:T(8,128)(2,1)}, u32[]{:S(2)}, u32[]{:S(2)}) collective-permute-start(bf16[3,128,1408]{2,1,0:T(8,128)(2,1)} %constant_dynamic-update-slice_fusion.refs_1_), channel_id=1, source_target_pairs={{0,2},{2,0},{1,3},{3,1},{4,6},{6,4},{5,7},{7,5},{8,10},{10,8},{9,1... | collective-permute-start | bytes 3244040 | tf_op jit(solution)/shard_map/ppermute | solution.py:265
  106.2 15.5 %collective-permute-start.3 = (bf16[3,64,1408]{2,1,0:T(8,128)(2,1)S(1)}, bf16[3,64,1408]{2,1,0:T(8,128)(2,1)}, u32[]{:S(2)}, u32[]{:S(2)}) collective-permute-start(bf16[3,64,1408]{2,1,0:T(8,128)(2,1)S(1)} %slice.25), channel_id=1, source_target_pairs={{0,12},{4,0},{8,4},{12,8},{1,13},{5,1},{9,5},{13,9},{2,14},{6,2},{... | collective-permute-start | bytes 1622024 | tf_op jit(solution)/shard_map/ppermute | solution.py:261
  110.9 16.3 %collective-permute-start.5 = (bf16[3,64,1408]{2,1,0:T(8,128)(2,1)S(1)}, bf16[3,64,1408]{2,1,0:T(8,128)(2,1)}, u32[]{:S(2)}, u32[]{:S(2)}) collective-permute-start(bf16[3,64,1408]{2,1,0:T(8,128)(2,1)S(1)} %slice.26), channel_id=1, source_target_pairs={{0,4},{4,8},{8,12},{12,0},{1,5},{5,9},{9,13},{13,1},{2,6},{6,10},{... | collective-permute-start | bytes 1622024 | tf_op jit(solution)/shard_map/ppermute | solution.py:261
  112.8 18.5 %collective-permute-start.2 = (bf16[3,128,1408]{2,1,0:T(8,128)(2,1)S(1)}, bf16[3,128,1408]{2,1,0:T(8,128)(2,1)}, u32[]{:S(2)}, u32[]{:S(2)}) collective-permute-start(bf16[3,128,1408]{2,1,0:T(8,128)(2,1)S(1)} %collective-permute-done.1.refs_3_), channel_id=1, source_target_pairs={{0,2},{2,0},{1,3},{3,1},{4,6},{6,4},{5,7},{7,5},{8,10},{10,8},{9,1... | collective-permute-start | bytes 3244040 | tf_op jit(solution)/shard_map/ppermute | solution.py:265
  114.8 16.6 %collective-permute-start.8 = (bf16[3,128,1408]{2,1,0:T(8,128)(2,1)S(1)}, bf16[3,128,1408]{2,1,0:T(8,128)(2,1)}, u32[]{:S(2)}, u32[]{:S(2)}) collective-permute-start(bf16[3,128,1408]{2,1,0:T(8,128)(2,1)S(1)} %collective-permute-done.4.refs_9_), channel_id=1, source_target_pairs={{0,2},{2,0},{1,3},{3,1},{4,6},{6,4},{5,7},{7,5},{8,10},{10,8},{9,1... | collective-permute-start | bytes 3244040 | tf_op jit(solution)/shard_map/ppermute | solution.py:265
  121.7 8.8 %collective-permute-start.6 = (bf16[3,64,1408]{2,1,0:T(8,128)(2,1)}, bf16[3,64,1408]{2,1,0:T(8,128)(2,1)}, u32[]{:S(2)}, u32[]{:S(2)}) collective-permute-start(bf16[3,64,1408]{2,1,0:T(8,128)(2,1)} %collective-permute-done.3.refs_5_), channel_id=1, source_target_pairs={{0,2},{2,0},{1,3},{3,1},{4,6},{6,4},{5,7},{7,5},{8,10},{10,8},{9,1... | collective-permute-start | bytes 1622024 | tf_op jit(solution)/shard_map/ppermute | solution.py:265
  127.2 4.2 %collective-permute-start.7 = (bf16[3,64,1408]{2,1,0:T(8,128)(2,1)}, bf16[3,64,1408]{2,1,0:T(8,128)(2,1)}, u32[]{:S(2)}, u32[]{:S(2)}) collective-permute-start(bf16[3,64,1408]{2,1,0:T(8,128)(2,1)} %collective-permute-done.5.refs_6_), channel_id=1, source_target_pairs={{0,2},{2,0},{1,3},{3,1},{4,6},{6,4},{5,7},{7,5},{8,10},{10,8},{9,1... | collective-permute-start | bytes 1622024 | tf_op jit(solution)/shard_map/ppermute | solution.py:265
  138.7 15.2 %copy-start.12 = (f32[1,128,2]{1,2,0:T(2,128)S(1)}, f32[1,128,2]{1,2,0:T(2,128)}, u32[]{:S(2)}) copy-start(f32[1,128,2]{1,2,0:T(2,128)} %param.22) | copy-start | bytes 3076
  138.7 54.0 %all-to-all-start.4 = ((bf16[64,40,128]{2,1,0:T(8,128)(2,1)}), bf16[64,40,128]{2,1,0:T(8,128)(2,1)S(1)}, u32[]{:S(2)}, u32[]{:S(2)}) async-start(bf16[64,40,128]{2,1,0:T(8,128)(2,1)} %bitcast.13), calls=%async_computation.4 | async-start | bytes 1310720 | tf_op jit(solution)/shard_map/all_to_all | solution.py:20

commit v5 on v3

--- a/solution.py
+++ b/solution.py
@@ -12,6 +12,7 @@
 OWNERS = ("z", "ylo", "yhi")
 LOG_ROWS = 8
 LANES = 128
+TILE = 512
 F32, BF16 = jnp.float32, jnp.bfloat16
 
 
@@ -44,7 +45,33 @@
     return block * cosine + pltpu.roll(block, block.shape[1] // 2, 1) * sine
 
 
-def summary_kernel(keys_ref, values_ref, log_ref, cos_ref, sin_ref, message_ref, turned_ref, total_ref):
+def summary_kernel(
+    keys_ref,
+    values_ref,
+    log_ref,
+    cos_ref,
+    sin_ref,
+    gate_hbm,
+    up_hbm,
+    down_hbm,
+    message_ref,
+    total_ref,
+    stacked_hbm,
+    shard_ref,
+    in_sems,
+    out_sems,
+):
+    shards = (gate_hbm, up_hbm, down_hbm)
+    loads = [
+        pltpu.make_async_copy(shard, shard_ref.at[index], in_sems.at[index])
+        for index, shard in enumerate(shards)
+    ]
+    stores = [
+        pltpu.make_async_copy(shard_ref.at[index], stacked_hbm.at[index], out_sems.at[index])
+        for index in range(len(shards))
+    ]
+    for load in loads:
+        load.start()
     heads, count = log_ref.shape
     head_dim = cos_ref.shape[1]
     parts = message_ref.shape[0] // heads
@@ -60,9 +87,12 @@
     trailing = jnp.exp(last - total)
     wide = jnp.broadcast_to(last, (heads, head_dim))
     for head in range(heads):
+        if head == heads // 2:
+            for load, store in zip(loads, stores):
+                load.wait()
+                store.start()
         lanes = slice(head * head_dim, (head + 1) * head_dim)
         keys = turned(keys_ref[:, lanes].astype(F32), cos_ref[...], sin_ref[...]).astype(BF16)
-        turned_ref[:, lanes] = keys
         faded = keys.astype(F32).T * trailing[head : head + 1]
         coarse = faded.astype(BF16)
         fine = (faded - coarse.astype(F32)).astype(BF16)
@@ -72,6 +102,8 @@
         for part in range(parts):
             message_ref[head * parts + part, :rows] = summary[part * rows : (part + 1) * rows]
             message_ref[head * parts + part, rows:] = logs
+    for store in stores:
+        store.wait()
 
 
 def inside_kernel(
@@ -82,20 +114,23 @@
     row = lax.broadcasted_iota(jnp.int32, (count, count), 0)
     column = lax.broadcasted_iota(jnp.int32, (count, count), 1)
     causal = row >= column
+    fade = jnp.zeros((count, count), F32)
     for head in range(heads):
         lanes = slice(head * head_dim, (head + 1) * head_dim)
         queries = turned(queries_ref[:, lanes].astype(F32), cos_ref[...], sin_ref[...])
         queries = (queries * head_dim ** (-0.5)).astype(BF16)
         turned_ref[:, lanes] = queries
+        keys = turned(keys_ref[:, lanes].astype(F32), cos_ref[...], sin_ref[...]).astype(BF16)
         scores = lax.dot_general(
-            queries, keys_ref[:, lanes], (((1,), (1,)), ((), ())), preferred_element_type=F32
+            queries, keys, (((1,), (1,)), ((), ())), preferred_element_type=F32
         )
         here = total_ref[head : head + 1, :]
         down = jnp.broadcast_to(here, (head_dim, count)).T
         spread = jnp.where(causal, down - here, 0.0)
         weights = jnp.where(causal, scores * jnp.exp(spread), 0.0).astype(BF16)
         inside_ref[:, lanes] = dot32(weights, values_ref[:, lanes])
-        fade_ref[:, lanes] = jnp.exp(down)
+        fade = jnp.where(column == head, jnp.exp(down), fade)
+    fade_ref[...] = fade
 
 
 def plane_sum_kernel(arrived_ref, message_ref):
@@ -147,7 +182,7 @@
     for head in range(chunks):
         lanes = slice(head * head_dim, (head + 1) * head_dim)
         far = dot32(queries_ref[:, lanes], state_ref[head * head_dim : (head + 1) * head_dim, :])
-        retrieved = inside_ref[:, lanes] + fade_ref[:, lanes] * far
+        retrieved = inside_ref[:, lanes] + fade_ref[:, head : head + 1] * far
         deviation = retrieved - jnp.mean(retrieved, axis=1, keepdims=True)
         variance = jnp.mean(deviation * deviation, axis=1, keepdims=True)
         normalized = deviation * lax.rsqrt(variance + 1e-05)
@@ -186,29 +221,30 @@
     arrived_ref, pieces, out_ref = refs[0], refs[1:-5], refs[-5]
     weights_ref, hidden_ref, packed_ref, sems = refs[-4:]
     width = weights_ref.shape[2]
-    copies = []
+    copies = [[] for _ in range(3)]
     for index in range(3):
         start = 0
         for number, piece in enumerate(pieces):
             size = piece.shape[1]
             copy = pltpu.make_async_copy(
                 piece.at[index],
-                weights_ref.at[index, pl.ds(start, size), :],
+                weights_ref.at[index, start : start + size, :],
                 sems.at[index, number],
             )
             copy.start()
-            copies.append(copy)
+            copies[index].append(copy)
             start += size
-    count = len(pieces)
-    for copy in copies[: 2 * count]:
+    for copy in copies[0]:
         copy.wait()
-    tile = 512
-    for start in range(0, width, tile):
-        columns = slice(start, min(width, start + tile))
+    for start in range(0, width, TILE):
+        columns = slice(start, min(width, start + TILE))
         gate = dot32(arrived_ref[...], weights_ref[0, :, columns])
+        if start == 0:
+            for copy in copies[1]:
+                copy.wait()
         up = dot32(arrived_ref[...], weights_ref[1, :, columns])
         hidden_ref[:, columns] = (gate / (1.0 + jnp.exp(-gate)) * up).astype(BF16)
-    for copy in copies[2 * count :]:
+    for copy in copies[2]:
         copy.wait()
     rows, lanes = arrived_ref.shape[0], packed_ref.shape[1]
     chunks = packed_ref.shape[0] // rows
@@ -302,23 +338,34 @@
     angles = position.astype(F32)[:, None] * np.tile(inverse, 2)[None, :]
     cosine, sine = jnp.cos(angles), jnp.sin(angles) * sign
 
-    out_message, turned_keys, total = pl.pallas_call(
+    shards = (3,) + w_gate.shape[1:]
+    any_space, in_vmem = pl.BlockSpec(memory_space=pl.ANY), pl.BlockSpec(memory_space=pltpu.VMEM)
+    out_message, total, stacked = pl.pallas_call(
         summary_kernel,
         name="summary",
-        out_shape=(shape(message, BF16), shape(wide, BF16), shape((head_count, tok_rows), F32)),
-        cost_estimate=cost(70000000, 1200000),
-        compiler_params=vmem(6),
-    )(keys[0], values[0], log_decay[0].T, cosine, sine)
+        out_shape=(
+            shape(message, BF16),
+            shape((head_count, tok_rows), F32),
+            shape(shards, BF16),
+        ),
+        in_specs=[in_vmem] * 5 + [any_space] * 3,
+        out_specs=(in_vmem, in_vmem, any_space),
+        scratch_shapes=[
+            pltpu.VMEM(shards, BF16),
+            pltpu.SemaphoreType.DMA((3,)),
+            pltpu.SemaphoreType.DMA((3,)),
+        ],
+        cost_estimate=cost(70000000, 3200000),
+    )(keys[0], values[0], log_decay[0].T, cosine, sine, w_gate[0], w_up[0], w_down[0])
     summaries = exchange(out_message, PLANE)
-    stacked = jnp.stack([w_gate[0], w_up[0], w_down[0]])
     after, before = along_x(stacked, 1), along_x(stacked, -1)
     turned_queries, inside, fade = pl.pallas_call(
         inside_kernel,
         name="inside",
-        out_shape=(shape(wide, BF16), shape(wide, F32), shape(wide, F32)),
+        out_shape=(shape(wide, BF16), shape(wide, F32), shape((tok_rows, tok_rows), F32)),
         cost_estimate=cost(70000000, 2200000),
         compiler_params=vmem(8),
-    )(queries[0], turned_keys, values[0], total, cosine, sine)
+    )(queries[0], keys[0], values[0], total, cosine, sine)
     sums = pl.pallas_call(
         plane_sum_kernel,
         name="plane_sum",

time: 195 us -> 195 us (level)
  local copies, waits for them, and re-layouts: 7.89 us -> 2.99 us
  Pallas kernels: 15.2 us -> 18.3 us
    unnamed x30 -> x24, local copies, waits for them, and re-layouts: 4.41 us -> 0.28 us
    pallas_call x1, Pallas kernels: 0.65 us -> 3.82 us  [body(): pl.pallas_call(summary_kernel, name='summary', out_shape=(shape(message,...]
  transfers between devices with their start and end apart: 13 -> 13, of which waited for: 7 -> 7; matrix products, arithmetic and copies ran while one was open for 3% -> 2% of each run, Pallas kernels for 1% -> 1%
where the time goes in v5:
time: 195 us; the launch traced here: 194 us
  waiting for transfers between devices  89.7 us (46%)
  starting transfers between devices  64.4 us (33%)
  Pallas kernels  18.3 us (9%)
  blocking collectives  16 us (8%)
  local copies, waits for them, and re-layouts  2.99 us (2%)
  other arithmetic  2.63 us (1%)
    all_to_all x4, waiting for transfers between devices, exchange(): return lax.all_to_all(blocks, axes, split_axis=0, concat_axis=0, tiled=True)  61.4 us
    all_to_all x4, starting transfers between devices, exchange(): return lax.all_to_all(blocks, axes, split_axis=0, concat_axis=0, tiled=True)  41.9 us
    ppermute x4, waiting for transfers between devices, along_x(): lax.ppermute(piece, 'x', [(i, (i - step) % size) for i in range(size)])  27.4 us
    all_to_all x1, blocking collectives, exchange(): return lax.all_to_all(blocks, axes, split_axis=0, concat_axis=0, tiled=True)  16 us
    ppermute x4, starting transfers between devices, along_x(): lax.ppermute(piece, 'x', [(i, (i - step) % size) for i in range(size)])  12.4 us
    ppermute x5, starting transfers between devices, swapped(): return lax.ppermute(piece, 'core', [(0, 1), (1, 0)])  10.1 us
    pallas_call x1, Pallas kernels, run_experts(): pl.pallas_call(expert_kernel, name='experts', out_shape=shape((rows * mod...  6.63 us
  transfers between devices with their start and end apart: 13, of which 7 were waited for; matrix products, arithmetic and copies ran while one was open for 2% of the time, Pallas kernels for 1%

profile of v5, /device:TPU:8, one launch (start us, length us, event | category | flops | bytes accessed | tf_op | source)
XLA Modules:
  0.0 194.3 jit_solution(10207187775940477198)
XLA Ops:
  0.0 1.6 fusion.3
  1.6 3.8 %summary.1 = (bf16[16,72,128]{2,1,0:T(8,128)(2,1)}, f32[8,128]{1,0:T(8,128)}, bf16[3,128,1408]{2,1,0:T(8,128)(2,1)}) custom-call(bf16[128,1024]{1,0:T(8,128)(2,1)} %bitcast.41, bf16[128,1024]{1,0:T(8,128)(2,1)} %bitcast.43, f32[8,128]{1,0:T(8,128)} %bitcast.54, f32[128,128]{1,0:T(8,128)} %get-tuple-element.24.cos_ref, f32[128,128]{1,0:T(8,128)} %get-tuple-element.23.sin_ref, ...), custom_call_target="tpu_custom_call" | custom-call | flops 70000000 | bytes 3200000 | tf_op jit(solution)/shard_map/summary/pallas_call | solution.py:343
  5.5 16.0 %all_to_all.25.arrived_ref = bf16[16,72,128]{2,1,0:T(8,128)(2,1)S(1)} all-to-all(bf16[16,72,128]{2,1,0:T(8,128)(2,1)} %get-tuple-element.13), channel_id=1, replica_groups=mesh['z'=16,'ylo'=2,'x'=4,'core'=2,'yhi'=2] {'ylo','x','core'}, dimensions={0} | all-to-all | bytes 589824 | tf_op jit(solution)/shard_map/all_to_all | solution.py:20
  21.4 0.8 plane_sum.1
  22.3 11.8 %all-to-all-start.1 = ((bf16[16,72,128]{2,1,0:T(8,128)(2,1)}), bf16[16,72,128]{2,1,0:T(8,128)(2,1)S(1)}, u32[]{:S(2)}, u32[]{:S(2)}) async-start(bf16[16,72,128]{2,1,0:T(8,128)(2,1)} %plane_sum.1), calls=%async_computation.1 | async-start | bytes 589824 | tf_op jit(solution)/shard_map/all_to_all | solution.py:20
  34.6 0.6 reduce-window.6
  35.7 18.3 %all-to-all-done.1.planes_ref = bf16[16,72,128]{2,1,0:T(8,128)(2,1)S(1)} async-done(((bf16[16,72,128]{2,1,0:T(8,128)(2,1)}), bf16[16,72,128]{2,1,0:T(8,128)(2,1)S(1)}, u32[]{:S(2)}, u32[]{:S(2)}) %all-to-all-start.1) | async-done | bytes 294944 | tf_op jit(solution)/shard_map/all_to_all | solution.py:20
  54.0 0.9 enter.1
  54.8 4.5 %all-to-all-start.2 = ((bf16[16,64,128]{2,1,0:T(8,128)(2,1)}), bf16[16,64,128]{2,1,0:T(8,128)(2,1)S(1)}, u32[]{:S(2)}, u32[]{:S(2)}) async-start(bf16[16,64,128]{2,1,0:T(8,128)(2,1)} %enter.1), calls=%async_computation.2 | async-start | bytes 524288 | tf_op jit(solution)/shard_map/all_to_all | solution.py:20
  59.6 1.5 inside.1
  61.1 4.8 %all-to-all-done.2 = bf16[16,64,128]{2,1,0:T(8,128)(2,1)S(1)} async-done(((bf16[16,64,128]{2,1,0:T(8,128)(2,1)}), bf16[16,64,128]{2,1,0:T(8,128)(2,1)S(1)}, u32[]{:S(2)}, u32[]{:S(2)}) %all-to-all-start.2) | async-done | bytes 262176 | tf_op jit(solution)/shard_map/all_to_all | solution.py:20
  65.8 2.8 %outgoing.1 = (f32[128,1024]{1,0:T(8,128)S(1)}, bf16[2560,128]{1,0:T(8,128)(2,1)}) custom-call(s32[8]{0:T(128)S(1)} %fusion.8.own_ref, bf16[1024,128]{1,0:T(8,128)(2,1)S(1)} %bitcast.45, bf16[128,1024]{1,0:T(8,128)(2,1)S(1)} %get-tuple-element.15.queries_ref, f32[128,1024]{1,0:T(8,128)S(1)} %get-tuple-element.16.inside_ref, ...), custom_call_target="tpu_custom_call" | custom-call | flops 120000000 | bytes 3000000 | tf_op jit(solution)/shard_map/outgoing/pallas_call | solution.py:407
  68.6 10.5 %all-to-all-start.3 = ((bf16[64,40,128]{2,1,0:T(8,128)(2,1)}), bf16[64,40,128]{2,1,0:T(8,128)(2,1)}, u32[]{:S(2)}, u32[]{:S(2)}) async-start(bf16[64,40,128]{2,1,0:T(8,128)(2,1)} %bitcast.15), calls=%async_computation.3 | async-start | bytes 1310720 | tf_op jit(solution)/shard_map/all_to_all | solution.py:20
  79.1 2.7 %collective-permute-start.1 = (bf16[3,128,1408]{2,1,0:T(8,128)(2,1)}, bf16[3,128,1408]{2,1,0:T(8,128)(2,1)S(1)}, u32[]{:S(2)}, u32[]{:S(2)}) collective-permute-start(bf16[3,128,1408]{2,1,0:T(8,128)(2,1)} %get-tuple-element.19.refs_1_), channel_id=1, source_target_pairs={{0,12},{4,0},{8,4},{12,8},{1,13},{5,1},{9,5},{13,9},{2,14},{6,2},{... | collective-permute-start | bytes 3244040 | tf_op jit(solution)/shard_map/ppermute | solution.py:296
  81.8 3.2 %collective-permute-start.4 = (bf16[3,128,1408]{2,1,0:T(8,128)(2,1)}, bf16[3,128,1408]{2,1,0:T(8,128)(2,1)S(1)}, u32[]{:S(2)}, u32[]{:S(2)}) collective-permute-start(bf16[3,128,1408]{2,1,0:T(8,128)(2,1)} %get-tuple-element.19.refs_1_), channel_id=1, source_target_pairs={{0,4},{4,8},{8,12},{12,0},{1,5},{5,9},{9,13},{13,1},{2,6},{6,10},{... | collective-permute-start | bytes 3244040 | tf_op jit(solution)/shard_map/ppermute | solution.py:296
  84.9 1.9 collective-permute-start
  86.9 19.3 %collective-permute-done.1.refs_3_ = bf16[3,128,1408]{2,1,0:T(8,128)(2,1)S(1)} collective-permute-done((bf16[3,128,1408]{2,1,0:T(8,128)(2,1)}, bf16[3,128,1408]{2,1,0:T(8,128)(2,1)S(1)}, u32[]{:S(2)}, u32[]{:S(2)}) %collective-permute-start.1) | collective-permute-done | bytes 1081376 | tf_op jit(solution)/shard_map/ppermute | solution.py:296
  106.2 4.6 %collective-permute-start.3 = (bf16[3,64,1408]{2,1,0:T(8,128)(2,1)S(1)}, bf16[3,64,1408]{2,1,0:T(8,128)(2,1)}, u32[]{:S(2)}, u32[]{:S(2)}) collective-permute-start(bf16[3,64,1408]{2,1,0:T(8,128)(2,1)S(1)} %slice.25), channel_id=1, source_target_pairs={{0,12},{4,0},{8,4},{12,8},{1,13},{5,1},{9,5},{13,9},{2,14},{6,2},{... | collective-permute-start | bytes 1622024 | tf_op jit(solution)/shard_map/ppermute | solution.py:296
  110.9 1.9 collective-permute-start.5
  112.8 1.9 collective-permute-start.2
  114.8 2.4 %collective-permute-start.8 = (bf16[3,128,1408]{2,1,0:T(8,128)(2,1)S(1)}, bf16[3,128,1408]{2,1,0:T(8,128)(2,1)}, u32[]{:S(2)}, u32[]{:S(2)}) collective-permute-start(bf16[3,128,1408]{2,1,0:T(8,128)(2,1)S(1)} %collective-permute-done.4.refs_9_), channel_id=1, source_target_pairs={{0,2},{2,0},{1,3},{3,1},{4,6},{6,4},{5,7},{7,5},{8,10},{10,8},{9,1... | collective-permute-start | bytes 3244040 | tf_op jit(solution)/shard_map/ppermute | solution.py:300
  117.2 4.5 %collective-permute-done.3.refs_5_ = bf16[3,64,1408]{2,1,0:T(8,128)(2,1)} collective-permute-done((bf16[3,64,1408]{2,1,0:T(8,128)(2,1)S(1)}, bf16[3,64,1408]{2,1,0:T(8,128)(2,1)}, u32[]{:S(2)}, u32[]{:S(2)}) %collective-permute-start.3) | collective-permute-done | bytes 540704 | tf_op jit(solution)/shard_map/ppermute | solution.py:296
  121.7 1.9 collective-permute-start.6
  123.6 3.6 %collective-permute-done.5.refs_6_ = bf16[3,64,1408]{2,1,0:T(8,128)(2,1)} collective-permute-done((bf16[3,64,1408]{2,1,0:T(8,128)(2,1)S(1)}, bf16[3,64,1408]{2,1,0:T(8,128)(2,1)}, u32[]{:S(2)}, u32[]{:S(2)}) %collective-permute-start.5) | collective-permute-done | bytes 540704 | tf_op jit(solution)/shard_map/ppermute | solution.py:296
  127.2 1.9 collective-permute-start.7
  129.1 1.4 reshape.50.refs_0_
  130.5 0.8 collective-permute-done.7.refs_8_
  131.3 6.6 %experts.1 = bf16[2560,128]{1,0:T(8,128)(2,1)} custom-call(bf16[320,1024]{1,0:T(8,128)(2,1)S(1)} %reshape.50.refs_0_, bf16[3,128,1408]{2,1,0:T(8,128)(2,1)} %get-tuple-element.19.refs_1_, bf16[3,128,1408]{2,1,0:T(8,128)(2,1)} %collective-permute-done.refs_2_, bf16[3,128,1408]{2,1,0:T(8,128)(2,1)S(1)} %collective-permute-done.1.refs_3_, ...), custom_call_target="tpu_custom_call" | custom-call | flops 2768240640 | bytes 8650752 | tf_op jit(solution)/shard_map/experts/pallas_call | solution.py:277
  138.0 15.1 %all-to-all-start.4 = ((bf16[64,40,128]{2,1,0:T(8,128)(2,1)}), bf16[64,40,128]{2,1,0:T(8,128)(2,1)S(1)}, u32[]{:S(2)}, u32[]{:S(2)}) async-start(bf16[64,40,128]{2,1,0:T(8,128)(2,1)} %bitcast.16), calls=%async_computation.4 | async-start | bytes 1310720 | tf_op jit(solution)/shard_map/all_to_all | solution.py:20
  153.7 38.4 %all-to-all-done.4 = bf16[64,40,128]{2,1,0:T(8,128)(2,1)S(1)} async-done(((bf16[64,40,128]{2,1,0:T(8,128)(2,1)}), bf16[64,40,128]{2,1,0:T(8,128)(2,1)S(1)}, u32[]{:S(2)}, u32[]{:S(2)}) %all-to-all-start.4) | async-done | bytes 655392 | tf_op jit(solution)/shard_map/all_to_all | solution.py:20
  192.1 0.3 reshape.52.returned_ref
  192.4 1.9 combine.1
  (50 shorter events, 1.7 us)
Async XLA Ops:
  5.5 28.6 %copy-start.9 = (s32[1,128,2]{1,2,0:T(2,128)S(1)}, s32[1,128,2]{1,2,0:T(2,128)}, u32[]{:S(2)}) copy-start(s32[1,128,2]{1,2,0:T(2,128)} %param.21) | copy-start | bytes 3076
  22.3 31.7 %all-to-all-start.1 = ((bf16[16,72,128]{2,1,0:T(8,128)(2,1)}), bf16[16,72,128]{2,1,0:T(8,128)(2,1)S(1)}, u32[]{:S(2)}, u32[]{:S(2)}) async-start(bf16[16,72,128]{2,1,0:T(8,128)(2,1)} %plane_sum.1), calls=%async_computation.1 | async-start | bytes 589824 | tf_op jit(solution)/shard_map/all_to_all | solution.py:20
  34.5 25.0 %copy-start = (bf16[1,128,1024]{2,1,0:T(8,128)(2,1)S(1)}, bf16[1,128,1024]{2,1,0:T(8,128)(2,1)}, u32[]{:S(2)}) copy-start(bf16[1,128,1024]{2,1,0:T(8,128)(2,1)} %param.16) | copy-start | bytes 786436
  34.5 25.0 %copy-start.1 = (bf16[1,128,1024]{2,1,0:T(8,128)(2,1)S(1)}, bf16[1,128,1024]{2,1,0:T(8,128)(2,1)}, u32[]{:S(2)}) copy-start(bf16[1,128,1024]{2,1,0:T(8,128)(2,1)} %param.17) | copy-start | bytes 786436
  34.5 25.0 %copy-start.2 = (f32[128,128]{1,0:T(8,128)S(1)}, f32[128,128]{1,0:T(8,128)}, u32[]{:S(2)}) copy-start(f32[128,128]{1,0:T(8,128)} %get-tuple-element.23.sin_ref) | copy-start | bytes 196612
  34.5 25.0 %copy-start.3 = (f32[128,128]{1,0:T(8,128)S(1)}, f32[128,128]{1,0:T(8,128)}, u32[]{:S(2)}) copy-start(f32[128,128]{1,0:T(8,128)} %get-tuple-element.24.cos_ref) | copy-start | bytes 196612
  34.6 25.0 %copy-start.4 = (bf16[1,128,1024]{2,1,0:T(8,128)(2,1)S(1)}, bf16[1,128,1024]{2,1,0:T(8,128)(2,1)}, u32[]{:S(2)}) copy-start(bf16[1,128,1024]{2,1,0:T(8,128)(2,1)} %param.15) | copy-start | bytes 786436
  34.6 25.0 %copy-start.8 = (f32[8,128]{1,0:T(8,128)S(1)}, f32[8,128]{1,0:T(8,128)}, u32[]{:S(2)}) copy-start(f32[8,128]{1,0:T(8,128)} %get-tuple-element.14.total_ref) | copy-start | bytes 12292
  54.8 11.0 %copy-start.5 = (bf16[1,128,1024]{2,1,0:T(8,128)(2,1)S(1)}, bf16[1,128,1024]{2,1,0:T(8,128)(2,1)}, u32[]{:S(2)}) copy-start(bf16[1,128,1024]{2,1,0:T(8,128)(2,1)} %param.14) | copy-start | bytes 786436
  54.8 11.0 %copy-start.6 = (f32[1024]{0:T(1024)S(1)}, f32[1024]{0:T(1024)}, u32[]{:S(2)}) copy-start(f32[1024]{0:T(1024)} %param.19) | copy-start | bytes 12292
  54.8 11.0 %copy-start.7 = (f32[1024]{0:T(1024)S(1)}, f32[1024]{0:T(1024)}, u32[]{:S(2)}) copy-start(f32[1024]{0:T(1024)} %param.20) | copy-start | bytes 12292
  54.8 11.0 %all-to-all-start.2 = ((bf16[16,64,128]{2,1,0:T(8,128)(2,1)}), bf16[16,64,128]{2,1,0:T(8,128)(2,1)S(1)}, u32[]{:S(2)}, u32[]{:S(2)}) async-start(bf16[16,64,128]{2,1,0:T(8,128)(2,1)} %enter.1), calls=%async_computation.2 | async-start | bytes 524288 | tf_op jit(solution)/shard_map/all_to_all | solution.py:20
  68.6 60.5 %all-to-all-start.3 = ((bf16[64,40,128]{2,1,0:T(8,128)(2,1)}), bf16[64,40,128]{2,1,0:T(8,128)(2,1)}, u32[]{:S(2)}, u32[]{:S(2)}) async-start(bf16[64,40,128]{2,1,0:T(8,128)(2,1)} %bitcast.15), calls=%async_computation.3 | async-start | bytes 1310720 | tf_op jit(solution)/shard_map/all_to_all | solution.py:20
  79.1 27.1 %collective-permute-start.1 = (bf16[3,128,1408]{2,1,0:T(8,128)(2,1)}, bf16[3,128,1408]{2,1,0:T(8,128)(2,1)S(1)}, u32[]{:S(2)}, u32[]{:S(2)}) collective-permute-start(bf16[3,128,1408]{2,1,0:T(8,128)(2,1)} %get-tuple-element.19.refs_1_), channel_id=1, source_target_pairs={{0,12},{4,0},{8,4},{12,8},{1,13},{5,1},{9,5},{13,9},{2,14},{6,2},{... | collective-permute-start | bytes 3244040 | tf_op jit(solution)/shard_map/ppermute | solution.py:296
  81.8 29.1 %collective-permute-start.4 = (bf16[3,128,1408]{2,1,0:T(8,128)(2,1)}, bf16[3,128,1408]{2,1,0:T(8,128)(2,1)S(1)}, u32[]{:S(2)}, u32[]{:S(2)}) collective-permute-start(bf16[3,128,1408]{2,1,0:T(8,128)(2,1)} %get-tuple-element.19.refs_1_), channel_id=1, source_target_pairs={{0,4},{4,8},{8,12},{12,0},{1,5},{5,9},{9,13},{13,1},{2,6},{6,10},{... | collective-permute-start | bytes 3244040 | tf_op jit(solution)/shard_map/ppermute | solution.py:296
  84.9 45.5 %collective-permute-start = (bf16[3,128,1408]{2,1,0:T(8,128)(2,1)}, bf16[3,128,1408]{2,1,0:T(8,128)(2,1)}, u32[]{:S(2)}, u32[]{:S(2)}) collective-permute-start(bf16[3,128,1408]{2,1,0:T(8,128)(2,1)} %get-tuple-element.19.refs_1_), channel_id=1, source_target_pairs={{0,2},{2,0},{1,3},{3,1},{4,6},{6,4},{5,7},{7,5},{8,10},{10,8},{9,1... | collective-permute-start | bytes 3244040 | tf_op jit(solution)/shard_map/ppermute | solution.py:300
  106.2 15.5 %collective-permute-start.3 = (bf16[3,64,1408]{2,1,0:T(8,128)(2,1)S(1)}, bf16[3,64,1408]{2,1,0:T(8,128)(2,1)}, u32[]{:S(2)}, u32[]{:S(2)}) collective-permute-start(bf16[3,64,1408]{2,1,0:T(8,128)(2,1)S(1)} %slice.25), channel_id=1, source_target_pairs={{0,12},{4,0},{8,4},{12,8},{1,13},{5,1},{9,5},{13,9},{2,14},{6,2},{... | collective-permute-start | bytes 1622024 | tf_op jit(solution)/shard_map/ppermute | solution.py:296
  110.9 16.3 %collective-permute-start.5 = (bf16[3,64,1408]{2,1,0:T(8,128)(2,1)S(1)}, bf16[3,64,1408]{2,1,0:T(8,128)(2,1)}, u32[]{:S(2)}, u32[]{:S(2)}) collective-permute-start(bf16[3,64,1408]{2,1,0:T(8,128)(2,1)S(1)} %slice.26), channel_id=1, source_target_pairs={{0,4},{4,8},{8,12},{12,0},{1,5},{5,9},{9,13},{13,1},{2,6},{6,10},{... | collective-permute-start | bytes 1622024 | tf_op jit(solution)/shard_map/ppermute | solution.py:296
  112.8 18.5 %collective-permute-start.2 = (bf16[3,128,1408]{2,1,0:T(8,128)(2,1)S(1)}, bf16[3,128,1408]{2,1,0:T(8,128)(2,1)}, u32[]{:S(2)}, u32[]{:S(2)}) collective-permute-start(bf16[3,128,1408]{2,1,0:T(8,128)(2,1)S(1)} %collective-permute-done.1.refs_3_), channel_id=1, source_target_pairs={{0,2},{2,0},{1,3},{3,1},{4,6},{6,4},{5,7},{7,5},{8,10},{10,8},{9,1... | collective-permute-start | bytes 3244040 | tf_op jit(solution)/shard_map/ppermute | solution.py:300
  114.8 16.6 %collective-permute-start.8 = (bf16[3,128,1408]{2,1,0:T(8,128)(2,1)S(1)}, bf16[3,128,1408]{2,1,0:T(8,128)(2,1)}, u32[]{:S(2)}, u32[]{:S(2)}) collective-permute-start(bf16[3,128,1408]{2,1,0:T(8,128)(2,1)S(1)} %collective-permute-done.4.refs_9_), channel_id=1, source_target_pairs={{0,2},{2,0},{1,3},{3,1},{4,6},{6,4},{5,7},{7,5},{8,10},{10,8},{9,1... | collective-permute-start | bytes 3244040 | tf_op jit(solution)/shard_map/ppermute | solution.py:300
  121.7 8.8 %collective-permute-start.6 = (bf16[3,64,1408]{2,1,0:T(8,128)(2,1)}, bf16[3,64,1408]{2,1,0:T(8,128)(2,1)}, u32[]{:S(2)}, u32[]{:S(2)}) collective-permute-start(bf16[3,64,1408]{2,1,0:T(8,128)(2,1)} %collective-permute-done.3.refs_5_), channel_id=1, source_target_pairs={{0,2},{2,0},{1,3},{3,1},{4,6},{6,4},{5,7},{7,5},{8,10},{10,8},{9,1... | collective-permute-start | bytes 1622024 | tf_op jit(solution)/shard_map/ppermute | solution.py:300
  127.2 4.2 %collective-permute-start.7 = (bf16[3,64,1408]{2,1,0:T(8,128)(2,1)}, bf16[3,64,1408]{2,1,0:T(8,128)(2,1)}, u32[]{:S(2)}, u32[]{:S(2)}) collective-permute-start(bf16[3,64,1408]{2,1,0:T(8,128)(2,1)} %collective-permute-done.5.refs_6_), channel_id=1, source_target_pairs={{0,2},{2,0},{1,3},{3,1},{4,6},{6,4},{5,7},{7,5},{8,10},{10,8},{9,1... | collective-permute-start | bytes 1622024 | tf_op jit(solution)/shard_map/ppermute | solution.py:300
  138.0 15.3 %copy-start.10 = (f32[1,128,2]{1,2,0:T(2,128)S(1)}, f32[1,128,2]{1,2,0:T(2,128)}, u32[]{:S(2)}) copy-start(f32[1,128,2]{1,2,0:T(2,128)} %param.22) | copy-start | bytes 3076
  138.0 54.1 %all-to-all-start.4 = ((bf16[64,40,128]{2,1,0:T(8,128)(2,1)}), bf16[64,40,128]{2,1,0:T(8,128)(2,1)S(1)}, u32[]{:S(2)}, u32[]{:S(2)}) async-start(bf16[64,40,128]{2,1,0:T(8,128)(2,1)} %bitcast.16), calls=%async_computation.4 | async-start | bytes 1310720 | tf_op jit(solution)/shard_map/all_to_all | solution.py:20

commit v6 on v5

--- a/solution.py
+++ b/solution.py
@@ -6,10 +6,10 @@
 from jax.experimental.pallas import tpu as pltpu
 from jax.sharding import Mesh, PartitionSpec as P
 
-CTX = ("z", "ylo")
+CTX = ("zhi", "zlo", "ylo")
 EXP = ("x", "core")
 PLANE = ("ylo", "x", "core")
-OWNERS = ("z", "ylo", "yhi")
+OWNERS = ("zhi", "zlo", "ylo", "yhi")
 LOG_ROWS = 8
 LANES = 128
 TILE = 512
@@ -46,8 +46,8 @@
 
 
 def summary_kernel(
-    keys_ref,
-    values_ref,
+    keys_hbm,
+    values_hbm,
     log_ref,
     cos_ref,
     sin_ref,
@@ -57,7 +57,10 @@
     message_ref,
     total_ref,
     stacked_hbm,
+    keys_ref,
+    values_ref,
     shard_ref,
+    own_sems,
     in_sems,
     out_sems,
 ):
@@ -70,7 +73,11 @@
         pltpu.make_async_copy(shard_ref.at[index], stacked_hbm.at[index], out_sems.at[index])
         for index in range(len(shards))
     ]
-    for load in loads:
+    own = [
+        pltpu.make_async_copy(keys_hbm, keys_ref, own_sems.at[0]),
+        pltpu.make_async_copy(values_hbm, values_ref, own_sems.at[1]),
+    ]
+    for load in own + loads:
         load.start()
     heads, count = log_ref.shape
     head_dim = cos_ref.shape[1]
@@ -86,8 +93,10 @@
     last = total[:, count - 1 :]
     trailing = jnp.exp(last - total)
     wide = jnp.broadcast_to(last, (heads, head_dim))
+    for load in own:
+        load.wait()
     for head in range(heads):
-        if head == heads // 2:
+        if head == 2:
             for load, store in zip(loads, stores):
                 load.wait()
                 store.start()
@@ -133,7 +142,7 @@
     fade_ref[...] = fade
 
 
-def plane_sum_kernel(arrived_ref, message_ref):
+def sum_kernel(arrived_ref, message_ref):
     plane, rows, head_dim = arrived_ref.shape
     rows = rows - LOG_ROWS
     total = jnp.zeros((rows, head_dim), F32)
@@ -143,19 +152,20 @@
         total = jnp.exp(log) * total + arrived_ref[block, :rows].astype(F32)
         log_total = log_total + log
     total, logs = total.astype(BF16), log_rows(log_total)
-    for z in range(message_ref.shape[0]):
-        message_ref[z, :rows] = total
-        message_ref[z, rows:] = logs
-
-
-def entering_kernel(own_ref, arrived_ref, planes_ref, entering_ref):
+    for member in range(message_ref.shape[0]):
+        message_ref[member, :rows] = total
+        message_ref[member, rows:] = logs
+
+
+def entering_kernel(own_ref, arrived_ref, near_ref, far_ref, entering_ref):
     rows = entering_ref.shape[1]
-    own = own_ref[0]
     state = jnp.zeros(entering_ref.shape[1:], F32)
-    for z in range(planes_ref.shape[0]):
-        log = log_row(planes_ref[z, rows:])
-        later = jnp.exp(log) * state + planes_ref[z, :rows].astype(F32)
-        state = jnp.where(z < own, later, state)
+    for level, sums_ref in enumerate((far_ref, near_ref)):
+        own = own_ref[level]
+        for member in range(sums_ref.shape[0]):
+            log = log_row(sums_ref[member, rows:])
+            later = jnp.exp(log) * state + sums_ref[member, :rows].astype(F32)
+            state = jnp.where(member < own, later, state)
     for block in range(arrived_ref.shape[0]):
         entering_ref[block] = state.astype(BF16)
         log = log_row(arrived_ref[block, rows:])
@@ -291,6 +301,16 @@
     )(arrived, *pieces)
 
 
+def summed(parts, members):
+    return pl.pallas_call(
+        sum_kernel,
+        name="sums",
+        out_shape=shape((members,) + parts.shape[1:], BF16),
+        cost_estimate=cost(500000, 600000),
+        compiler_params=vmem(4),
+    )(parts)
+
+
 def along_x(piece, step):
     size = lax.axis_size("x")
     return lax.ppermute(piece, "x", [(i, (i - step) % size) for i in range(size)])
@@ -326,7 +346,7 @@
     head_count = log_decay.shape[2]
     head_dim = model_width // head_count
     wide = (tok_rows, model_width)
-    plane, depth = lax.axis_size(PLANE), lax.axis_size("z")
+    plane = lax.axis_size(PLANE)
     part_rows = head_count * head_dim // plane
     message = (plane, part_rows + LOG_ROWS, head_dim)
 
@@ -348,10 +368,13 @@
             shape((head_count, tok_rows), F32),
             shape(shards, BF16),
         ),
-        in_specs=[in_vmem] * 5 + [any_space] * 3,
+        in_specs=[any_space] * 2 + [in_vmem] * 3 + [any_space] * 3,
         out_specs=(in_vmem, in_vmem, any_space),
         scratch_shapes=[
+            pltpu.VMEM(wide, BF16),
+            pltpu.VMEM(wide, BF16),
             pltpu.VMEM(shards, BF16),
+            pltpu.SemaphoreType.DMA((2,)),
             pltpu.SemaphoreType.DMA((3,)),
             pltpu.SemaphoreType.DMA((3,)),
         ],
@@ -366,24 +389,18 @@
         cost_estimate=cost(70000000, 2200000),
         compiler_params=vmem(8),
     )(queries[0], keys[0], values[0], total, cosine, sine)
-    sums = pl.pallas_call(
-        plane_sum_kernel,
-        name="plane_sum",
-        out_shape=shape((depth,) + message[1:], BF16),
-        cost_estimate=cost(500000, 600000),
-        compiler_params=vmem(4),
-    )(summaries)
-    sums = exchange(sums, "z")
+    near = exchange(summed(summaries, lax.axis_size("zlo")), "zlo")
+    far = exchange(summed(near, lax.axis_size("zhi")), "zhi")
     own_other = swapped(stacked)
     entering = pl.pallas_call(
         entering_kernel,
         name="enter",
         out_shape=shape((plane, part_rows, head_dim), BF16),
         in_specs=[pl.BlockSpec(memory_space=pltpu.SMEM)]
-        + [pl.BlockSpec(memory_space=pltpu.VMEM)] * 2,
+        + [pl.BlockSpec(memory_space=pltpu.VMEM)] * 3,
         cost_estimate=cost(900000, 900000),
         compiler_params=vmem(4),
-    )(lax.axis_index("z")[None], summaries, sums)
+    )(jnp.stack([lax.axis_index("zhi"), lax.axis_index("zlo")]), summaries, near, far)
     state_in = exchange(entering, PLANE).reshape(model_width, head_dim)
     after_other, before_other = swapped(after), swapped(before)
 
@@ -430,9 +447,10 @@
     packed = (expert_count, capacity * model_width // LANES, LANES)
     arrived = exchange(outgoing.reshape(packed), OWNERS).reshape(slot_count, model_width)
     cut = stacked.shape[1] // 2
-    far = [along_x(after[:, :cut], 1), along_x(before[:, cut:], -1)]
-    far_other = [swapped(piece) for piece in far]
-    pieces = [stacked, own_other, after, after_other, *far, *far_other, before, before_other]
+    relayed = [along_x(after[:, :cut], 1), along_x(before[:, cut:], -1)]
+    relayed_other = [swapped(piece) for piece in relayed]
+    pieces = [stacked, own_other, after, after_other]
+    pieces += [*relayed, *relayed_other, before, before_other]
     expert_out = run_experts(arrived, pieces)
     returned = exchange(expert_out.reshape(packed), OWNERS).reshape(slot_count, model_width)
     picks = [
@@ -455,7 +473,8 @@
 def solution(mesh):
     ctx, exp, dp = mesh.shape["ctx"], mesh.shape["exp"], mesh.shape["dp"]
     split = Mesh(
-        mesh.devices.reshape(ctx // 2, 2, exp // 2, 2, dp), ("z", "ylo", "x", "core", "yhi")
+        mesh.devices.reshape(ctx // 8, 4, 2, exp // 2, 2, dp),
+        ("zhi", "zlo", "ylo", "x", "core", "yhi"),
     )
     tokens = P("yhi", CTX + EXP, None)
     experts = P(OWNERS, EXP, None)

time: 195 us -> 197 us (1.010)
  blocking collectives: 16 us -> 0 us
  starting transfers between devices: 64.4 us -> 74.2 us
  waiting for transfers between devices: 89.7 us -> 95.3 us
    all_to_all x1 -> x0, blocking collectives: 16 us -> none  [exchange(): return lax.all_to_all(blocks, axes, split_axis=0, concat_axis=0, tiled=True)]
    all_to_all x4 -> x6, starting transfers between devices: 41.9 us -> 51.8 us  [exchange(): return lax.all_to_all(blocks, axes, split_axis=0, concat_axis=0, tiled=True)]
    all_to_all x4 -> x6, waiting for transfers between devices: 61.4 us -> 67.1 us  [exchange(): return lax.all_to_all(blocks, axes, split_axis=0, concat_axis=0, tiled=True)]
  transfers between devices with their start and end apart: 13 -> 15, of which waited for: 7 -> 9; matrix products, arithmetic and copies ran while one was open for 2% -> 2% of each run, Pallas kernels for 1% -> 1%
where the time goes in v6:
time: 197 us; the launch traced here: 196 us
  waiting for transfers between devices  95.3 us (48%)
  starting transfers between devices  74.2 us (38%)
  Pallas kernels  19.9 us (10%)
  local copies, waits for them, and re-layouts  2.98 us (2%)
  other arithmetic  2.7 us (1%)
    all_to_all x6, waiting for transfers between devices, exchange(): return lax.all_to_all(blocks, axes, split_axis=0, concat_axis=0, tiled=True)  67.1 us
    all_to_all x6, starting transfers between devices, exchange(): return lax.all_to_all(blocks, axes, split_axis=0, concat_axis=0, tiled=True)  51.8 us
    ppermute x4, waiting for transfers between devices, along_x(): lax.ppermute(piece, 'x', [(i, (i - step) % size) for i in range(size)])  27.4 us
    ppermute x4, starting transfers between devices, along_x(): lax.ppermute(piece, 'x', [(i, (i - step) % size) for i in range(size)])  12.4 us
    ppermute x5, starting transfers between devices, swapped(): return lax.ppermute(piece, 'core', [(0, 1), (1, 0)])  10.1 us
    pallas_call x1, Pallas kernels, run_experts(): pl.pallas_call(expert_kernel, name='experts', out_shape=shape((rows * mod...  6.68 us
    pallas_call x1, Pallas kernels, body(): pl.pallas_call(summary_kernel, name='summary', out_shape=(shape(message,...  4.28 us
  transfers between devices with their start and end apart: 15, of which 9 were waited for; matrix products, arithmetic and copies ran while one was open for 2% of the time, Pallas kernels for 1%

profile of v6, /device:TPU:8, one launch (start us, length us, event | category | flops | bytes accessed | tf_op | source)
XLA Modules:
  0.0 195.5 jit_solution(3683682132879128535)
XLA Ops:
  0.0 1.6 fusion.3
  1.6 4.3 %summary.1 = (bf16[16,72,128]{2,1,0:T(8,128)(2,1)}, f32[8,128]{1,0:T(8,128)}, bf16[3,128,1408]{2,1,0:T(8,128)(2,1)}) custom-call(bf16[128,1024]{1,0:T(8,128)(2,1)} %bitcast.42, bf16[128,1024]{1,0:T(8,128)(2,1)} %bitcast.44, f32[8,128]{1,0:T(8,128)} %bitcast.55, f32[128,128]{1,0:T(8,128)} %get-tuple-element.24.cos_ref, f32[128,128]{1,0:T(8,128)} %get-tuple-element.23.sin_ref, ...), custom_call_target="tpu_custom_call" | custom-call | flops 70000000 | bytes 3200000 | tf_op jit(solution)/shard_map/summary/pallas_call | solution.py:363
  5.9 9.2 %all-to-all-start = ((bf16[16,72,128]{2,1,0:T(8,128)(2,1)}), bf16[16,72,128]{2,1,0:T(8,128)(2,1)S(1)}, u32[]{:S(2)}, u32[]{:S(2)}) async-start(bf16[16,72,128]{2,1,0:T(8,128)(2,1)} %get-tuple-element.13), calls=%async_computation | async-start | bytes 589824 | tf_op jit(solution)/shard_map/all_to_all | solution.py:20
  15.4 6.5 %all-to-all-done.arrived_ref = bf16[16,72,128]{2,1,0:T(8,128)(2,1)S(1)} async-done(((bf16[16,72,128]{2,1,0:T(8,128)(2,1)}), bf16[16,72,128]{2,1,0:T(8,128)(2,1)S(1)}, u32[]{:S(2)}, u32[]{:S(2)}) %all-to-all-start) | async-done | bytes 294944 | tf_op jit(solution)/shard_map/all_to_all | solution.py:20
  22.6 3.3 %all-to-all-start.1 = ((bf16[4,72,128]{2,1,0:T(8,128)(2,1)}), bf16[4,72,128]{2,1,0:T(8,128)(2,1)S(1)}, u32[]{:S(2)}, u32[]{:S(2)}) async-start(bf16[4,72,128]{2,1,0:T(8,128)(2,1)} %sums.2), calls=%async_computation.1 | async-start | bytes 147456 | tf_op jit(solution)/shard_map/all_to_all | solution.py:20
  27.0 4.7 %all-to-all-done.1.arrived_ref.near_ref = bf16[4,72,128]{2,1,0:T(8,128)(2,1)S(1)} async-done(((bf16[4,72,128]{2,1,0:T(8,128)(2,1)}), bf16[4,72,128]{2,1,0:T(8,128)(2,1)S(1)}, u32[]{:S(2)}, u32[]{:S(2)}) %all-to-all-start.1) | async-done | bytes 73760 | tf_op jit(solution)/shard_map/all_to_all | solution.py:20
  32.3 11.7 %all-to-all-start.2 = ((bf16[4,72,128]{2,1,0:T(8,128)(2,1)}), bf16[4,72,128]{2,1,0:T(8,128)(2,1)S(1)}, u32[]{:S(2)}, u32[]{:S(2)}) async-start(bf16[4,72,128]{2,1,0:T(8,128)(2,1)} %sums.3), calls=%async_computation.2 | async-start | bytes 147456 | tf_op jit(solution)/shard_map/all_to_all | solution.py:20
  44.3 12.8 %all-to-all-done.2.far_ref = bf16[4,72,128]{2,1,0:T(8,128)(2,1)S(1)} async-done(((bf16[4,72,128]{2,1,0:T(8,128)(2,1)}), bf16[4,72,128]{2,1,0:T(8,128)(2,1)S(1)}, u32[]{:S(2)}, u32[]{:S(2)}) %all-to-all-start.2) | async-done | bytes 73760 | tf_op jit(solution)/shard_map/all_to_all | solution.py:20
  57.1 1.4 enter.1
  58.5 5.0 %all-to-all-start.3 = ((bf16[16,64,128]{2,1,0:T(8,128)(2,1)}), bf16[16,64,128]{2,1,0:T(8,128)(2,1)S(1)}, u32[]{:S(2)}, u32[]{:S(2)}) async-start(bf16[16,64,128]{2,1,0:T(8,128)(2,1)} %enter.1), calls=%async_computation.3 | async-start | bytes 524288 | tf_op jit(solution)/shard_map/all_to_all | solution.py:20
  63.7 1.5 inside.1
  65.1 4.8 %all-to-all-done.3 = bf16[16,64,128]{2,1,0:T(8,128)(2,1)S(1)} async-done(((bf16[16,64,128]{2,1,0:T(8,128)(2,1)}), bf16[16,64,128]{2,1,0:T(8,128)(2,1)S(1)}, u32[]{:S(2)}, u32[]{:S(2)}) %all-to-all-start.3) | async-done | bytes 262176 | tf_op jit(solution)/shard_map/all_to_all | solution.py:20
  69.9 2.8 %outgoing.1 = (f32[128,1024]{1,0:T(8,128)S(1)}, bf16[2560,128]{1,0:T(8,128)(2,1)}) custom-call(s32[8]{0:T(128)S(1)} %fusion.8.own_ref, bf16[1024,128]{1,0:T(8,128)(2,1)S(1)} %bitcast.46, bf16[128,1024]{1,0:T(8,128)(2,1)S(1)} %get-tuple-element.15.queries_ref, f32[128,1024]{1,0:T(8,128)S(1)} %get-tuple-element.16.inside_ref, ...), custom_call_target="tpu_custom_call" | custom-call | flops 120000000 | bytes 3000000 | tf_op jit(solution)/shard_map/outgoing/pallas_call | solution.py:424
  72.7 7.5 %all-to-all-start.4 = ((bf16[64,40,128]{2,1,0:T(8,128)(2,1)}), bf16[64,40,128]{2,1,0:T(8,128)(2,1)}, u32[]{:S(2)}, u32[]{:S(2)}) async-start(bf16[64,40,128]{2,1,0:T(8,128)(2,1)} %bitcast.16), calls=%async_computation.4 | async-start | bytes 1310720 | tf_op jit(solution)/shard_map/all_to_all | solution.py:20
  80.3 2.7 %collective-permute-start.1 = (bf16[3,128,1408]{2,1,0:T(8,128)(2,1)}, bf16[3,128,1408]{2,1,0:T(8,128)(2,1)S(1)}, u32[]{:S(2)}, u32[]{:S(2)}) collective-permute-start(bf16[3,128,1408]{2,1,0:T(8,128)(2,1)} %get-tuple-element.19.refs_1_), channel_id=1, source_target_pairs={{0,12},{4,0},{8,4},{12,8},{1,13},{5,1},{9,5},{13,9},{2,14},{6,2},{... | collective-permute-start | bytes 3244040 | tf_op jit(solution)/shard_map/ppermute | solution.py:316
  82.9 3.2 %collective-permute-start.4 = (bf16[3,128,1408]{2,1,0:T(8,128)(2,1)}, bf16[3,128,1408]{2,1,0:T(8,128)(2,1)S(1)}, u32[]{:S(2)}, u32[]{:S(2)}) collective-permute-start(bf16[3,128,1408]{2,1,0:T(8,128)(2,1)} %get-tuple-element.19.refs_1_), channel_id=1, source_target_pairs={{0,4},{4,8},{8,12},{12,0},{1,5},{5,9},{9,13},{13,1},{2,6},{6,10},{... | collective-permute-start | bytes 3244040 | tf_op jit(solution)/shard_map/ppermute | solution.py:316
  86.1 1.9 collective-permute-start
  88.0 19.3 %collective-permute-done.1.refs_3_ = bf16[3,128,1408]{2,1,0:T(8,128)(2,1)S(1)} collective-permute-done((bf16[3,128,1408]{2,1,0:T(8,128)(2,1)}, bf16[3,128,1408]{2,1,0:T(8,128)(2,1)S(1)}, u32[]{:S(2)}, u32[]{:S(2)}) %collective-permute-start.1) | collective-permute-done | bytes 1081376 | tf_op jit(solution)/shard_map/ppermute | solution.py:316
  107.4 4.6 %collective-permute-start.3 = (bf16[3,64,1408]{2,1,0:T(8,128)(2,1)S(1)}, bf16[3,64,1408]{2,1,0:T(8,128)(2,1)}, u32[]{:S(2)}, u32[]{:S(2)}) collective-permute-start(bf16[3,64,1408]{2,1,0:T(8,128)(2,1)S(1)} %slice.25), channel_id=1, source_target_pairs={{0,12},{4,0},{8,4},{12,8},{1,13},{5,1},{9,5},{13,9},{2,14},{6,2},{... | collective-permute-start | bytes 1622024 | tf_op jit(solution)/shard_map/ppermute | solution.py:316
  112.1 1.9 collective-permute-start.5
  114.0 1.9 collective-permute-start.2
  115.9 2.4 %collective-permute-start.8 = (bf16[3,128,1408]{2,1,0:T(8,128)(2,1)S(1)}, bf16[3,128,1408]{2,1,0:T(8,128)(2,1)}, u32[]{:S(2)}, u32[]{:S(2)}) collective-permute-start(bf16[3,128,1408]{2,1,0:T(8,128)(2,1)S(1)} %collective-permute-done.4.refs_9_), channel_id=1, source_target_pairs={{0,2},{2,0},{1,3},{3,1},{4,6},{6,4},{5,7},{7,5},{8,10},{10,8},{9,1... | collective-permute-start | bytes 3244040 | tf_op jit(solution)/shard_map/ppermute | solution.py:320
  118.3 4.5 %collective-permute-done.3.refs_5_ = bf16[3,64,1408]{2,1,0:T(8,128)(2,1)} collective-permute-done((bf16[3,64,1408]{2,1,0:T(8,128)(2,1)S(1)}, bf16[3,64,1408]{2,1,0:T(8,128)(2,1)}, u32[]{:S(2)}, u32[]{:S(2)}) %collective-permute-start.3) | collective-permute-done | bytes 540704 | tf_op jit(solution)/shard_map/ppermute | solution.py:316
  122.9 1.9 collective-permute-start.6
  124.8 3.6 %collective-permute-done.5.refs_6_ = bf16[3,64,1408]{2,1,0:T(8,128)(2,1)} collective-permute-done((bf16[3,64,1408]{2,1,0:T(8,128)(2,1)S(1)}, bf16[3,64,1408]{2,1,0:T(8,128)(2,1)}, u32[]{:S(2)}, u32[]{:S(2)}) %collective-permute-start.5) | collective-permute-done | bytes 540704 | tf_op jit(solution)/shard_map/ppermute | solution.py:316
  128.4 1.9 collective-permute-start.7
  130.3 1.4 reshape.50.refs_0_
  131.7 0.8 collective-permute-done.7.refs_8_
  132.5 6.7 %experts.1 = bf16[2560,128]{1,0:T(8,128)(2,1)} custom-call(bf16[320,1024]{1,0:T(8,128)(2,1)S(1)} %reshape.50.refs_0_, bf16[3,128,1408]{2,1,0:T(8,128)(2,1)} %get-tuple-element.19.refs_1_, bf16[3,128,1408]{2,1,0:T(8,128)(2,1)} %collective-permute-done.refs_2_, bf16[3,128,1408]{2,1,0:T(8,128)(2,1)S(1)} %collective-permute-done.1.refs_3_, ...), custom_call_target="tpu_custom_call" | custom-call | flops 2768240640 | bytes 8650752 | tf_op jit(solution)/shard_map/experts/pallas_call | solution.py:287
  139.2 15.1 %all-to-all-start.5 = ((bf16[64,40,128]{2,1,0:T(8,128)(2,1)}), bf16[64,40,128]{2,1,0:T(8,128)(2,1)S(1)}, u32[]{:S(2)}, u32[]{:S(2)}) async-start(bf16[64,40,128]{2,1,0:T(8,128)(2,1)} %bitcast.17), calls=%async_computation.5 | async-start | bytes 1310720 | tf_op jit(solution)/shard_map/all_to_all | solution.py:20
  154.9 38.4 %all-to-all-done.5 = bf16[64,40,128]{2,1,0:T(8,128)(2,1)S(1)} async-done(((bf16[64,40,128]{2,1,0:T(8,128)(2,1)}), bf16[64,40,128]{2,1,0:T(8,128)(2,1)S(1)}, u32[]{:S(2)}, u32[]{:S(2)}) %all-to-all-start.5) | async-done | bytes 655392 | tf_op jit(solution)/shard_map/all_to_all | solution.py:20
  193.6 1.9 combine.1
  (55 shorter events, 4.1 us)
Async XLA Ops:
  1.6 13.5 %copy-start.9 = (s32[1,128,2]{1,2,0:T(2,128)S(1)}, s32[1,128,2]{1,2,0:T(2,128)}, u32[]{:S(2)}) copy-start(s32[1,128,2]{1,2,0:T(2,128)} %param.21) | copy-start | bytes 3076
  5.9 16.0 %all-to-all-start = ((bf16[16,72,128]{2,1,0:T(8,128)(2,1)}), bf16[16,72,128]{2,1,0:T(8,128)(2,1)S(1)}, u32[]{:S(2)}, u32[]{:S(2)}) async-start(bf16[16,72,128]{2,1,0:T(8,128)(2,1)} %get-tuple-element.13), calls=%async_computation | async-start | bytes 589824 | tf_op jit(solution)/shard_map/all_to_all | solution.py:20
  22.6 9.0 %all-to-all-start.1 = ((bf16[4,72,128]{2,1,0:T(8,128)(2,1)}), bf16[4,72,128]{2,1,0:T(8,128)(2,1)S(1)}, u32[]{:S(2)}, u32[]{:S(2)}) async-start(bf16[4,72,128]{2,1,0:T(8,128)(2,1)} %sums.2), calls=%async_computation.1 | async-start | bytes 147456 | tf_op jit(solution)/shard_map/all_to_all | solution.py:20
  26.7 36.9 %copy-start = (bf16[1,128,1024]{2,1,0:T(8,128)(2,1)S(1)}, bf16[1,128,1024]{2,1,0:T(8,128)(2,1)}, u32[]{:S(2)}) copy-start(bf16[1,128,1024]{2,1,0:T(8,128)(2,1)} %param.16) | copy-start | bytes 786436
  26.7 36.9 %copy-start.1 = (bf16[1,128,1024]{2,1,0:T(8,128)(2,1)S(1)}, bf16[1,128,1024]{2,1,0:T(8,128)(2,1)}, u32[]{:S(2)}) copy-start(bf16[1,128,1024]{2,1,0:T(8,128)(2,1)} %param.17) | copy-start | bytes 786436
  26.7 36.9 %copy-start.2 = (f32[128,128]{1,0:T(8,128)S(1)}, f32[128,128]{1,0:T(8,128)}, u32[]{:S(2)}) copy-start(f32[128,128]{1,0:T(8,128)} %get-tuple-element.23.sin_ref) | copy-start | bytes 196612
  26.7 36.9 %copy-start.3 = (f32[128,128]{1,0:T(8,128)S(1)}, f32[128,128]{1,0:T(8,128)}, u32[]{:S(2)}) copy-start(f32[128,128]{1,0:T(8,128)} %get-tuple-element.24.cos_ref) | copy-start | bytes 196612
  26.7 36.9 %copy-start.4 = (bf16[1,128,1024]{2,1,0:T(8,128)(2,1)S(1)}, bf16[1,128,1024]{2,1,0:T(8,128)(2,1)}, u32[]{:S(2)}) copy-start(bf16[1,128,1024]{2,1,0:T(8,128)(2,1)} %param.15) | copy-start | bytes 786436
  26.7 36.9 %copy-start.8 = (f32[8,128]{1,0:T(8,128)S(1)}, f32[8,128]{1,0:T(8,128)}, u32[]{:S(2)}) copy-start(f32[8,128]{1,0:T(8,128)} %get-tuple-element.14.total_ref) | copy-start | bytes 12292
  32.3 24.8 %all-to-all-start.2 = ((bf16[4,72,128]{2,1,0:T(8,128)(2,1)}), bf16[4,72,128]{2,1,0:T(8,128)(2,1)S(1)}, u32[]{:S(2)}, u32[]{:S(2)}) async-start(bf16[4,72,128]{2,1,0:T(8,128)(2,1)} %sums.3), calls=%async_computation.2 | async-start | bytes 147456 | tf_op jit(solution)/shard_map/all_to_all | solution.py:20
  58.5 11.4 %copy-start.5 = (bf16[1,128,1024]{2,1,0:T(8,128)(2,1)S(1)}, bf16[1,128,1024]{2,1,0:T(8,128)(2,1)}, u32[]{:S(2)}) copy-start(bf16[1,128,1024]{2,1,0:T(8,128)(2,1)} %param.14) | copy-start | bytes 786436
  58.5 11.4 %copy-start.6 = (f32[1024]{0:T(1024)S(1)}, f32[1024]{0:T(1024)}, u32[]{:S(2)}) copy-start(f32[1024]{0:T(1024)} %param.19) | copy-start | bytes 12292
  58.5 11.4 %copy-start.7 = (f32[1024]{0:T(1024)S(1)}, f32[1024]{0:T(1024)}, u32[]{:S(2)}) copy-start(f32[1024]{0:T(1024)} %param.20) | copy-start | bytes 12292
  58.5 11.4 %all-to-all-start.3 = ((bf16[16,64,128]{2,1,0:T(8,128)(2,1)}), bf16[16,64,128]{2,1,0:T(8,128)(2,1)S(1)}, u32[]{:S(2)}, u32[]{:S(2)}) async-start(bf16[16,64,128]{2,1,0:T(8,128)(2,1)} %enter.1), calls=%async_computation.3 | async-start | bytes 524288 | tf_op jit(solution)/shard_map/all_to_all | solution.py:20
  72.7 57.6 %all-to-all-start.4 = ((bf16[64,40,128]{2,1,0:T(8,128)(2,1)}), bf16[64,40,128]{2,1,0:T(8,128)(2,1)}, u32[]{:S(2)}, u32[]{:S(2)}) async-start(bf16[64,40,128]{2,1,0:T(8,128)(2,1)} %bitcast.16), calls=%async_computation.4 | async-start | bytes 1310720 | tf_op jit(solution)/shard_map/all_to_all | solution.py:20
  80.3 27.1 %collective-permute-start.1 = (bf16[3,128,1408]{2,1,0:T(8,128)(2,1)}, bf16[3,128,1408]{2,1,0:T(8,128)(2,1)S(1)}, u32[]{:S(2)}, u32[]{:S(2)}) collective-permute-start(bf16[3,128,1408]{2,1,0:T(8,128)(2,1)} %get-tuple-element.19.refs_1_), channel_id=1, source_target_pairs={{0,12},{4,0},{8,4},{12,8},{1,13},{5,1},{9,5},{13,9},{2,14},{6,2},{... | collective-permute-start | bytes 3244040 | tf_op jit(solution)/shard_map/ppermute | solution.py:316
  82.9 29.1 %collective-permute-start.4 = (bf16[3,128,1408]{2,1,0:T(8,128)(2,1)}, bf16[3,128,1408]{2,1,0:T(8,128)(2,1)S(1)}, u32[]{:S(2)}, u32[]{:S(2)}) collective-permute-start(bf16[3,128,1408]{2,1,0:T(8,128)(2,1)} %get-tuple-element.19.refs_1_), channel_id=1, source_target_pairs={{0,4},{4,8},{8,12},{12,0},{1,5},{5,9},{9,13},{13,1},{2,6},{6,10},{... | collective-permute-start | bytes 3244040 | tf_op jit(solution)/shard_map/ppermute | solution.py:316
  86.1 45.6 %collective-permute-start = (bf16[3,128,1408]{2,1,0:T(8,128)(2,1)}, bf16[3,128,1408]{2,1,0:T(8,128)(2,1)}, u32[]{:S(2)}, u32[]{:S(2)}) collective-permute-start(bf16[3,128,1408]{2,1,0:T(8,128)(2,1)} %get-tuple-element.19.refs_1_), channel_id=1, source_target_pairs={{0,2},{2,0},{1,3},{3,1},{4,6},{6,4},{5,7},{7,5},{8,10},{10,8},{9,1... | collective-permute-start | bytes 3244040 | tf_op jit(solution)/shard_map/ppermute | solution.py:320
  107.4 15.5 %collective-permute-start.3 = (bf16[3,64,1408]{2,1,0:T(8,128)(2,1)S(1)}, bf16[3,64,1408]{2,1,0:T(8,128)(2,1)}, u32[]{:S(2)}, u32[]{:S(2)}) collective-permute-start(bf16[3,64,1408]{2,1,0:T(8,128)(2,1)S(1)} %slice.25), channel_id=1, source_target_pairs={{0,12},{4,0},{8,4},{12,8},{1,13},{5,1},{9,5},{13,9},{2,14},{6,2},{... | collective-permute-start | bytes 1622024 | tf_op jit(solution)/shard_map/ppermute | solution.py:316
  112.1 16.3 %collective-permute-start.5 = (bf16[3,64,1408]{2,1,0:T(8,128)(2,1)S(1)}, bf16[3,64,1408]{2,1,0:T(8,128)(2,1)}, u32[]{:S(2)}, u32[]{:S(2)}) collective-permute-start(bf16[3,64,1408]{2,1,0:T(8,128)(2,1)S(1)} %slice.26), channel_id=1, source_target_pairs={{0,4},{4,8},{8,12},{12,0},{1,5},{5,9},{9,13},{13,1},{2,6},{6,10},{... | collective-permute-start | bytes 1622024 | tf_op jit(solution)/shard_map/ppermute | solution.py:316
  114.0 18.5 %collective-permute-start.2 = (bf16[3,128,1408]{2,1,0:T(8,128)(2,1)S(1)}, bf16[3,128,1408]{2,1,0:T(8,128)(2,1)}, u32[]{:S(2)}, u32[]{:S(2)}) collective-permute-start(bf16[3,128,1408]{2,1,0:T(8,128)(2,1)S(1)} %collective-permute-done.1.refs_3_), channel_id=1, source_target_pairs={{0,2},{2,0},{1,3},{3,1},{4,6},{6,4},{5,7},{7,5},{8,10},{10,8},{9,1... | collective-permute-start | bytes 3244040 | tf_op jit(solution)/shard_map/ppermute | solution.py:320
  115.9 16.6 %collective-permute-start.8 = (bf16[3,128,1408]{2,1,0:T(8,128)(2,1)S(1)}, bf16[3,128,1408]{2,1,0:T(8,128)(2,1)}, u32[]{:S(2)}, u32[]{:S(2)}) collective-permute-start(bf16[3,128,1408]{2,1,0:T(8,128)(2,1)S(1)} %collective-permute-done.4.refs_9_), channel_id=1, source_target_pairs={{0,2},{2,0},{1,3},{3,1},{4,6},{6,4},{5,7},{7,5},{8,10},{10,8},{9,1... | collective-permute-start | bytes 3244040 | tf_op jit(solution)/shard_map/ppermute | solution.py:320
  122.9 8.8 %collective-permute-start.6 = (bf16[3,64,1408]{2,1,0:T(8,128)(2,1)}, bf16[3,64,1408]{2,1,0:T(8,128)(2,1)}, u32[]{:S(2)}, u32[]{:S(2)}) collective-permute-start(bf16[3,64,1408]{2,1,0:T(8,128)(2,1)} %collective-permute-done.3.refs_5_), channel_id=1, source_target_pairs={{0,2},{2,0},{1,3},{3,1},{4,6},{6,4},{5,7},{7,5},{8,10},{10,8},{9,1... | collective-permute-start | bytes 1622024 | tf_op jit(solution)/shard_map/ppermute | solution.py:320
  128.4 4.2 %collective-permute-start.7 = (bf16[3,64,1408]{2,1,0:T(8,128)(2,1)}, bf16[3,64,1408]{2,1,0:T(8,128)(2,1)}, u32[]{:S(2)}, u32[]{:S(2)}) collective-permute-start(bf16[3,64,1408]{2,1,0:T(8,128)(2,1)} %collective-permute-done.5.refs_6_), channel_id=1, source_target_pairs={{0,2},{2,0},{1,3},{3,1},{4,6},{6,4},{5,7},{7,5},{8,10},{10,8},{9,1... | collective-permute-start | bytes 1622024 | tf_op jit(solution)/shard_map/ppermute | solution.py:320
  139.2 15.3 %copy-start.10 = (f32[1,128,2]{1,2,0:T(2,128)S(1)}, f32[1,128,2]{1,2,0:T(2,128)}, u32[]{:S(2)}) copy-start(f32[1,128,2]{1,2,0:T(2,128)} %param.22) | copy-start | bytes 3076
  139.2 54.1 %all-to-all-start.5 = ((bf16[64,40,128]{2,1,0:T(8,128)(2,1)}), bf16[64,40,128]{2,1,0:T(8,128)(2,1)S(1)}, u32[]{:S(2)}, u32[]{:S(2)}) async-start(bf16[64,40,128]{2,1,0:T(8,128)(2,1)} %bitcast.17), calls=%async_computation.5 | async-start | bytes 1310720 | tf_op jit(solution)/shard_map/all_to_all | solution.py:20

commit v7 on v5

--- a/solution.py
+++ b/solution.py
@@ -45,33 +45,23 @@
     return block * cosine + pltpu.roll(block, block.shape[1] // 2, 1) * sine
 
 
+def tables(start_ref, cos_ref, sin_ref):
+    cosine = start_ref[0:1] * cos_ref[...] - start_ref[1:2] * sin_ref[...]
+    sine = start_ref[1:2] * cos_ref[...] + start_ref[0:1] * sin_ref[...]
+    return cosine, sine * start_ref[2:3]
+
+
 def summary_kernel(
     keys_ref,
     values_ref,
     log_ref,
+    start_ref,
     cos_ref,
     sin_ref,
-    gate_hbm,
-    up_hbm,
-    down_hbm,
     message_ref,
     total_ref,
-    stacked_hbm,
-    shard_ref,
-    in_sems,
-    out_sems,
 ):
-    shards = (gate_hbm, up_hbm, down_hbm)
-    loads = [
-        pltpu.make_async_copy(shard, shard_ref.at[index], in_sems.at[index])
-        for index, shard in enumerate(shards)
-    ]
-    stores = [
-        pltpu.make_async_copy(shard_ref.at[index], stacked_hbm.at[index], out_sems.at[index])
-        for index in range(len(shards))
-    ]
-    for load in loads:
-        load.start()
+    cosine, sine = tables(start_ref, cos_ref, sin_ref)
     heads, count = log_ref.shape
     head_dim = cos_ref.shape[1]
     parts = message_ref.shape[0] // heads
@@ -87,12 +77,8 @@
     trailing = jnp.exp(last - total)
     wide = jnp.broadcast_to(last, (heads, head_dim))
     for head in range(heads):
-        if head == heads // 2:
-            for load, store in zip(loads, stores):
-                load.wait()
-                store.start()
         lanes = slice(head * head_dim, (head + 1) * head_dim)
-        keys = turned(keys_ref[:, lanes].astype(F32), cos_ref[...], sin_ref[...]).astype(BF16)
+        keys = turned(keys_ref[:, lanes].astype(F32), cosine, sine).astype(BF16)
         faded = keys.astype(F32).T * trailing[head : head + 1]
         coarse = faded.astype(BF16)
         fine = (faded - coarse.astype(F32)).astype(BF16)
@@ -102,13 +88,40 @@
         for part in range(parts):
             message_ref[head * parts + part, :rows] = summary[part * rows : (part + 1) * rows]
             message_ref[head * parts + part, rows:] = logs
+
+
+def stack_kernel(gate_hbm, up_hbm, down_hbm, stacked_hbm, shard_ref, in_sems, out_sems):
+    shards = (gate_hbm, up_hbm, down_hbm)
+    loads = [
+        pltpu.make_async_copy(shard, shard_ref.at[index], in_sems.at[index])
+        for index, shard in enumerate(shards)
+    ]
+    stores = [
+        pltpu.make_async_copy(shard_ref.at[index], stacked_hbm.at[index], out_sems.at[index])
+        for index in range(len(shards))
+    ]
+    for load in loads:
+        load.start()
+    for load, store in zip(loads, stores):
+        load.wait()
+        store.start()
     for store in stores:
         store.wait()
 
 
 def inside_kernel(
-    queries_ref, keys_ref, values_ref, total_ref, cos_ref, sin_ref, turned_ref, inside_ref, fade_ref
+    queries_ref,
+    keys_ref,
+    values_ref,
+    total_ref,
+    start_ref,
+    cos_ref,
+    sin_ref,
+    turned_ref,
+    inside_ref,
+    fade_ref,
 ):
+    cosine, sine = tables(start_ref, cos_ref, sin_ref)
     heads, count = total_ref.shape
     head_dim = cos_ref.shape[1]
     row = lax.broadcasted_iota(jnp.int32, (count, count), 0)
@@ -117,10 +130,10 @@
     fade = jnp.zeros((count, count), F32)
     for head in range(heads):
         lanes = slice(head * head_dim, (head + 1) * head_dim)
-        queries = turned(queries_ref[:, lanes].astype(F32), cos_ref[...], sin_ref[...])
+        queries = turned(queries_ref[:, lanes].astype(F32), cosine, sine)
         queries = (queries * head_dim ** (-0.5)).astype(BF16)
         turned_ref[:, lanes] = queries
-        keys = turned(keys_ref[:, lanes].astype(F32), cos_ref[...], sin_ref[...]).astype(BF16)
+        keys = turned(keys_ref[:, lanes].astype(F32), cosine, sine).astype(BF16)
         scores = lax.dot_general(
             queries, keys, (((1,), (1,)), ((), ())), preferred_element_type=F32
         )
@@ -218,8 +231,10 @@
 
 
 def expert_kernel(*refs):
-    arrived_ref, pieces, out_ref = refs[0], refs[1:-5], refs[-5]
-    weights_ref, hidden_ref, packed_ref, sems = refs[-4:]
+    incoming_hbm, pieces, out_ref = refs[0], refs[1:-8], refs[-8]
+    weights_ref, hidden_ref, packed_ref, incoming_ref, arrived_ref, sems, sem = refs[-7:]
+    incoming = pltpu.make_async_copy(incoming_hbm, incoming_ref, sem)
+    incoming.start()
     width = weights_ref.shape[2]
     copies = [[] for _ in range(3)]
     for index in range(3):
@@ -234,6 +249,14 @@
             copy.start()
             copies[index].append(copy)
             start += size
+    rows, lanes = arrived_ref.shape[0], packed_ref.shape[1]
+    chunks = packed_ref.shape[0] // rows
+    incoming.wait()
+    packed_ref[...] = incoming_ref[...].astype(F32)
+    for chunk in range(chunks):
+        arrived_ref[:, chunk * lanes : (chunk + 1) * lanes] = packed_ref[
+            pl.ds(chunk, rows, stride=chunks), :
+        ].astype(BF16)
     for copy in copies[0]:
         copy.wait()
     for start in range(0, width, TILE):
@@ -246,8 +269,6 @@
         hidden_ref[:, columns] = (gate / (1.0 + jnp.exp(-gate)) * up).astype(BF16)
     for copy in copies[2]:
         copy.wait()
-    rows, lanes = arrived_ref.shape[0], packed_ref.shape[1]
-    chunks = packed_ref.shape[0] // rows
     for chunk in range(0, chunks, 2):
         pair = lax.dot_general(
             hidden_ref[...],
@@ -271,23 +292,26 @@
 
 
 def run_experts(arrived, pieces):
-    rows, model_width = arrived.shape
+    model_width = sum(piece.shape[1] for piece in pieces)
+    rows = arrived.size // model_width
     width = pieces[0].shape[2]
     anywhere = pl.BlockSpec(memory_space=pl.ANY)
     return pl.pallas_call(
         expert_kernel,
         name="experts",
         out_shape=shape((rows * model_width // LANES, LANES), BF16),
-        in_specs=[pl.BlockSpec(memory_space=pltpu.VMEM)] + [anywhere] * len(pieces),
+        in_specs=[anywhere] * (1 + len(pieces)),
         out_specs=pl.BlockSpec(memory_space=pltpu.VMEM),
         scratch_shapes=[
             pltpu.VMEM((3, model_width, width), BF16),
             pltpu.VMEM((rows, width), BF16),
             pltpu.VMEM((rows * model_width // LANES, LANES), F32),
+            pltpu.VMEM((rows * model_width // LANES, LANES), BF16),
+            pltpu.VMEM((rows, model_width), BF16),
             pltpu.SemaphoreType.DMA((3, len(pieces))),
+            pltpu.SemaphoreType.DMA,
         ],
         cost_estimate=cost(6 * rows * model_width * width, 6 * model_width * width),
-        compiler_params=vmem(20),
     )(arrived, *pieces)
 
 
@@ -331,33 +355,35 @@
     message = (plane, part_rows + LOG_ROWS, head_dim)
 
     half = head_dim // 2
-    inverse = (10000.0 ** (-np.arange(half) / half)).astype(np.float32)
+    inverse = np.tile(10000.0 ** (-np.arange(half) / half), 2)
     sign = np.repeat(np.array([-1.0, 1.0], np.float32), half)
+    within = np.arange(tok_rows)[:, None] * inverse[None, :]
     block_index = lax.axis_index(CTX) * lax.axis_size(EXP) + lax.axis_index(EXP)
-    position = block_index * tok_rows + jnp.arange(tok_rows, dtype=jnp.int32)
-    angles = position.astype(F32)[:, None] * np.tile(inverse, 2)[None, :]
-    cosine, sine = jnp.cos(angles), jnp.sin(angles) * sign
-
-    shards = (3,) + w_gate.shape[1:]
-    any_space, in_vmem = pl.BlockSpec(memory_space=pl.ANY), pl.BlockSpec(memory_space=pltpu.VMEM)
-    out_message, total, stacked = pl.pallas_call(
+    start = (block_index * tok_rows).astype(F32) * inverse.astype(np.float32)[None, :]
+    start = jnp.concatenate([jnp.cos(start), jnp.sin(start), sign[None, :]])
+    turn = (start, np.cos(within).astype(np.float32), np.sin(within).astype(np.float32))
+
+    out_message, total = pl.pallas_call(
         summary_kernel,
         name="summary",
-        out_shape=(
-            shape(message, BF16),
-            shape((head_count, tok_rows), F32),
-            shape(shards, BF16),
-        ),
-        in_specs=[in_vmem] * 5 + [any_space] * 3,
-        out_specs=(in_vmem, in_vmem, any_space),
+        out_shape=(shape(message, BF16), shape((head_count, tok_rows), F32)),
+        cost_estimate=cost(70000000, 1200000),
+    )(keys[0], values[0], log_decay[0].T, *turn)
+    summaries = exchange(out_message, PLANE)
+    shards = (3,) + w_gate.shape[1:]
+    stacked = pl.pallas_call(
+        stack_kernel,
+        name="stack",
+        out_shape=shape(shards, BF16),
+        in_specs=[pl.BlockSpec(memory_space=pl.ANY)] * 3,
+        out_specs=pl.BlockSpec(memory_space=pl.ANY),
         scratch_shapes=[
             pltpu.VMEM(shards, BF16),
             pltpu.SemaphoreType.DMA((3,)),
             pltpu.SemaphoreType.DMA((3,)),
         ],
-        cost_estimate=cost(70000000, 3200000),
-    )(keys[0], values[0], log_decay[0].T, cosine, sine, w_gate[0], w_up[0], w_down[0])
-    summaries = exchange(out_message, PLANE)
+        cost_estimate=cost(0, 2200000),
+    )(w_gate[0], w_up[0], w_down[0])
     after, before = along_x(stacked, 1), along_x(stacked, -1)
     turned_queries, inside, fade = pl.pallas_call(
         inside_kernel,
@@ -365,7 +391,7 @@
         out_shape=(shape(wide, BF16), shape(wide, F32), shape((tok_rows, tok_rows), F32)),
         cost_estimate=cost(70000000, 2200000),
         compiler_params=vmem(8),
-    )(queries[0], keys[0], values[0], total, cosine, sine)
+    )(queries[0], keys[0], values[0], total, *turn)
     sums = pl.pallas_call(
         plane_sum_kernel,
         name="plane_sum",
@@ -428,7 +454,7 @@
         placing,
     )
     packed = (expert_count, capacity * model_width // LANES, LANES)
-    arrived = exchange(outgoing.reshape(packed), OWNERS).reshape(slot_count, model_width)
+    arrived = exchange(outgoing.reshape(packed), OWNERS).reshape(flat)
     cut = stacked.shape[1] // 2
     far = [along_x(after[:, :cut], 1), along_x(before[:, cut:], -1)]
     far_other = [swapped(piece) for piece in far]

time: 195 us -> 200 us (1.026)
  Pallas kernels: 18.3 us -> 21.1 us
    unnamed x24 -> x44, local copies, waits for them, and re-layouts: 0.28 us -> 2.88 us
    pallas_call x1, Pallas kernels: 6.63 us -> 8.77 us  [run_experts(): pl.pallas_call(expert_kernel, name='experts', out_shape=shape((rows * mod...]
    pallas_call x0 -> x1, Pallas kernels: none -> 2.05 us  [body(): pl.pallas_call(stack_kernel, name='stack', out_shape=shape(shards, BF16),...]
  transfers between devices with their start and end apart: 13 -> 13, of which waited for: 7 -> 7; matrix products, arithmetic and copies ran while one was open for 2% -> 1% of each run, Pallas kernels for 1% -> 2%
where the time goes in v7:
time: 200 us; the launch traced here: 199 us
  waiting for transfers between devices  90.5 us (45%)
  starting transfers between devices  64.2 us (32%)
  Pallas kernels  21.1 us (11%)
  blocking collectives  15.9 us (8%)
  local copies, waits for them, and re-layouts  4.22 us (2%)
  other arithmetic  2.93 us (1%)
    all_to_all x4, waiting for transfers between devices, exchange(): return lax.all_to_all(blocks, axes, split_axis=0, concat_axis=0, tiled=True)  61.4 us
    all_to_all x4, starting transfers between devices, exchange(): return lax.all_to_all(blocks, axes, split_axis=0, concat_axis=0, tiled=True)  41.7 us
    ppermute x4, waiting for transfers between devices, along_x(): lax.ppermute(piece, 'x', [(i, (i - step) % size) for i in range(size)])  27.2 us
    all_to_all x1, blocking collectives, exchange(): return lax.all_to_all(blocks, axes, split_axis=0, concat_axis=0, tiled=True)  15.9 us
    ppermute x4, starting transfers between devices, along_x(): lax.ppermute(piece, 'x', [(i, (i - step) % size) for i in range(size)])  12.4 us
    ppermute x5, starting transfers between devices, swapped(): return lax.ppermute(piece, 'core', [(0, 1), (1, 0)])  10.1 us
    pallas_call x1, Pallas kernels, run_experts(): pl.pallas_call(expert_kernel, name='experts', out_shape=shape((rows * mod...  8.77 us
  transfers between devices with their start and end apart: 13, of which 7 were waited for; matrix products, arithmetic and copies ran while one was open for 1% of the time, Pallas kernels for 2%

profile of v7, /device:TPU:8, one launch (start us, length us, event | category | flops | bytes accessed | tf_op | source)
XLA Modules:
  0.0 199.2 jit_solution(12731405050228165607)
XLA Ops:
  0.7 1.2 pad_maximum_fusion.start_ref
  1.9 2.4 %summary.1 = (bf16[16,72,128]{2,1,0:T(8,128)(2,1)}, f32[8,128]{1,0:T(8,128)}) custom-call(bf16[128,1024]{1,0:T(8,128)(2,1)} %bitcast.42, bf16[128,1024]{1,0:T(8,128)(2,1)} %bitcast.44, f32[8,128]{1,0:T(8,128)} %bitcast.57, f32[3,128]{1,0:T(4,128)} %pad_maximum_fusion.start_ref, f32[128,128]{1,0:T(8,128)} %constant.82.clone.cos_ref, ...), custom_call_target="tpu_custom_call" | custom-call | flops 70000000 | bytes 1200000 | tf_op jit(solution)/shard_map/summary/pallas_call | solution.py:366
  4.4 15.9 %all_to_all.25.arrived_ref = bf16[16,72,128]{2,1,0:T(8,128)(2,1)S(1)} all-to-all(bf16[16,72,128]{2,1,0:T(8,128)(2,1)} %get-tuple-element.12), channel_id=1, replica_groups=mesh['z'=16,'ylo'=2,'x'=4,'core'=2,'yhi'=2] {'ylo','x','core'}, dimensions={0} | all-to-all | bytes 589824 | tf_op jit(solution)/shard_map/all_to_all | solution.py:20
  20.3 0.8 plane_sum.1
  21.1 11.8 %all-to-all-start.1 = ((bf16[16,72,128]{2,1,0:T(8,128)(2,1)}), bf16[16,72,128]{2,1,0:T(8,128)(2,1)S(1)}, u32[]{:S(2)}, u32[]{:S(2)}) async-start(bf16[16,72,128]{2,1,0:T(8,128)(2,1)} %plane_sum.1), calls=%async_computation.1 | async-start | bytes 589824 | tf_op jit(solution)/shard_map/all_to_all | solution.py:20
  34.6 18.3 %all-to-all-done.1.planes_ref = bf16[16,72,128]{2,1,0:T(8,128)(2,1)S(1)} async-done(((bf16[16,72,128]{2,1,0:T(8,128)(2,1)}), bf16[16,72,128]{2,1,0:T(8,128)(2,1)S(1)}, u32[]{:S(2)}, u32[]{:S(2)}) %all-to-all-start.1) | async-done | bytes 294944 | tf_op jit(solution)/shard_map/all_to_all | solution.py:20
  52.8 0.9 enter.1
  53.7 4.5 %all-to-all-start.2 = ((bf16[16,64,128]{2,1,0:T(8,128)(2,1)}), bf16[16,64,128]{2,1,0:T(8,128)(2,1)S(1)}, u32[]{:S(2)}, u32[]{:S(2)}) async-start(bf16[16,64,128]{2,1,0:T(8,128)(2,1)} %enter.1), calls=%async_computation.2 | async-start | bytes 524288 | tf_op jit(solution)/shard_map/all_to_all | solution.py:20
  58.5 1.5 inside.1
  59.9 4.8 %all-to-all-done.2 = bf16[16,64,128]{2,1,0:T(8,128)(2,1)S(1)} async-done(((bf16[16,64,128]{2,1,0:T(8,128)(2,1)}), bf16[16,64,128]{2,1,0:T(8,128)(2,1)S(1)}, u32[]{:S(2)}, u32[]{:S(2)}) %all-to-all-start.2) | async-done | bytes 262176 | tf_op jit(solution)/shard_map/all_to_all | solution.py:20
  64.7 2.8 %outgoing.1 = (f32[128,1024]{1,0:T(8,128)S(1)}, bf16[2560,128]{1,0:T(8,128)(2,1)}) custom-call(s32[8]{0:T(128)S(1)} %fusion.7.own_ref, bf16[1024,128]{1,0:T(8,128)(2,1)S(1)} %bitcast.46, bf16[128,1024]{1,0:T(8,128)(2,1)S(1)} %get-tuple-element.14.queries_ref, f32[128,1024]{1,0:T(8,128)S(1)} %get-tuple-element.15.inside_ref, ...), custom_call_target="tpu_custom_call" | custom-call | flops 120000000 | bytes 3000000 | tf_op jit(solution)/shard_map/outgoing/pallas_call | solution.py:433
  67.5 10.3 %all-to-all-start.3 = ((bf16[64,40,128]{2,1,0:T(8,128)(2,1)}), bf16[64,40,128]{2,1,0:T(8,128)(2,1)S(1)}, u32[]{:S(2)}, u32[]{:S(2)}) async-start(bf16[64,40,128]{2,1,0:T(8,128)(2,1)} %bitcast.12), calls=%async_computation.3 | async-start | bytes 1310720 | tf_op jit(solution)/shard_map/all_to_all | solution.py:20
  77.8 2.1 %stack.1.refs_1_ = bf16[3,128,1408]{2,1,0:T(8,128)(2,1)} custom-call(bf16[128,1408]{1,0:T(8,128)(2,1)} %bitcast.54, bf16[128,1408]{1,0:T(8,128)(2,1)} %bitcast.55, bf16[128,1408]{1,0:T(8,128)(2,1)} %bitcast.56), custom_call_target="tpu_custom_call" | custom-call | bytes 2200000 | tf_op jit(solution)/shard_map/stack/pallas_call | solution.py:374
  79.8 2.7 %collective-permute-start.1 = (bf16[3,128,1408]{2,1,0:T(8,128)(2,1)}, bf16[3,128,1408]{2,1,0:T(8,128)(2,1)S(1)}, u32[]{:S(2)}, u32[]{:S(2)}) collective-permute-start(bf16[3,128,1408]{2,1,0:T(8,128)(2,1)} %stack.1.refs_1_), channel_id=1, source_target_pairs={{0,12},{4,0},{8,4},{12,8},{1,13},{5,1},{9,5},{13,9},{2,14},{6,2},{... | collective-permute-start | bytes 3244040 | tf_op jit(solution)/shard_map/ppermute | solution.py:320
  82.5 3.2 %collective-permute-start.4 = (bf16[3,128,1408]{2,1,0:T(8,128)(2,1)}, bf16[3,128,1408]{2,1,0:T(8,128)(2,1)S(1)}, u32[]{:S(2)}, u32[]{:S(2)}) collective-permute-start(bf16[3,128,1408]{2,1,0:T(8,128)(2,1)} %stack.1.refs_1_), channel_id=1, source_target_pairs={{0,4},{4,8},{8,12},{12,0},{1,5},{5,9},{9,13},{13,1},{2,6},{6,10},{... | collective-permute-start | bytes 3244040 | tf_op jit(solution)/shard_map/ppermute | solution.py:320
  85.7 1.9 collective-permute-start
  87.6 19.3 %collective-permute-done.1.refs_3_ = bf16[3,128,1408]{2,1,0:T(8,128)(2,1)S(1)} collective-permute-done((bf16[3,128,1408]{2,1,0:T(8,128)(2,1)}, bf16[3,128,1408]{2,1,0:T(8,128)(2,1)S(1)}, u32[]{:S(2)}, u32[]{:S(2)}) %collective-permute-start.1) | collective-permute-done | bytes 1081376 | tf_op jit(solution)/shard_map/ppermute | solution.py:320
  107.0 4.6 %collective-permute-start.3 = (bf16[3,64,1408]{2,1,0:T(8,128)(2,1)S(1)}, bf16[3,64,1408]{2,1,0:T(8,128)(2,1)S(1)}, u32[]{:S(2)}, u32[]{:S(2)}) collective-permute-start(bf16[3,64,1408]{2,1,0:T(8,128)(2,1)S(1)} %slice.25), channel_id=1, source_target_pairs={{0,12},{4,0},{8,4},{12,8},{1,13},{5,1},{9,5},{13,9},{2,14},{6,2},{... | collective-permute-start | bytes 1622024 | tf_op jit(solution)/shard_map/ppermute | solution.py:320
  111.7 1.9 collective-permute-start.5
  113.6 1.9 collective-permute-start.2
  115.5 2.4 %collective-permute-start.8 = (bf16[3,128,1408]{2,1,0:T(8,128)(2,1)S(1)}, bf16[3,128,1408]{2,1,0:T(8,128)(2,1)}, u32[]{:S(2)}, u32[]{:S(2)}) collective-permute-start(bf16[3,128,1408]{2,1,0:T(8,128)(2,1)S(1)} %collective-permute-done.4.refs_9_), channel_id=1, source_target_pairs={{0,2},{2,0},{1,3},{3,1},{4,6},{6,4},{5,7},{7,5},{8,10},{10,8},{9,1... | collective-permute-start | bytes 3244040 | tf_op jit(solution)/shard_map/ppermute | solution.py:324
  117.9 4.4 %collective-permute-done.3.refs_5_ = bf16[3,64,1408]{2,1,0:T(8,128)(2,1)S(1)} collective-permute-done((bf16[3,64,1408]{2,1,0:T(8,128)(2,1)S(1)}, bf16[3,64,1408]{2,1,0:T(8,128)(2,1)S(1)}, u32[]{:S(2)}, u32[]{:S(2)}) %collective-permute-start.3) | collective-permute-done | bytes 540704 | tf_op jit(solution)/shard_map/ppermute | solution.py:320
  122.3 1.9 collective-permute-start.6
  124.3 3.5 %collective-permute-done.5.refs_6_ = bf16[3,64,1408]{2,1,0:T(8,128)(2,1)S(1)} collective-permute-done((bf16[3,64,1408]{2,1,0:T(8,128)(2,1)S(1)}, bf16[3,64,1408]{2,1,0:T(8,128)(2,1)S(1)}, u32[]{:S(2)}, u32[]{:S(2)}) %collective-permute-start.5) | collective-permute-done | bytes 540704 | tf_op jit(solution)/shard_map/ppermute | solution.py:320
  127.7 1.9 collective-permute-start.7
  129.7 1.9 collective-permute-done.7.refs_8_
  132.4 1.0 copy-done.16
  133.4 0.8 copy-done.10
  134.2 8.8 %experts.1 = bf16[2560,128]{1,0:T(8,128)(2,1)} custom-call(bf16[2560,128]{1,0:T(8,128)(2,1)} %bitcast.52, bf16[3,128,1408]{2,1,0:T(8,128)(2,1)} %stack.1.refs_1_, bf16[3,128,1408]{2,1,0:T(8,128)(2,1)} %copy-done.15, bf16[3,128,1408]{2,1,0:T(8,128)(2,1)} %copy-done.11, bf16[3,128,1408]{2,1,0:T(8,128)(2,1)} %copy-done.16, bf16[3,64,1408]{2,1,0:T(8,128)(2,1)} %copy-done.17, ...), custom_call_target="tpu_custom_call" | custom-call | flops 2768240640 | bytes 8650752 | tf_op jit(solution)/shard_map/experts/pallas_call | solution.py:299
  143.0 15.1 %all-to-all-start.4 = ((bf16[64,40,128]{2,1,0:T(8,128)(2,1)}), bf16[64,40,128]{2,1,0:T(8,128)(2,1)S(1)}, u32[]{:S(2)}, u32[]{:S(2)}) async-start(bf16[64,40,128]{2,1,0:T(8,128)(2,1)} %bitcast.53), calls=%async_computation.4 | async-start | bytes 1310720 | tf_op jit(solution)/shard_map/all_to_all | solution.py:20
  158.6 38.4 %all-to-all-done.4 = bf16[64,40,128]{2,1,0:T(8,128)(2,1)S(1)} async-done(((bf16[64,40,128]{2,1,0:T(8,128)(2,1)}), bf16[64,40,128]{2,1,0:T(8,128)(2,1)S(1)}, u32[]{:S(2)}, u32[]{:S(2)}) %all-to-all-start.4) | async-done | bytes 655392 | tf_op jit(solution)/shard_map/all_to_all | solution.py:20
  197.3 1.9 combine.1
  (70 shorter events, 4.1 us)
Async XLA Ops:
  1.9 31.0 %copy-start.13 = (s32[1,128,2]{1,2,0:T(2,128)S(1)}, s32[1,128,2]{1,2,0:T(2,128)}, u32[]{:S(2)}) copy-start(s32[1,128,2]{1,2,0:T(2,128)} %param.23) | copy-start | bytes 3076
  21.1 31.7 %all-to-all-start.1 = ((bf16[16,72,128]{2,1,0:T(8,128)(2,1)}), bf16[16,72,128]{2,1,0:T(8,128)(2,1)S(1)}, u32[]{:S(2)}, u32[]{:S(2)}) async-start(bf16[16,72,128]{2,1,0:T(8,128)(2,1)} %plane_sum.1), calls=%async_computation.1 | async-start | bytes 589824 | tf_op jit(solution)/shard_map/all_to_all | solution.py:20
  33.4 25.0 %copy-start = (bf16[1,128,1024]{2,1,0:T(8,128)(2,1)S(1)}, bf16[1,128,1024]{2,1,0:T(8,128)(2,1)}, u32[]{:S(2)}) copy-start(bf16[1,128,1024]{2,1,0:T(8,128)(2,1)} %param.18) | copy-start | bytes 786436
  33.4 25.0 %copy-start.1 = (bf16[1,128,1024]{2,1,0:T(8,128)(2,1)S(1)}, bf16[1,128,1024]{2,1,0:T(8,128)(2,1)}, u32[]{:S(2)}) copy-start(bf16[1,128,1024]{2,1,0:T(8,128)(2,1)} %param.19) | copy-start | bytes 786436
  33.4 25.0 %copy-start.2 = (f32[128,128]{1,0:T(8,128)S(1)}, f32[128,128]{1,0:T(8,128)}, u32[]{:S(2)}) copy-start(f32[128,128]{1,0:T(8,128)} %constant.82.clone.cos_ref) | copy-start | bytes 196612
  33.4 25.0 %copy-start.3 = (f32[128,128]{1,0:T(8,128)S(1)}, f32[128,128]{1,0:T(8,128)}, u32[]{:S(2)}) copy-start(f32[128,128]{1,0:T(8,128)} %constant.83.clone.sin_ref) | copy-start | bytes 196612
  33.4 25.0 %copy-start.4 = (bf16[1,128,1024]{2,1,0:T(8,128)(2,1)S(1)}, bf16[1,128,1024]{2,1,0:T(8,128)(2,1)}, u32[]{:S(2)}) copy-start(bf16[1,128,1024]{2,1,0:T(8,128)(2,1)} %param.17) | copy-start | bytes 786436
  33.4 25.0 %copy-start.6 = (f32[3,128]{1,0:T(4,128)S(1)}, f32[3,128]{1,0:T(4,128)}, u32[]{:S(2)}) copy-start(f32[3,128]{1,0:T(4,128)} %pad_maximum_fusion.start_ref) | copy-start | bytes 4612
  33.4 25.0 %copy-start.9 = (f32[8,128]{1,0:T(8,128)S(1)}, f32[8,128]{1,0:T(8,128)}, u32[]{:S(2)}) copy-start(f32[8,128]{1,0:T(8,128)} %get-tuple-element.13.total_ref) | copy-start | bytes 12292
  53.7 11.0 %copy-start.5 = (bf16[1,128,1024]{2,1,0:T(8,128)(2,1)S(1)}, bf16[1,128,1024]{2,1,0:T(8,128)(2,1)}, u32[]{:S(2)}) copy-start(bf16[1,128,1024]{2,1,0:T(8,128)(2,1)} %param.16) | copy-start | bytes 786436
  53.7 11.0 %copy-start.7 = (f32[1024]{0:T(1024)S(1)}, f32[1024]{0:T(1024)}, u32[]{:S(2)}) copy-start(f32[1024]{0:T(1024)} %param.21) | copy-start | bytes 12292
  53.7 11.0 %copy-start.8 = (f32[1024]{0:T(1024)S(1)}, f32[1024]{0:T(1024)}, u32[]{:S(2)}) copy-start(f32[1024]{0:T(1024)} %param.22) | copy-start | bytes 12292
  53.7 11.0 %all-to-all-start.2 = ((bf16[16,64,128]{2,1,0:T(8,128)(2,1)}), bf16[16,64,128]{2,1,0:T(8,128)(2,1)S(1)}, u32[]{:S(2)}, u32[]{:S(2)}) async-start(bf16[16,64,128]{2,1,0:T(8,128)(2,1)} %enter.1), calls=%async_computation.2 | async-start | bytes 524288 | tf_op jit(solution)/shard_map/all_to_all | solution.py:20
  67.5 65.9 %all-to-all-start.3 = ((bf16[64,40,128]{2,1,0:T(8,128)(2,1)}), bf16[64,40,128]{2,1,0:T(8,128)(2,1)S(1)}, u32[]{:S(2)}, u32[]{:S(2)}) async-start(bf16[64,40,128]{2,1,0:T(8,128)(2,1)} %bitcast.12), calls=%async_computation.3 | async-start | bytes 1310720 | tf_op jit(solution)/shard_map/all_to_all | solution.py:20
  79.8 27.1 %collective-permute-start.1 = (bf16[3,128,1408]{2,1,0:T(8,128)(2,1)}, bf16[3,128,1408]{2,1,0:T(8,128)(2,1)S(1)}, u32[]{:S(2)}, u32[]{:S(2)}) collective-permute-start(bf16[3,128,1408]{2,1,0:T(8,128)(2,1)} %stack.1.refs_1_), channel_id=1, source_target_pairs={{0,12},{4,0},{8,4},{12,8},{1,13},{5,1},{9,5},{13,9},{2,14},{6,2},{... | collective-permute-start | bytes 3244040 | tf_op jit(solution)/shard_map/ppermute | solution.py:320
  82.5 29.1 %collective-permute-start.4 = (bf16[3,128,1408]{2,1,0:T(8,128)(2,1)}, bf16[3,128,1408]{2,1,0:T(8,128)(2,1)S(1)}, u32[]{:S(2)}, u32[]{:S(2)}) collective-permute-start(bf16[3,128,1408]{2,1,0:T(8,128)(2,1)} %stack.1.refs_1_), channel_id=1, source_target_pairs={{0,4},{4,8},{8,12},{12,0},{1,5},{5,9},{9,13},{13,1},{2,6},{6,10},{... | collective-permute-start | bytes 3244040 | tf_op jit(solution)/shard_map/ppermute | solution.py:320
  85.7 44.0 %collective-permute-start = (bf16[3,128,1408]{2,1,0:T(8,128)(2,1)}, bf16[3,128,1408]{2,1,0:T(8,128)(2,1)S(1)}, u32[]{:S(2)}, u32[]{:S(2)}) collective-permute-start(bf16[3,128,1408]{2,1,0:T(8,128)(2,1)} %stack.1.refs_1_), channel_id=1, source_target_pairs={{0,2},{2,0},{1,3},{3,1},{4,6},{6,4},{5,7},{7,5},{8,10},{10,8},{9,1... | collective-permute-start | bytes 3244040 | tf_op jit(solution)/shard_map/ppermute | solution.py:324
  106.9 6.7 %copy-start.11 = (bf16[3,128,1408]{2,1,0:T(8,128)(2,1)}, bf16[3,128,1408]{2,1,0:T(8,128)(2,1)S(1)}, u32[]{:S(2)}) copy-start(bf16[3,128,1408]{2,1,0:T(8,128)(2,1)S(1)} %collective-permute-done.1.refs_3_) | copy-start | bytes 3244036
  107.0 15.4 %collective-permute-start.3 = (bf16[3,64,1408]{2,1,0:T(8,128)(2,1)S(1)}, bf16[3,64,1408]{2,1,0:T(8,128)(2,1)S(1)}, u32[]{:S(2)}, u32[]{:S(2)}) collective-permute-start(bf16[3,64,1408]{2,1,0:T(8,128)(2,1)S(1)} %slice.25), channel_id=1, source_target_pairs={{0,12},{4,0},{8,4},{12,8},{1,13},{5,1},{9,5},{13,9},{2,14},{6,2},{... | collective-permute-start | bytes 1622024 | tf_op jit(solution)/shard_map/ppermute | solution.py:320
  111.6 21.8 %copy-start.12 = (bf16[3,128,1408]{2,1,0:T(8,128)(2,1)}, bf16[3,128,1408]{2,1,0:T(8,128)(2,1)S(1)}, u32[]{:S(2)}) copy-start(bf16[3,128,1408]{2,1,0:T(8,128)(2,1)S(1)} %collective-permute-done.4.refs_9_) | copy-start | bytes 3244036
  111.7 16.1 %collective-permute-start.5 = (bf16[3,64,1408]{2,1,0:T(8,128)(2,1)S(1)}, bf16[3,64,1408]{2,1,0:T(8,128)(2,1)S(1)}, u32[]{:S(2)}, u32[]{:S(2)}) collective-permute-start(bf16[3,64,1408]{2,1,0:T(8,128)(2,1)S(1)} %slice.26), channel_id=1, source_target_pairs={{0,4},{4,8},{8,12},{12,0},{1,5},{5,9},{9,13},{13,1},{2,6},{6,10},{... | collective-permute-start | bytes 1622024 | tf_op jit(solution)/shard_map/ppermute | solution.py:320
  113.6 18.0 %collective-permute-start.2 = (bf16[3,128,1408]{2,1,0:T(8,128)(2,1)S(1)}, bf16[3,128,1408]{2,1,0:T(8,128)(2,1)S(1)}, u32[]{:S(2)}, u32[]{:S(2)}) collective-permute-start(bf16[3,128,1408]{2,1,0:T(8,128)(2,1)S(1)} %collective-permute-done.1.refs_3_), channel_id=1, source_target_pairs={{0,2},{2,0},{1,3},{3,1},{4,6},{6,4},{5,7},{7,5},{8,10},{10,8},{9,1... | collective-permute-start | bytes 3244040 | tf_op jit(solution)/shard_map/ppermute | solution.py:324
  115.5 17.8 %collective-permute-start.8 = (bf16[3,128,1408]{2,1,0:T(8,128)(2,1)S(1)}, bf16[3,128,1408]{2,1,0:T(8,128)(2,1)}, u32[]{:S(2)}, u32[]{:S(2)}) collective-permute-start(bf16[3,128,1408]{2,1,0:T(8,128)(2,1)S(1)} %collective-permute-done.4.refs_9_), channel_id=1, source_target_pairs={{0,2},{2,0},{1,3},{3,1},{4,6},{6,4},{5,7},{7,5},{8,10},{10,8},{9,1... | collective-permute-start | bytes 3244040 | tf_op jit(solution)/shard_map/ppermute | solution.py:324
  122.3 9.2 %copy-start.17 = (bf16[3,64,1408]{2,1,0:T(8,128)(2,1)}, bf16[3,64,1408]{2,1,0:T(8,128)(2,1)S(1)}, u32[]{:S(2)}) copy-start(bf16[3,64,1408]{2,1,0:T(8,128)(2,1)S(1)} %collective-permute-done.3.refs_5_) | copy-start | bytes 1622020
  122.3 7.3 %collective-permute-start.6 = (bf16[3,64,1408]{2,1,0:T(8,128)(2,1)S(1)}, bf16[3,64,1408]{2,1,0:T(8,128)(2,1)S(1)}, u32[]{:S(2)}, u32[]{:S(2)}) collective-permute-start(bf16[3,64,1408]{2,1,0:T(8,128)(2,1)S(1)} %collective-permute-done.3.refs_5_), channel_id=1, source_target_pairs={{0,2},{2,0},{1,3},{3,1},{4,6},{6,4},{5,7},{7,5},{8,10},{10,8},{9,1... | collective-permute-start | bytes 1622024 | tf_op jit(solution)/shard_map/ppermute | solution.py:324
  127.7 3.8 %copy-start.18 = (bf16[3,64,1408]{2,1,0:T(8,128)(2,1)}, bf16[3,64,1408]{2,1,0:T(8,128)(2,1)S(1)}, u32[]{:S(2)}) copy-start(bf16[3,64,1408]{2,1,0:T(8,128)(2,1)S(1)} %collective-permute-done.5.refs_6_) | copy-start | bytes 1622020
  127.7 3.8 %collective-permute-start.7 = (bf16[3,64,1408]{2,1,0:T(8,128)(2,1)S(1)}, bf16[3,64,1408]{2,1,0:T(8,128)(2,1)S(1)}, u32[]{:S(2)}, u32[]{:S(2)}) collective-permute-start(bf16[3,64,1408]{2,1,0:T(8,128)(2,1)S(1)} %collective-permute-done.5.refs_6_), channel_id=1, source_target_pairs={{0,2},{2,0},{1,3},{3,1},{4,6},{6,4},{5,7},{7,5},{8,10},{10,8},{9,1... | collective-permute-start | bytes 1622024 | tf_op jit(solution)/shard_map/ppermute | solution.py:324
  129.7 1.9 copy-start.15
  129.7 1.9 copy-start.19
  132.4 1.0 copy-start.16
  143.0 15.3 %copy-start.14 = (f32[1,128,2]{1,2,0:T(2,128)S(1)}, f32[1,128,2]{1,2,0:T(2,128)}, u32[]{:S(2)}) copy-start(f32[1,128,2]{1,2,0:T(2,128)} %param.24) | copy-start | bytes 3076
  143.0 54.1 %all-to-all-start.4 = ((bf16[64,40,128]{2,1,0:T(8,128)(2,1)}), bf16[64,40,128]{2,1,0:T(8,128)(2,1)S(1)}, u32[]{:S(2)}, u32[]{:S(2)}) async-start(bf16[64,40,128]{2,1,0:T(8,128)(2,1)} %bitcast.53), calls=%async_computation.4 | async-start | bytes 1310720 | tf_op jit(solution)/shard_map/all_to_all | solution.py:20
  (2 other events, 1.7 us)

commit v8 on v5

--- a/solution.py
+++ b/solution.py
@@ -45,10 +45,19 @@
     return block * cosine + pltpu.roll(block, block.shape[1] // 2, 1) * sine
 
 
+def tables(cos_start_ref, sin_start_ref, cos_ref, sin_ref):
+    cosine = cos_start_ref[...] * cos_ref[...] - sin_start_ref[...] * sin_ref[...]
+    sine = sin_start_ref[...] * cos_ref[...] + cos_start_ref[...] * sin_ref[...]
+    lane = lax.broadcasted_iota(jnp.int32, sine.shape, 1)
+    return cosine, jnp.where(lane < sine.shape[1] // 2, -sine, sine)
+
+
 def summary_kernel(
     keys_ref,
     values_ref,
     log_ref,
+    cos_start_ref,
+    sin_start_ref,
     cos_ref,
     sin_ref,
     gate_hbm,
@@ -72,6 +81,7 @@
     ]
     for load in loads:
         load.start()
+    cosine, sine = tables(cos_start_ref, sin_start_ref, cos_ref, sin_ref)
     heads, count = log_ref.shape
     head_dim = cos_ref.shape[1]
     parts = message_ref.shape[0] // heads
@@ -92,7 +102,7 @@
                 load.wait()
                 store.start()
         lanes = slice(head * head_dim, (head + 1) * head_dim)
-        keys = turned(keys_ref[:, lanes].astype(F32), cos_ref[...], sin_ref[...]).astype(BF16)
+        keys = turned(keys_ref[:, lanes].astype(F32), cosine, sine).astype(BF16)
         faded = keys.astype(F32).T * trailing[head : head + 1]
         coarse = faded.astype(BF16)
         fine = (faded - coarse.astype(F32)).astype(BF16)
@@ -107,8 +117,19 @@
 
 
 def inside_kernel(
-    queries_ref, keys_ref, values_ref, total_ref, cos_ref, sin_ref, turned_ref, inside_ref, fade_ref
+    queries_ref,
+    keys_ref,
+    values_ref,
+    total_ref,
+    cos_start_ref,
+    sin_start_ref,
+    cos_ref,
+    sin_ref,
+    turned_ref,
+    inside_ref,
+    fade_ref,
 ):
+    cosine, sine = tables(cos_start_ref, sin_start_ref, cos_ref, sin_ref)
     heads, count = total_ref.shape
     head_dim = cos_ref.shape[1]
     row = lax.broadcasted_iota(jnp.int32, (count, count), 0)
@@ -117,10 +138,10 @@
     fade = jnp.zeros((count, count), F32)
     for head in range(heads):
         lanes = slice(head * head_dim, (head + 1) * head_dim)
-        queries = turned(queries_ref[:, lanes].astype(F32), cos_ref[...], sin_ref[...])
+        queries = turned(queries_ref[:, lanes].astype(F32), cosine, sine)
         queries = (queries * head_dim ** (-0.5)).astype(BF16)
         turned_ref[:, lanes] = queries
-        keys = turned(keys_ref[:, lanes].astype(F32), cos_ref[...], sin_ref[...]).astype(BF16)
+        keys = turned(keys_ref[:, lanes].astype(F32), cosine, sine).astype(BF16)
         scores = lax.dot_general(
             queries, keys, (((1,), (1,)), ((), ())), preferred_element_type=F32
         )
@@ -331,12 +352,16 @@
     message = (plane, part_rows + LOG_ROWS, head_dim)
 
     half = head_dim // 2
-    inverse = (10000.0 ** (-np.arange(half) / half)).astype(np.float32)
-    sign = np.repeat(np.array([-1.0, 1.0], np.float32), half)
+    inverse = np.tile(10000.0 ** (-np.arange(half) / half), 2)
+    within = np.arange(tok_rows)[:, None] * inverse[None, :]
     block_index = lax.axis_index(CTX) * lax.axis_size(EXP) + lax.axis_index(EXP)
-    position = block_index * tok_rows + jnp.arange(tok_rows, dtype=jnp.int32)
-    angles = position.astype(F32)[:, None] * np.tile(inverse, 2)[None, :]
-    cosine, sine = jnp.cos(angles), jnp.sin(angles) * sign
+    start = (block_index * tok_rows).astype(F32) * inverse.astype(np.float32)[None, :]
+    turn = (
+        jnp.cos(start),
+        jnp.sin(start),
+        np.cos(within).astype(np.float32),
+        np.sin(within).astype(np.float32),
+    )
 
     shards = (3,) + w_gate.shape[1:]
     any_space, in_vmem = pl.BlockSpec(memory_space=pl.ANY), pl.BlockSpec(memory_space=pltpu.VMEM)
@@ -348,7 +373,7 @@
             shape((head_count, tok_rows), F32),
             shape(shards, BF16),
         ),
-        in_specs=[in_vmem] * 5 + [any_space] * 3,
+        in_specs=[in_vmem] * 7 + [any_space] * 3,
         out_specs=(in_vmem, in_vmem, any_space),
         scratch_shapes=[
             pltpu.VMEM(shards, BF16),
@@ -356,7 +381,7 @@
             pltpu.SemaphoreType.DMA((3,)),
         ],
         cost_estimate=cost(70000000, 3200000),
-    )(keys[0], values[0], log_decay[0].T, cosine, sine, w_gate[0], w_up[0], w_down[0])
+    )(keys[0], values[0], log_decay[0].T, *turn, w_gate[0], w_up[0], w_down[0])
     summaries = exchange(out_message, PLANE)
     after, before = along_x(stacked, 1), along_x(stacked, -1)
     turned_queries, inside, fade = pl.pallas_call(
@@ -365,7 +390,7 @@
         out_shape=(shape(wide, BF16), shape(wide, F32), shape((tok_rows, tok_rows), F32)),
         cost_estimate=cost(70000000, 2200000),
         compiler_params=vmem(8),
-    )(queries[0], keys[0], values[0], total, cosine, sine)
+    )(queries[0], keys[0], values[0], total, *turn)
     sums = pl.pallas_call(
         plane_sum_kernel,
         name="plane_sum",

time: 195 us -> 195 us (level)
  no operation moved by 1% of the time
where the time goes in v8:
time: 195 us; the launch traced here: 194 us
  waiting for transfers between devices  89.6 us (46%)
  starting transfers between devices  64.4 us (33%)
  Pallas kernels  18.3 us (9%)
  blocking collectives  16 us (8%)
  local copies, waits for them, and re-layouts  3.01 us (2%)
  other arithmetic  2.27 us (1%)
    all_to_all x4, waiting for transfers between devices, exchange(): return lax.all_to_all(blocks, axes, split_axis=0, concat_axis=0, tiled=True)  61.4 us
    all_to_all x4, starting transfers between devices, exchange(): return lax.all_to_all(blocks, axes, split_axis=0, concat_axis=0, tiled=True)  41.9 us
    ppermute x4, waiting for transfers between devices, along_x(): lax.ppermute(piece, 'x', [(i, (i - step) % size) for i in range(size)])  27.4 us
    all_to_all x1, blocking collectives, exchange(): return lax.all_to_all(blocks, axes, split_axis=0, concat_axis=0, tiled=True)  16 us
    ppermute x4, starting transfers between devices, along_x(): lax.ppermute(piece, 'x', [(i, (i - step) % size) for i in range(size)])  12.4 us
    ppermute x5, starting transfers between devices, swapped(): return lax.ppermute(piece, 'core', [(0, 1), (1, 0)])  10.1 us
    pallas_call x1, Pallas kernels, run_experts(): pl.pallas_call(expert_kernel, name='experts', out_shape=shape((rows * mod...  6.64 us
  transfers between devices with their start and end apart: 13, of which 7 were waited for; matrix products, arithmetic and copies ran while one was open for 2% of the time, Pallas kernels for 1%

profile of v8, /device:TPU:8, one launch (start us, length us, event | category | flops | bytes accessed | tf_op | source)
XLA Modules:
  0.0 193.9 jit_solution(4465371548138101495)
XLA Ops:
  0.0 1.3 multiply_sine_fusion
  1.3 3.8 %summary.1 = (bf16[16,72,128]{2,1,0:T(8,128)(2,1)}, f32[8,128]{1,0:T(8,128)}, bf16[3,128,1408]{2,1,0:T(8,128)(2,1)}) custom-call(bf16[128,1024]{1,0:T(8,128)(2,1)} %bitcast.42, bf16[128,1024]{1,0:T(8,128)(2,1)} %bitcast.44, f32[8,128]{1,0:T(8,128)} %bitcast.54, f32[1,128]{1,0:T(1,128)} %get-tuple-element.24.cos_start_ref, ...), custom_call_target="tpu_custom_call" | custom-call | flops 70000000 | bytes 3200000 | tf_op jit(solution)/shard_map/summary/pallas_call | solution.py:368
  5.1 16.0 %all_to_all.25.arrived_ref = bf16[16,72,128]{2,1,0:T(8,128)(2,1)S(1)} all-to-all(bf16[16,72,128]{2,1,0:T(8,128)(2,1)} %get-tuple-element.13), channel_id=1, replica_groups=mesh['z'=16,'ylo'=2,'x'=4,'core'=2,'yhi'=2] {'ylo','x','core'}, dimensions={0} | all-to-all | bytes 589824 | tf_op jit(solution)/shard_map/all_to_all | solution.py:20
  21.1 0.8 plane_sum.1
  21.9 11.8 %all-to-all-start.1 = ((bf16[16,72,128]{2,1,0:T(8,128)(2,1)}), bf16[16,72,128]{2,1,0:T(8,128)(2,1)S(1)}, u32[]{:S(2)}, u32[]{:S(2)}) async-start(bf16[16,72,128]{2,1,0:T(8,128)(2,1)} %plane_sum.1), calls=%async_computation.1 | async-start | bytes 589824 | tf_op jit(solution)/shard_map/all_to_all | solution.py:20
  34.3 0.6 reduce-window.6
  35.4 18.3 %all-to-all-done.1.planes_ref = bf16[16,72,128]{2,1,0:T(8,128)(2,1)S(1)} async-done(((bf16[16,72,128]{2,1,0:T(8,128)(2,1)}), bf16[16,72,128]{2,1,0:T(8,128)(2,1)S(1)}, u32[]{:S(2)}, u32[]{:S(2)}) %all-to-all-start.1) | async-done | bytes 294944 | tf_op jit(solution)/shard_map/all_to_all | solution.py:20
  53.6 0.9 enter.1
  54.5 4.5 %all-to-all-start.2 = ((bf16[16,64,128]{2,1,0:T(8,128)(2,1)}), bf16[16,64,128]{2,1,0:T(8,128)(2,1)S(1)}, u32[]{:S(2)}, u32[]{:S(2)}) async-start(bf16[16,64,128]{2,1,0:T(8,128)(2,1)} %enter.1), calls=%async_computation.2 | async-start | bytes 524288 | tf_op jit(solution)/shard_map/all_to_all | solution.py:20
  59.3 1.5 inside.1
  60.7 4.7 %all-to-all-done.2 = bf16[16,64,128]{2,1,0:T(8,128)(2,1)S(1)} async-done(((bf16[16,64,128]{2,1,0:T(8,128)(2,1)}), bf16[16,64,128]{2,1,0:T(8,128)(2,1)S(1)}, u32[]{:S(2)}, u32[]{:S(2)}) %all-to-all-start.2) | async-done | bytes 262176 | tf_op jit(solution)/shard_map/all_to_all | solution.py:20
  65.5 2.8 %outgoing.1 = (f32[128,1024]{1,0:T(8,128)S(1)}, bf16[2560,128]{1,0:T(8,128)(2,1)}) custom-call(s32[8]{0:T(128)S(1)} %fusion.7.own_ref, bf16[1024,128]{1,0:T(8,128)(2,1)S(1)} %bitcast.41, bf16[128,1024]{1,0:T(8,128)(2,1)S(1)} %get-tuple-element.15.queries_ref, f32[128,1024]{1,0:T(8,128)S(1)} %get-tuple-element.16.inside_ref, ...), custom_call_target="tpu_custom_call" | custom-call | flops 120000000 | bytes 3000000 | tf_op jit(solution)/shard_map/outgoing/pallas_call | solution.py:432
  68.3 10.5 %all-to-all-start.3 = ((bf16[64,40,128]{2,1,0:T(8,128)(2,1)}), bf16[64,40,128]{2,1,0:T(8,128)(2,1)}, u32[]{:S(2)}, u32[]{:S(2)}) async-start(bf16[64,40,128]{2,1,0:T(8,128)(2,1)} %bitcast.15), calls=%async_computation.3 | async-start | bytes 1310720 | tf_op jit(solution)/shard_map/all_to_all | solution.py:20
  78.8 2.7 %collective-permute-start.1 = (bf16[3,128,1408]{2,1,0:T(8,128)(2,1)}, bf16[3,128,1408]{2,1,0:T(8,128)(2,1)S(1)}, u32[]{:S(2)}, u32[]{:S(2)}) collective-permute-start(bf16[3,128,1408]{2,1,0:T(8,128)(2,1)} %get-tuple-element.19.refs_1_), channel_id=1, source_target_pairs={{0,12},{4,0},{8,4},{12,8},{1,13},{5,1},{9,5},{13,9},{2,14},{6,2},{... | collective-permute-start | bytes 3244040 | tf_op jit(solution)/shard_map/ppermute | solution.py:317
  81.5 3.2 %collective-permute-start.4 = (bf16[3,128,1408]{2,1,0:T(8,128)(2,1)}, bf16[3,128,1408]{2,1,0:T(8,128)(2,1)S(1)}, u32[]{:S(2)}, u32[]{:S(2)}) collective-permute-start(bf16[3,128,1408]{2,1,0:T(8,128)(2,1)} %get-tuple-element.19.refs_1_), channel_id=1, source_target_pairs={{0,4},{4,8},{8,12},{12,0},{1,5},{5,9},{9,13},{13,1},{2,6},{6,10},{... | collective-permute-start | bytes 3244040 | tf_op jit(solution)/shard_map/ppermute | solution.py:317
  84.6 1.9 collective-permute-start
  86.6 19.3 %collective-permute-done.1.refs_3_ = bf16[3,128,1408]{2,1,0:T(8,128)(2,1)S(1)} collective-permute-done((bf16[3,128,1408]{2,1,0:T(8,128)(2,1)}, bf16[3,128,1408]{2,1,0:T(8,128)(2,1)S(1)}, u32[]{:S(2)}, u32[]{:S(2)}) %collective-permute-start.1) | collective-permute-done | bytes 1081376 | tf_op jit(solution)/shard_map/ppermute | solution.py:317
  105.9 4.6 %collective-permute-start.3 = (bf16[3,64,1408]{2,1,0:T(8,128)(2,1)S(1)}, bf16[3,64,1408]{2,1,0:T(8,128)(2,1)}, u32[]{:S(2)}, u32[]{:S(2)}) collective-permute-start(bf16[3,64,1408]{2,1,0:T(8,128)(2,1)S(1)} %slice.25), channel_id=1, source_target_pairs={{0,12},{4,0},{8,4},{12,8},{1,13},{5,1},{9,5},{13,9},{2,14},{6,2},{... | collective-permute-start | bytes 1622024 | tf_op jit(solution)/shard_map/ppermute | solution.py:317
  110.6 1.9 collective-permute-start.5
  112.5 1.9 collective-permute-start.2
  114.4 2.4 %collective-permute-start.8 = (bf16[3,128,1408]{2,1,0:T(8,128)(2,1)S(1)}, bf16[3,128,1408]{2,1,0:T(8,128)(2,1)}, u32[]{:S(2)}, u32[]{:S(2)}) collective-permute-start(bf16[3,128,1408]{2,1,0:T(8,128)(2,1)S(1)} %collective-permute-done.4.refs_9_), channel_id=1, source_target_pairs={{0,2},{2,0},{1,3},{3,1},{4,6},{6,4},{5,7},{7,5},{8,10},{10,8},{9,1... | collective-permute-start | bytes 3244040 | tf_op jit(solution)/shard_map/ppermute | solution.py:321
  116.8 4.5 %collective-permute-done.3.refs_5_ = bf16[3,64,1408]{2,1,0:T(8,128)(2,1)} collective-permute-done((bf16[3,64,1408]{2,1,0:T(8,128)(2,1)S(1)}, bf16[3,64,1408]{2,1,0:T(8,128)(2,1)}, u32[]{:S(2)}, u32[]{:S(2)}) %collective-permute-start.3) | collective-permute-done | bytes 540704 | tf_op jit(solution)/shard_map/ppermute | solution.py:317
  121.4 1.9 collective-permute-start.6
  123.3 3.6 %collective-permute-done.5.refs_6_ = bf16[3,64,1408]{2,1,0:T(8,128)(2,1)} collective-permute-done((bf16[3,64,1408]{2,1,0:T(8,128)(2,1)S(1)}, bf16[3,64,1408]{2,1,0:T(8,128)(2,1)}, u32[]{:S(2)}, u32[]{:S(2)}) %collective-permute-start.5) | collective-permute-done | bytes 540704 | tf_op jit(solution)/shard_map/ppermute | solution.py:317
  126.9 1.9 collective-permute-start.7
  128.8 1.4 reshape.44.refs_0_
  130.2 0.8 collective-permute-done.7.refs_8_
  131.0 6.6 %experts.1 = bf16[2560,128]{1,0:T(8,128)(2,1)} custom-call(bf16[320,1024]{1,0:T(8,128)(2,1)S(1)} %reshape.44.refs_0_, bf16[3,128,1408]{2,1,0:T(8,128)(2,1)} %get-tuple-element.19.refs_1_, bf16[3,128,1408]{2,1,0:T(8,128)(2,1)} %collective-permute-done.refs_2_, bf16[3,128,1408]{2,1,0:T(8,128)(2,1)S(1)} %collective-permute-done.1.refs_3_, ...), custom_call_target="tpu_custom_call" | custom-call | flops 2768240640 | bytes 8650752 | tf_op jit(solution)/shard_map/experts/pallas_call | solution.py:298
  137.7 15.1 %all-to-all-start.4 = ((bf16[64,40,128]{2,1,0:T(8,128)(2,1)}), bf16[64,40,128]{2,1,0:T(8,128)(2,1)S(1)}, u32[]{:S(2)}, u32[]{:S(2)}) async-start(bf16[64,40,128]{2,1,0:T(8,128)(2,1)} %bitcast.16), calls=%async_computation.4 | async-start | bytes 1310720 | tf_op jit(solution)/shard_map/all_to_all | solution.py:20
  153.4 38.4 %all-to-all-done.4 = bf16[64,40,128]{2,1,0:T(8,128)(2,1)S(1)} async-done(((bf16[64,40,128]{2,1,0:T(8,128)(2,1)}), bf16[64,40,128]{2,1,0:T(8,128)(2,1)S(1)}, u32[]{:S(2)}, u32[]{:S(2)}) %all-to-all-start.4) | async-done | bytes 655392 | tf_op jit(solution)/shard_map/all_to_all | solution.py:20
  191.8 0.3 reshape.46.returned_ref
  192.0 1.9 combine.1
  (53 shorter events, 1.8 us)
Async XLA Ops:
  5.1 28.6 %copy-start.11 = (s32[1,128,2]{1,2,0:T(2,128)S(1)}, s32[1,128,2]{1,2,0:T(2,128)}, u32[]{:S(2)}) copy-start(s32[1,128,2]{1,2,0:T(2,128)} %param.22) | copy-start | bytes 3076
  21.9 31.7 %all-to-all-start.1 = ((bf16[16,72,128]{2,1,0:T(8,128)(2,1)}), bf16[16,72,128]{2,1,0:T(8,128)(2,1)S(1)}, u32[]{:S(2)}, u32[]{:S(2)}) async-start(bf16[16,72,128]{2,1,0:T(8,128)(2,1)} %plane_sum.1), calls=%async_computation.1 | async-start | bytes 589824 | tf_op jit(solution)/shard_map/all_to_all | solution.py:20
  34.2 25.0 %copy-start = (bf16[1,128,1024]{2,1,0:T(8,128)(2,1)S(1)}, bf16[1,128,1024]{2,1,0:T(8,128)(2,1)}, u32[]{:S(2)}) copy-start(bf16[1,128,1024]{2,1,0:T(8,128)(2,1)} %param.17) | copy-start | bytes 786436
  34.2 25.0 %copy-start.1 = (bf16[1,128,1024]{2,1,0:T(8,128)(2,1)S(1)}, bf16[1,128,1024]{2,1,0:T(8,128)(2,1)}, u32[]{:S(2)}) copy-start(bf16[1,128,1024]{2,1,0:T(8,128)(2,1)} %param.18) | copy-start | bytes 786436
  34.2 25.0 %copy-start.2 = (f32[128,128]{1,0:T(8,128)S(1)}, f32[128,128]{1,0:T(8,128)}, u32[]{:S(2)}) copy-start(f32[128,128]{1,0:T(8,128)} %constant.79.clone.cos_ref) | copy-start | bytes 196612
  34.2 25.0 %copy-start.3 = (f32[128,128]{1,0:T(8,128)S(1)}, f32[128,128]{1,0:T(8,128)}, u32[]{:S(2)}) copy-start(f32[128,128]{1,0:T(8,128)} %constant.80.clone.sin_ref) | copy-start | bytes 196612
  34.2 25.0 %copy-start.4 = (bf16[1,128,1024]{2,1,0:T(8,128)(2,1)S(1)}, bf16[1,128,1024]{2,1,0:T(8,128)(2,1)}, u32[]{:S(2)}) copy-start(bf16[1,128,1024]{2,1,0:T(8,128)(2,1)} %param.16) | copy-start | bytes 786436
  34.2 25.0 %copy-start.6 = (f32[1,128]{1,0:T(1,128)S(1)}, f32[1,128]{1,0:T(1,128)}, u32[]{:S(2)}) copy-start(f32[1,128]{1,0:T(1,128)} %get-tuple-element.23.sin_start_ref) | copy-start | bytes 1540
  34.2 25.0 %copy-start.7 = (f32[1,128]{1,0:T(1,128)S(1)}, f32[1,128]{1,0:T(1,128)}, u32[]{:S(2)}) copy-start(f32[1,128]{1,0:T(1,128)} %get-tuple-element.24.cos_start_ref) | copy-start | bytes 1540
  34.3 25.0 %copy-start.10 = (f32[8,128]{1,0:T(8,128)S(1)}, f32[8,128]{1,0:T(8,128)}, u32[]{:S(2)}) copy-start(f32[8,128]{1,0:T(8,128)} %get-tuple-element.14.total_ref) | copy-start | bytes 12292
  54.5 11.0 %copy-start.5 = (bf16[1,128,1024]{2,1,0:T(8,128)(2,1)S(1)}, bf16[1,128,1024]{2,1,0:T(8,128)(2,1)}, u32[]{:S(2)}) copy-start(bf16[1,128,1024]{2,1,0:T(8,128)(2,1)} %param.15) | copy-start | bytes 786436
  54.5 11.0 %copy-start.8 = (f32[1024]{0:T(1024)S(1)}, f32[1024]{0:T(1024)}, u32[]{:S(2)}) copy-start(f32[1024]{0:T(1024)} %param.20) | copy-start | bytes 12292
  54.5 11.0 %copy-start.9 = (f32[1024]{0:T(1024)S(1)}, f32[1024]{0:T(1024)}, u32[]{:S(2)}) copy-start(f32[1024]{0:T(1024)} %param.21) | copy-start | bytes 12292
  54.5 11.0 %all-to-all-start.2 = ((bf16[16,64,128]{2,1,0:T(8,128)(2,1)}), bf16[16,64,128]{2,1,0:T(8,128)(2,1)S(1)}, u32[]{:S(2)}, u32[]{:S(2)}) async-start(bf16[16,64,128]{2,1,0:T(8,128)(2,1)} %enter.1), calls=%async_computation.2 | async-start | bytes 524288 | tf_op jit(solution)/shard_map/all_to_all | solution.py:20
  68.3 60.5 %all-to-all-start.3 = ((bf16[64,40,128]{2,1,0:T(8,128)(2,1)}), bf16[64,40,128]{2,1,0:T(8,128)(2,1)}, u32[]{:S(2)}, u32[]{:S(2)}) async-start(bf16[64,40,128]{2,1,0:T(8,128)(2,1)} %bitcast.15), calls=%async_computation.3 | async-start | bytes 1310720 | tf_op jit(solution)/shard_map/all_to_all | solution.py:20
  78.8 27.1 %collective-permute-start.1 = (bf16[3,128,1408]{2,1,0:T(8,128)(2,1)}, bf16[3,128,1408]{2,1,0:T(8,128)(2,1)S(1)}, u32[]{:S(2)}, u32[]{:S(2)}) collective-permute-start(bf16[3,128,1408]{2,1,0:T(8,128)(2,1)} %get-tuple-element.19.refs_1_), channel_id=1, source_target_pairs={{0,12},{4,0},{8,4},{12,8},{1,13},{5,1},{9,5},{13,9},{2,14},{6,2},{... | collective-permute-start | bytes 3244040 | tf_op jit(solution)/shard_map/ppermute | solution.py:317
  81.5 29.1 %collective-permute-start.4 = (bf16[3,128,1408]{2,1,0:T(8,128)(2,1)}, bf16[3,128,1408]{2,1,0:T(8,128)(2,1)S(1)}, u32[]{:S(2)}, u32[]{:S(2)}) collective-permute-start(bf16[3,128,1408]{2,1,0:T(8,128)(2,1)} %get-tuple-element.19.refs_1_), channel_id=1, source_target_pairs={{0,4},{4,8},{8,12},{12,0},{1,5},{5,9},{9,13},{13,1},{2,6},{6,10},{... | collective-permute-start | bytes 3244040 | tf_op jit(solution)/shard_map/ppermute | solution.py:317
  84.6 45.5 %collective-permute-start = (bf16[3,128,1408]{2,1,0:T(8,128)(2,1)}, bf16[3,128,1408]{2,1,0:T(8,128)(2,1)}, u32[]{:S(2)}, u32[]{:S(2)}) collective-permute-start(bf16[3,128,1408]{2,1,0:T(8,128)(2,1)} %get-tuple-element.19.refs_1_), channel_id=1, source_target_pairs={{0,2},{2,0},{1,3},{3,1},{4,6},{6,4},{5,7},{7,5},{8,10},{10,8},{9,1... | collective-permute-start | bytes 3244040 | tf_op jit(solution)/shard_map/ppermute | solution.py:321
  105.9 15.5 %collective-permute-start.3 = (bf16[3,64,1408]{2,1,0:T(8,128)(2,1)S(1)}, bf16[3,64,1408]{2,1,0:T(8,128)(2,1)}, u32[]{:S(2)}, u32[]{:S(2)}) collective-permute-start(bf16[3,64,1408]{2,1,0:T(8,128)(2,1)S(1)} %slice.25), channel_id=1, source_target_pairs={{0,12},{4,0},{8,4},{12,8},{1,13},{5,1},{9,5},{13,9},{2,14},{6,2},{... | collective-permute-start | bytes 1622024 | tf_op jit(solution)/shard_map/ppermute | solution.py:317
  110.6 16.3 %collective-permute-start.5 = (bf16[3,64,1408]{2,1,0:T(8,128)(2,1)S(1)}, bf16[3,64,1408]{2,1,0:T(8,128)(2,1)}, u32[]{:S(2)}, u32[]{:S(2)}) collective-permute-start(bf16[3,64,1408]{2,1,0:T(8,128)(2,1)S(1)} %slice.26), channel_id=1, source_target_pairs={{0,4},{4,8},{8,12},{12,0},{1,5},{5,9},{9,13},{13,1},{2,6},{6,10},{... | collective-permute-start | bytes 1622024 | tf_op jit(solution)/shard_map/ppermute | solution.py:317
  112.5 18.5 %collective-permute-start.2 = (bf16[3,128,1408]{2,1,0:T(8,128)(2,1)S(1)}, bf16[3,128,1408]{2,1,0:T(8,128)(2,1)}, u32[]{:S(2)}, u32[]{:S(2)}) collective-permute-start(bf16[3,128,1408]{2,1,0:T(8,128)(2,1)S(1)} %collective-permute-done.1.refs_3_), channel_id=1, source_target_pairs={{0,2},{2,0},{1,3},{3,1},{4,6},{6,4},{5,7},{7,5},{8,10},{10,8},{9,1... | collective-permute-start | bytes 3244040 | tf_op jit(solution)/shard_map/ppermute | solution.py:321
  114.4 16.6 %collective-permute-start.8 = (bf16[3,128,1408]{2,1,0:T(8,128)(2,1)S(1)}, bf16[3,128,1408]{2,1,0:T(8,128)(2,1)}, u32[]{:S(2)}, u32[]{:S(2)}) collective-permute-start(bf16[3,128,1408]{2,1,0:T(8,128)(2,1)S(1)} %collective-permute-done.4.refs_9_), channel_id=1, source_target_pairs={{0,2},{2,0},{1,3},{3,1},{4,6},{6,4},{5,7},{7,5},{8,10},{10,8},{9,1... | collective-permute-start | bytes 3244040 | tf_op jit(solution)/shard_map/ppermute | solution.py:321
  121.4 8.8 %collective-permute-start.6 = (bf16[3,64,1408]{2,1,0:T(8,128)(2,1)}, bf16[3,64,1408]{2,1,0:T(8,128)(2,1)}, u32[]{:S(2)}, u32[]{:S(2)}) collective-permute-start(bf16[3,64,1408]{2,1,0:T(8,128)(2,1)} %collective-permute-done.3.refs_5_), channel_id=1, source_target_pairs={{0,2},{2,0},{1,3},{3,1},{4,6},{6,4},{5,7},{7,5},{8,10},{10,8},{9,1... | collective-permute-start | bytes 1622024 | tf_op jit(solution)/shard_map/ppermute | solution.py:321
  126.9 4.2 %collective-permute-start.7 = (bf16[3,64,1408]{2,1,0:T(8,128)(2,1)}, bf16[3,64,1408]{2,1,0:T(8,128)(2,1)}, u32[]{:S(2)}, u32[]{:S(2)}) collective-permute-start(bf16[3,64,1408]{2,1,0:T(8,128)(2,1)} %collective-permute-done.5.refs_6_), channel_id=1, source_target_pairs={{0,2},{2,0},{1,3},{3,1},{4,6},{6,4},{5,7},{7,5},{8,10},{10,8},{9,1... | collective-permute-start | bytes 1622024 | tf_op jit(solution)/shard_map/ppermute | solution.py:321
  137.7 15.3 %copy-start.12 = (f32[1,128,2]{1,2,0:T(2,128)S(1)}, f32[1,128,2]{1,2,0:T(2,128)}, u32[]{:S(2)}) copy-start(f32[1,128,2]{1,2,0:T(2,128)} %param.23) | copy-start | bytes 3076
  137.7 54.1 %all-to-all-start.4 = ((bf16[64,40,128]{2,1,0:T(8,128)(2,1)}), bf16[64,40,128]{2,1,0:T(8,128)(2,1)S(1)}, u32[]{:S(2)}, u32[]{:S(2)}) async-start(bf16[64,40,128]{2,1,0:T(8,128)(2,1)} %bitcast.16), calls=%async_computation.4 | async-start | bytes 1310720 | tf_op jit(solution)/shard_map/all_to_all | solution.py:20

commit v9 on v8

--- a/solution.py
+++ b/solution.py
@@ -45,9 +45,15 @@
     return block * cosine + pltpu.roll(block, block.shape[1] // 2, 1) * sine
 
 
-def tables(cos_start_ref, sin_start_ref, cos_ref, sin_ref):
-    cosine = cos_start_ref[...] * cos_ref[...] - sin_start_ref[...] * sin_ref[...]
-    sine = sin_start_ref[...] * cos_ref[...] + cos_start_ref[...] * sin_ref[...]
+def turn_by(cosine, sine, row, table):
+    cos_row, sin_row = table[0, pl.ds(row, 1), :], table[1, pl.ds(row, 1), :]
+    return cosine * cos_row - sine * sin_row, sine * cos_row + cosine * sin_row
+
+
+def tables(plane_ref, block_ref, plane_table, block_table, within_table):
+    cosine, sine = within_table[0], within_table[1]
+    cosine, sine = turn_by(cosine, sine, plane_ref[0], plane_table)
+    cosine, sine = turn_by(cosine, sine, block_ref[0], block_table)
     lane = lax.broadcasted_iota(jnp.int32, sine.shape, 1)
     return cosine, jnp.where(lane < sine.shape[1] // 2, -sine, sine)
 
@@ -56,10 +62,11 @@
     keys_ref,
     values_ref,
     log_ref,
-    cos_start_ref,
-    sin_start_ref,
-    cos_ref,
-    sin_ref,
+    plane_ref,
+    block_ref,
+    plane_table,
+    block_table,
+    within_table,
     gate_hbm,
     up_hbm,
     down_hbm,
@@ -81,9 +88,9 @@
     ]
     for load in loads:
         load.start()
-    cosine, sine = tables(cos_start_ref, sin_start_ref, cos_ref, sin_ref)
+    cosine, sine = tables(plane_ref, block_ref, plane_table, block_table, within_table)
     heads, count = log_ref.shape
-    head_dim = cos_ref.shape[1]
+    head_dim = within_table.shape[2]
     parts = message_ref.shape[0] // heads
     rows = head_dim // parts
     earlier = lax.broadcasted_iota(jnp.int32, (count, count), 0)
@@ -121,17 +128,18 @@
     keys_ref,
     values_ref,
     total_ref,
-    cos_start_ref,
-    sin_start_ref,
-    cos_ref,
-    sin_ref,
+    plane_ref,
+    block_ref,
+    plane_table,
+    block_table,
+    within_table,
     turned_ref,
     inside_ref,
     fade_ref,
 ):
-    cosine, sine = tables(cos_start_ref, sin_start_ref, cos_ref, sin_ref)
+    cosine, sine = tables(plane_ref, block_ref, plane_table, block_table, within_table)
     heads, count = total_ref.shape
-    head_dim = cos_ref.shape[1]
+    head_dim = within_table.shape[2]
     row = lax.broadcasted_iota(jnp.int32, (count, count), 0)
     column = lax.broadcasted_iota(jnp.int32, (count, count), 1)
     causal = row >= column
@@ -353,15 +361,20 @@
 
     half = head_dim // 2
     inverse = np.tile(10000.0 ** (-np.arange(half) / half), 2)
-    within = np.arange(tok_rows)[:, None] * inverse[None, :]
-    block_index = lax.axis_index(CTX) * lax.axis_size(EXP) + lax.axis_index(EXP)
-    start = (block_index * tok_rows).astype(F32) * inverse.astype(np.float32)[None, :]
+
+
+    def angle_table(rows, step):
+        angles = np.arange(0, rows * step, step)[:, None] * inverse[None, :]
+        return np.stack([np.cos(angles), np.sin(angles)]).astype(np.float32)
+
     turn = (
-        jnp.cos(start),
-        jnp.sin(start),
-        np.cos(within).astype(np.float32),
-        np.sin(within).astype(np.float32),
+        lax.axis_index("z")[None],
+        lax.axis_index(PLANE)[None],
+        angle_table(lax.axis_size("z"), plane * tok_rows),
+        angle_table(plane, tok_rows),
+        angle_table(tok_rows, 1),
     )
+    in_smem = pl.BlockSpec(memory_space=pltpu.SMEM)
 
     shards = (3,) + w_gate.shape[1:]
     any_space, in_vmem = pl.BlockSpec(memory_space=pl.ANY), pl.BlockSpec(memory_space=pltpu.VMEM)
@@ -373,7 +386,7 @@
             shape((head_count, tok_rows), F32),
             shape(shards, BF16),
         ),
-        in_specs=[in_vmem] * 7 + [any_space] * 3,
+        in_specs=[in_vmem] * 3 + [in_smem] * 2 + [in_vmem] * 3 + [any_space] * 3,
         out_specs=(in_vmem, in_vmem, any_space),
         scratch_shapes=[
             pltpu.VMEM(shards, BF16),
@@ -388,6 +401,7 @@
         inside_kernel,
         name="inside",
         out_shape=(shape(wide, BF16), shape(wide, F32), shape((tok_rows, tok_rows), F32)),
+        in_specs=[in_vmem] * 4 + [in_smem] * 2 + [in_vmem] * 3,
         cost_estimate=cost(70000000, 2200000),
         compiler_params=vmem(8),
     )(queries[0], keys[0], values[0], total, *turn)

time: 195 us -> 194 us (level)
  no operation moved by 1% of the time
where the time goes in v9:
time: 194 us; the launch traced here: 193 us
  waiting for transfers between devices  89.6 us (46%)
  starting transfers between devices  64.3 us (33%)
  Pallas kernels  18.3 us (9%)
  blocking collectives  16 us (8%)
  local copies, waits for them, and re-layouts  3.01 us (2%)
    all_to_all x4, waiting for transfers between devices, exchange(): return lax.all_to_all(blocks, axes, split_axis=0, concat_axis=0, tiled=True)  61.4 us
    all_to_all x4, starting transfers between devices, exchange(): return lax.all_to_all(blocks, axes, split_axis=0, concat_axis=0, tiled=True)  41.9 us
    ppermute x4, waiting for transfers between devices, along_x(): lax.ppermute(piece, 'x', [(i, (i - step) % size) for i in range(size)])  27.4 us
    all_to_all x1, blocking collectives, exchange(): return lax.all_to_all(blocks, axes, split_axis=0, concat_axis=0, tiled=True)  16 us
    ppermute x4, starting transfers between devices, along_x(): lax.ppermute(piece, 'x', [(i, (i - step) % size) for i in range(size)])  12.4 us
    ppermute x5, starting transfers between devices, swapped(): return lax.ppermute(piece, 'core', [(0, 1), (1, 0)])  10.1 us
    pallas_call x1, Pallas kernels, run_experts(): pl.pallas_call(expert_kernel, name='experts', out_shape=shape((rows * mod...  6.64 us
  transfers between devices with their start and end apart: 13, of which 7 were waited for; matrix products, arithmetic and copies ran while one was open for 2% of the time, Pallas kernels for 1%

profile of v9, /device:TPU:8, one launch (start us, length us, event | category | flops | bytes accessed | tf_op | source)
XLA Modules:
  0.0 192.7 jit_solution(15029573847131227315)
XLA Ops:
  0.0 3.9 %summary.1 = (bf16[16,72,128]{2,1,0:T(8,128)(2,1)}, f32[8,128]{1,0:T(8,128)}, bf16[3,128,1408]{2,1,0:T(8,128)(2,1)}) custom-call(bf16[128,1024]{1,0:T(8,128)(2,1)} %bitcast.42, bf16[128,1024]{1,0:T(8,128)(2,1)} %bitcast.44, f32[8,128]{1,0:T(8,128)} %bitcast.55, s32[1]{0:T(128)} %bitcast.plane_ref.own_ref, s32[1]{0:T(128)} %bitcast.5.block_ref, ...), custom_call_target="tpu_custom_call" | custom-call | flops 70000000 | bytes 3200000 | tf_op jit(solution)/shard_map/summary/pallas_call | solution.py:381
  3.9 16.0 %all_to_all.25.arrived_ref = bf16[16,72,128]{2,1,0:T(8,128)(2,1)S(1)} all-to-all(bf16[16,72,128]{2,1,0:T(8,128)(2,1)} %get-tuple-element.13), channel_id=1, replica_groups=mesh['z'=16,'ylo'=2,'x'=4,'core'=2,'yhi'=2] {'ylo','x','core'}, dimensions={0} | all-to-all | bytes 589824 | tf_op jit(solution)/shard_map/all_to_all | solution.py:20
  19.8 0.8 plane_sum.1
  20.7 11.8 %all-to-all-start.1 = ((bf16[16,72,128]{2,1,0:T(8,128)(2,1)}), bf16[16,72,128]{2,1,0:T(8,128)(2,1)S(1)}, u32[]{:S(2)}, u32[]{:S(2)}) async-start(bf16[16,72,128]{2,1,0:T(8,128)(2,1)} %plane_sum.1), calls=%async_computation.1 | async-start | bytes 589824 | tf_op jit(solution)/shard_map/all_to_all | solution.py:20
  33.0 0.6 reduce-window.6
  33.6 0.2 slice_reduce_fusion.2
  34.1 18.3 %all-to-all-done.1.planes_ref = bf16[16,72,128]{2,1,0:T(8,128)(2,1)S(1)} async-done(((bf16[16,72,128]{2,1,0:T(8,128)(2,1)}), bf16[16,72,128]{2,1,0:T(8,128)(2,1)S(1)}, u32[]{:S(2)}, u32[]{:S(2)}) %all-to-all-start.1) | async-done | bytes 294944 | tf_op jit(solution)/shard_map/all_to_all | solution.py:20
  52.4 0.9 enter.1
  53.3 4.5 %all-to-all-start.2 = ((bf16[16,64,128]{2,1,0:T(8,128)(2,1)}), bf16[16,64,128]{2,1,0:T(8,128)(2,1)S(1)}, u32[]{:S(2)}, u32[]{:S(2)}) async-start(bf16[16,64,128]{2,1,0:T(8,128)(2,1)} %enter.1), calls=%async_computation.2 | async-start | bytes 524288 | tf_op jit(solution)/shard_map/all_to_all | solution.py:20
  58.0 1.4 inside.1
  59.5 4.8 %all-to-all-done.2 = bf16[16,64,128]{2,1,0:T(8,128)(2,1)S(1)} async-done(((bf16[16,64,128]{2,1,0:T(8,128)(2,1)}), bf16[16,64,128]{2,1,0:T(8,128)(2,1)S(1)}, u32[]{:S(2)}, u32[]{:S(2)}) %all-to-all-start.2) | async-done | bytes 262176 | tf_op jit(solution)/shard_map/all_to_all | solution.py:20
  64.2 2.8 %outgoing.1 = (f32[128,1024]{1,0:T(8,128)S(1)}, bf16[2560,128]{1,0:T(8,128)(2,1)}) custom-call(s32[8]{0:T(128)S(1)} %fusion.7.own_ref, bf16[1024,128]{1,0:T(8,128)(2,1)S(1)} %bitcast.46, bf16[128,1024]{1,0:T(8,128)(2,1)S(1)} %get-tuple-element.15.queries_ref, f32[128,1024]{1,0:T(8,128)S(1)} %get-tuple-element.16.inside_ref, ...), custom_call_target="tpu_custom_call" | custom-call | flops 120000000 | bytes 3000000 | tf_op jit(solution)/shard_map/outgoing/pallas_call | solution.py:446
  67.0 10.5 %all-to-all-start.3 = ((bf16[64,40,128]{2,1,0:T(8,128)(2,1)}), bf16[64,40,128]{2,1,0:T(8,128)(2,1)}, u32[]{:S(2)}, u32[]{:S(2)}) async-start(bf16[64,40,128]{2,1,0:T(8,128)(2,1)} %bitcast.16), calls=%async_computation.3 | async-start | bytes 1310720 | tf_op jit(solution)/shard_map/all_to_all | solution.py:20
  77.5 2.7 %collective-permute-start.1 = (bf16[3,128,1408]{2,1,0:T(8,128)(2,1)}, bf16[3,128,1408]{2,1,0:T(8,128)(2,1)S(1)}, u32[]{:S(2)}, u32[]{:S(2)}) collective-permute-start(bf16[3,128,1408]{2,1,0:T(8,128)(2,1)} %get-tuple-element.19.refs_1_), channel_id=1, source_target_pairs={{0,12},{4,0},{8,4},{12,8},{1,13},{5,1},{9,5},{13,9},{2,14},{6,2},{... | collective-permute-start | bytes 3244040 | tf_op jit(solution)/shard_map/ppermute | solution.py:325
  80.2 3.2 %collective-permute-start.4 = (bf16[3,128,1408]{2,1,0:T(8,128)(2,1)}, bf16[3,128,1408]{2,1,0:T(8,128)(2,1)S(1)}, u32[]{:S(2)}, u32[]{:S(2)}) collective-permute-start(bf16[3,128,1408]{2,1,0:T(8,128)(2,1)} %get-tuple-element.19.refs_1_), channel_id=1, source_target_pairs={{0,4},{4,8},{8,12},{12,0},{1,5},{5,9},{9,13},{13,1},{2,6},{6,10},{... | collective-permute-start | bytes 3244040 | tf_op jit(solution)/shard_map/ppermute | solution.py:325
  83.4 1.9 collective-permute-start
  85.3 19.3 %collective-permute-done.1.refs_3_ = bf16[3,128,1408]{2,1,0:T(8,128)(2,1)S(1)} collective-permute-done((bf16[3,128,1408]{2,1,0:T(8,128)(2,1)}, bf16[3,128,1408]{2,1,0:T(8,128)(2,1)S(1)}, u32[]{:S(2)}, u32[]{:S(2)}) %collective-permute-start.1) | collective-permute-done | bytes 1081376 | tf_op jit(solution)/shard_map/ppermute | solution.py:325
  104.6 4.6 %collective-permute-start.3 = (bf16[3,64,1408]{2,1,0:T(8,128)(2,1)S(1)}, bf16[3,64,1408]{2,1,0:T(8,128)(2,1)}, u32[]{:S(2)}, u32[]{:S(2)}) collective-permute-start(bf16[3,64,1408]{2,1,0:T(8,128)(2,1)S(1)} %slice.25), channel_id=1, source_target_pairs={{0,12},{4,0},{8,4},{12,8},{1,13},{5,1},{9,5},{13,9},{2,14},{6,2},{... | collective-permute-start | bytes 1622024 | tf_op jit(solution)/shard_map/ppermute | solution.py:325
  109.3 1.9 collective-permute-start.5
  111.2 1.9 collective-permute-start.2
  113.2 2.4 %collective-permute-start.8 = (bf16[3,128,1408]{2,1,0:T(8,128)(2,1)S(1)}, bf16[3,128,1408]{2,1,0:T(8,128)(2,1)}, u32[]{:S(2)}, u32[]{:S(2)}) collective-permute-start(bf16[3,128,1408]{2,1,0:T(8,128)(2,1)S(1)} %collective-permute-done.4.refs_9_), channel_id=1, source_target_pairs={{0,2},{2,0},{1,3},{3,1},{4,6},{6,4},{5,7},{7,5},{8,10},{10,8},{9,1... | collective-permute-start | bytes 3244040 | tf_op jit(solution)/shard_map/ppermute | solution.py:329
  115.6 4.5 %collective-permute-done.3.refs_5_ = bf16[3,64,1408]{2,1,0:T(8,128)(2,1)} collective-permute-done((bf16[3,64,1408]{2,1,0:T(8,128)(2,1)S(1)}, bf16[3,64,1408]{2,1,0:T(8,128)(2,1)}, u32[]{:S(2)}, u32[]{:S(2)}) %collective-permute-start.3) | collective-permute-done | bytes 540704 | tf_op jit(solution)/shard_map/ppermute | solution.py:325
  120.1 1.9 collective-permute-start.6
  122.0 3.6 %collective-permute-done.5.refs_6_ = bf16[3,64,1408]{2,1,0:T(8,128)(2,1)} collective-permute-done((bf16[3,64,1408]{2,1,0:T(8,128)(2,1)S(1)}, bf16[3,64,1408]{2,1,0:T(8,128)(2,1)}, u32[]{:S(2)}, u32[]{:S(2)}) %collective-permute-start.5) | collective-permute-done | bytes 540704 | tf_op jit(solution)/shard_map/ppermute | solution.py:325
  125.6 1.9 collective-permute-start.7
  127.5 1.4 reshape.44.refs_0_
  128.9 0.8 collective-permute-done.7.refs_8_
  129.8 6.6 %experts.1 = bf16[2560,128]{1,0:T(8,128)(2,1)} custom-call(bf16[320,1024]{1,0:T(8,128)(2,1)S(1)} %reshape.44.refs_0_, bf16[3,128,1408]{2,1,0:T(8,128)(2,1)} %get-tuple-element.19.refs_1_, bf16[3,128,1408]{2,1,0:T(8,128)(2,1)} %collective-permute-done.refs_2_, bf16[3,128,1408]{2,1,0:T(8,128)(2,1)S(1)} %collective-permute-done.1.refs_3_, ...), custom_call_target="tpu_custom_call" | custom-call | flops 2768240640 | bytes 8650752 | tf_op jit(solution)/shard_map/experts/pallas_call | solution.py:306
  136.4 15.1 %all-to-all-start.4 = ((bf16[64,40,128]{2,1,0:T(8,128)(2,1)}), bf16[64,40,128]{2,1,0:T(8,128)(2,1)S(1)}, u32[]{:S(2)}, u32[]{:S(2)}) async-start(bf16[64,40,128]{2,1,0:T(8,128)(2,1)} %bitcast.17), calls=%async_computation.4 | async-start | bytes 1310720 | tf_op jit(solution)/shard_map/all_to_all | solution.py:20
  152.1 38.4 %all-to-all-done.4 = bf16[64,40,128]{2,1,0:T(8,128)(2,1)S(1)} async-done(((bf16[64,40,128]{2,1,0:T(8,128)(2,1)}), bf16[64,40,128]{2,1,0:T(8,128)(2,1)S(1)}, u32[]{:S(2)}, u32[]{:S(2)}) %all-to-all-start.4) | async-done | bytes 655392 | tf_op jit(solution)/shard_map/all_to_all | solution.py:20
  190.5 0.3 reshape.46.returned_ref
  190.8 1.9 combine.1
  (50 shorter events, 1.6 us)
Async XLA Ops:
  3.9 28.6 %copy-start.10 = (s32[1,128,2]{1,2,0:T(2,128)S(1)}, s32[1,128,2]{1,2,0:T(2,128)}, u32[]{:S(2)}) copy-start(s32[1,128,2]{1,2,0:T(2,128)} %param.22) | copy-start | bytes 3076
  20.7 31.7 %all-to-all-start.1 = ((bf16[16,72,128]{2,1,0:T(8,128)(2,1)}), bf16[16,72,128]{2,1,0:T(8,128)(2,1)S(1)}, u32[]{:S(2)}, u32[]{:S(2)}) async-start(bf16[16,72,128]{2,1,0:T(8,128)(2,1)} %plane_sum.1), calls=%async_computation.1 | async-start | bytes 589824 | tf_op jit(solution)/shard_map/all_to_all | solution.py:20
  32.9 25.0 %copy-start = (bf16[1,128,1024]{2,1,0:T(8,128)(2,1)S(1)}, bf16[1,128,1024]{2,1,0:T(8,128)(2,1)}, u32[]{:S(2)}) copy-start(bf16[1,128,1024]{2,1,0:T(8,128)(2,1)} %param.17) | copy-start | bytes 786436
  32.9 25.0 %copy-start.1 = (bf16[1,128,1024]{2,1,0:T(8,128)(2,1)S(1)}, bf16[1,128,1024]{2,1,0:T(8,128)(2,1)}, u32[]{:S(2)}) copy-start(bf16[1,128,1024]{2,1,0:T(8,128)(2,1)} %param.18) | copy-start | bytes 786436
  32.9 25.0 %copy-start.2 = (f32[2,128,128]{2,1,0:T(8,128)S(1)}, f32[2,128,128]{2,1,0:T(8,128)}, u32[]{:S(2)}) copy-start(f32[2,128,128]{2,1,0:T(8,128)} %constant.78.clone.within_table) | copy-start | bytes 393220
  33.0 25.0 %copy-start.3 = (bf16[1,128,1024]{2,1,0:T(8,128)(2,1)S(1)}, bf16[1,128,1024]{2,1,0:T(8,128)(2,1)}, u32[]{:S(2)}) copy-start(bf16[1,128,1024]{2,1,0:T(8,128)(2,1)} %param.16) | copy-start | bytes 786436
  33.0 25.0 %copy-start.5 = (f32[2,16,128]{2,1,0:T(8,128)S(1)}, f32[2,16,128]{2,1,0:T(8,128)}, u32[]{:S(2)}) copy-start(f32[2,16,128]{2,1,0:T(8,128)} %constant.76.clone.plane_table) | copy-start | bytes 49156
  33.0 25.0 %copy-start.6 = (f32[2,16,128]{2,1,0:T(8,128)S(1)}, f32[2,16,128]{2,1,0:T(8,128)}, u32[]{:S(2)}) copy-start(f32[2,16,128]{2,1,0:T(8,128)} %constant.77.clone.block_table) | copy-start | bytes 49156
  33.0 25.0 %copy-start.9 = (f32[8,128]{1,0:T(8,128)S(1)}, f32[8,128]{1,0:T(8,128)}, u32[]{:S(2)}) copy-start(f32[8,128]{1,0:T(8,128)} %get-tuple-element.14.total_ref) | copy-start | bytes 12292
  53.3 11.0 %copy-start.4 = (bf16[1,128,1024]{2,1,0:T(8,128)(2,1)S(1)}, bf16[1,128,1024]{2,1,0:T(8,128)(2,1)}, u32[]{:S(2)}) copy-start(bf16[1,128,1024]{2,1,0:T(8,128)(2,1)} %param.15) | copy-start | bytes 786436
  53.3 11.0 %copy-start.7 = (f32[1024]{0:T(1024)S(1)}, f32[1024]{0:T(1024)}, u32[]{:S(2)}) copy-start(f32[1024]{0:T(1024)} %param.20) | copy-start | bytes 12292
  53.3 11.0 %copy-start.8 = (f32[1024]{0:T(1024)S(1)}, f32[1024]{0:T(1024)}, u32[]{:S(2)}) copy-start(f32[1024]{0:T(1024)} %param.21) | copy-start | bytes 12292
  53.3 11.0 %all-to-all-start.2 = ((bf16[16,64,128]{2,1,0:T(8,128)(2,1)}), bf16[16,64,128]{2,1,0:T(8,128)(2,1)S(1)}, u32[]{:S(2)}, u32[]{:S(2)}) async-start(bf16[16,64,128]{2,1,0:T(8,128)(2,1)} %enter.1), calls=%async_computation.2 | async-start | bytes 524288 | tf_op jit(solution)/shard_map/all_to_all | solution.py:20
  67.0 60.5 %all-to-all-start.3 = ((bf16[64,40,128]{2,1,0:T(8,128)(2,1)}), bf16[64,40,128]{2,1,0:T(8,128)(2,1)}, u32[]{:S(2)}, u32[]{:S(2)}) async-start(bf16[64,40,128]{2,1,0:T(8,128)(2,1)} %bitcast.16), calls=%async_computation.3 | async-start | bytes 1310720 | tf_op jit(solution)/shard_map/all_to_all | solution.py:20
  77.5 27.1 %collective-permute-start.1 = (bf16[3,128,1408]{2,1,0:T(8,128)(2,1)}, bf16[3,128,1408]{2,1,0:T(8,128)(2,1)S(1)}, u32[]{:S(2)}, u32[]{:S(2)}) collective-permute-start(bf16[3,128,1408]{2,1,0:T(8,128)(2,1)} %get-tuple-element.19.refs_1_), channel_id=1, source_target_pairs={{0,12},{4,0},{8,4},{12,8},{1,13},{5,1},{9,5},{13,9},{2,14},{6,2},{... | collective-permute-start | bytes 3244040 | tf_op jit(solution)/shard_map/ppermute | solution.py:325
  80.2 29.1 %collective-permute-start.4 = (bf16[3,128,1408]{2,1,0:T(8,128)(2,1)}, bf16[3,128,1408]{2,1,0:T(8,128)(2,1)S(1)}, u32[]{:S(2)}, u32[]{:S(2)}) collective-permute-start(bf16[3,128,1408]{2,1,0:T(8,128)(2,1)} %get-tuple-element.19.refs_1_), channel_id=1, source_target_pairs={{0,4},{4,8},{8,12},{12,0},{1,5},{5,9},{9,13},{13,1},{2,6},{6,10},{... | collective-permute-start | bytes 3244040 | tf_op jit(solution)/shard_map/ppermute | solution.py:325
  83.4 45.5 %collective-permute-start = (bf16[3,128,1408]{2,1,0:T(8,128)(2,1)}, bf16[3,128,1408]{2,1,0:T(8,128)(2,1)}, u32[]{:S(2)}, u32[]{:S(2)}) collective-permute-start(bf16[3,128,1408]{2,1,0:T(8,128)(2,1)} %get-tuple-element.19.refs_1_), channel_id=1, source_target_pairs={{0,2},{2,0},{1,3},{3,1},{4,6},{6,4},{5,7},{7,5},{8,10},{10,8},{9,1... | collective-permute-start | bytes 3244040 | tf_op jit(solution)/shard_map/ppermute | solution.py:329
  104.6 15.5 %collective-permute-start.3 = (bf16[3,64,1408]{2,1,0:T(8,128)(2,1)S(1)}, bf16[3,64,1408]{2,1,0:T(8,128)(2,1)}, u32[]{:S(2)}, u32[]{:S(2)}) collective-permute-start(bf16[3,64,1408]{2,1,0:T(8,128)(2,1)S(1)} %slice.25), channel_id=1, source_target_pairs={{0,12},{4,0},{8,4},{12,8},{1,13},{5,1},{9,5},{13,9},{2,14},{6,2},{... | collective-permute-start | bytes 1622024 | tf_op jit(solution)/shard_map/ppermute | solution.py:325
  109.3 16.3 %collective-permute-start.5 = (bf16[3,64,1408]{2,1,0:T(8,128)(2,1)S(1)}, bf16[3,64,1408]{2,1,0:T(8,128)(2,1)}, u32[]{:S(2)}, u32[]{:S(2)}) collective-permute-start(bf16[3,64,1408]{2,1,0:T(8,128)(2,1)S(1)} %slice.26), channel_id=1, source_target_pairs={{0,4},{4,8},{8,12},{12,0},{1,5},{5,9},{9,13},{13,1},{2,6},{6,10},{... | collective-permute-start | bytes 1622024 | tf_op jit(solution)/shard_map/ppermute | solution.py:325
  111.2 18.5 %collective-permute-start.2 = (bf16[3,128,1408]{2,1,0:T(8,128)(2,1)S(1)}, bf16[3,128,1408]{2,1,0:T(8,128)(2,1)}, u32[]{:S(2)}, u32[]{:S(2)}) collective-permute-start(bf16[3,128,1408]{2,1,0:T(8,128)(2,1)S(1)} %collective-permute-done.1.refs_3_), channel_id=1, source_target_pairs={{0,2},{2,0},{1,3},{3,1},{4,6},{6,4},{5,7},{7,5},{8,10},{10,8},{9,1... | collective-permute-start | bytes 3244040 | tf_op jit(solution)/shard_map/ppermute | solution.py:329
  113.2 16.6 %collective-permute-start.8 = (bf16[3,128,1408]{2,1,0:T(8,128)(2,1)S(1)}, bf16[3,128,1408]{2,1,0:T(8,128)(2,1)}, u32[]{:S(2)}, u32[]{:S(2)}) collective-permute-start(bf16[3,128,1408]{2,1,0:T(8,128)(2,1)S(1)} %collective-permute-done.4.refs_9_), channel_id=1, source_target_pairs={{0,2},{2,0},{1,3},{3,1},{4,6},{6,4},{5,7},{7,5},{8,10},{10,8},{9,1... | collective-permute-start | bytes 3244040 | tf_op jit(solution)/shard_map/ppermute | solution.py:329
  120.1 8.8 %collective-permute-start.6 = (bf16[3,64,1408]{2,1,0:T(8,128)(2,1)}, bf16[3,64,1408]{2,1,0:T(8,128)(2,1)}, u32[]{:S(2)}, u32[]{:S(2)}) collective-permute-start(bf16[3,64,1408]{2,1,0:T(8,128)(2,1)} %collective-permute-done.3.refs_5_), channel_id=1, source_target_pairs={{0,2},{2,0},{1,3},{3,1},{4,6},{6,4},{5,7},{7,5},{8,10},{10,8},{9,1... | collective-permute-start | bytes 1622024 | tf_op jit(solution)/shard_map/ppermute | solution.py:329
  125.6 4.2 %collective-permute-start.7 = (bf16[3,64,1408]{2,1,0:T(8,128)(2,1)}, bf16[3,64,1408]{2,1,0:T(8,128)(2,1)}, u32[]{:S(2)}, u32[]{:S(2)}) collective-permute-start(bf16[3,64,1408]{2,1,0:T(8,128)(2,1)} %collective-permute-done.5.refs_6_), channel_id=1, source_target_pairs={{0,2},{2,0},{1,3},{3,1},{4,6},{6,4},{5,7},{7,5},{8,10},{10,8},{9,1... | collective-permute-start | bytes 1622024 | tf_op jit(solution)/shard_map/ppermute | solution.py:329
  136.4 15.2 %copy-start.11 = (f32[1,128,2]{1,2,0:T(2,128)S(1)}, f32[1,128,2]{1,2,0:T(2,128)}, u32[]{:S(2)}) copy-start(f32[1,128,2]{1,2,0:T(2,128)} %param.23) | copy-start | bytes 3076
  136.4 54.1 %all-to-all-start.4 = ((bf16[64,40,128]{2,1,0:T(8,128)(2,1)}), bf16[64,40,128]{2,1,0:T(8,128)(2,1)S(1)}, u32[]{:S(2)}, u32[]{:S(2)}) async-start(bf16[64,40,128]{2,1,0:T(8,128)(2,1)} %bitcast.17), calls=%async_computation.4 | async-start | bytes 1310720 | tf_op jit(solution)/shard_map/all_to_all | solution.py:20
